TPU v7x, 256 devices: a whole 4x4x8 slice. The times are simulated.
256 devices in a mesh: dp: 64 (over y_lo, z, x), cluster: 4 (over y_hi, core).
Axes of the slice: x: 4, y: 4 (y_hi: 2, y_lo: 2; y = y_hi * 2 + y_lo), z: 8, core: 2. Of those that a mesh axis runs over, the one named last changes fastest.
Arguments:
- home_rows: bfloat16 [393216, 768], P(('dp', 'cluster')), may hold values from -6 to 6
- guest_rows: bfloat16 [65536, 768], P(('dp', 'cluster')), may hold values from -6 to 6
- home_cluster: int32 [1536], replicated, may hold values from 0 to 7, as said below
- guest_cluster: int32 [256], replicated, may hold values from 0 to 7, as said below
- pair_mask: int32 [256, 6, 64], P(('dp', 'cluster')), may hold values from 0 to 1, as said below
Outputs:
- home_score: float32 [393216], P(('dp', 'cluster'))
- guest_score: float32 [65536], P(('dp', 'cluster'))
Inputs may be any that keep to these rules, and one draw needn't show every extreme that they name: `home_cluster`: blocks of the devices at cluster indices 2 g and 2 g + 1 carry ids from g * 4 to (g + 1) * 4 - 1. `guest_cluster`: blocks of the devices at cluster indices 2 g and 2 g + 1 carry ids from g * 4 to (g + 1) * 4 - 1. `pair_mask`: an entry is 1 where the resident block and the visiting block it names carry one cluster id, else 0.
All inputs are finite; a program needn't handle non-finite values.
Results may differ from a plain program's by a relative error of at most 0.0003.
Values may be sent and summed in bfloat16 or wider, within the bound.
No kernel may reach another device: no remote copies, remote signals or barrier semaphores. Data moves between devices by JAX's collectives and lax.ppermute only.
A program may use at most 128 MiB of HBM per device.

v0:
```python
import functools
import math

import jax
import jax.numpy as jnp
from jax import lax
from jax.experimental import pallas as pl
from jax.experimental.pallas import tpu as pltpu
from jax.sharding import Mesh
from jax.sharding import PartitionSpec as P

BLOCK = 256
LANES = 128
SHARPNESS = 30.0
EPSILON = 1e-06
EXP2_SCALE = SHARPNESS / math.log(2.0)
UNROLL = 4
FAR_FROM = 4
IDS_AT = 3

NY, NZ, NX, NH, NK = 2, 8, 4, 2, 2
AXES = ("y", "z", "x", "h", "k")

SLOTS = (
    ( ((0, 1), ((0, 0),)), ((-1, 0), ((0, 0),)), ((0, -1), ((0, 0),)), ((1, 0), ((0, 0),)) ),
    ( ((1, 0), ((1, 0),)), ((-1, 0), ((-1, 0),)), ((0, 1), ((0, 1),)), ((0, -1), ((-1, 0),)) ),
    ( ((0, 1), ((2, 0),)), ((0, -1), ((1, 0),)), ((-1, 0), ((-2, 0),)), ((1, 0), ((2, 0),)) ),
    ( ((-1, 0), ((0, 2), (0, 1),)), ((1, 0), ((0, 2), (0, 1),)), ((0, 1), ((3, 0), (-3, 0),)), ((0, -1), ((3, 0), (-3, 0),)) ),
    ( ((-1, 0), ((3, -1), (-3, -1),)), ((0, 1), ((3, 1), (-3, 1),)), ((0, -1), ((-2, 0),)), ((1, 0), ((3, 1), (-3, 1),)) ),
    ( ((0, 1), ((-2, 1),)), ((0, -1), ((2, -1),)), ((1, 0), ((3, 0),)), ((-1, 0), ((-3, 2),)) ),
)


def node(dz, dx):
    return ((dz + 3) % NZ - 3, (dx + 1) % NX - 1)


def shift(value, dz, dx):
    if dx == 0:
        return lax.ppermute(value, "z", [(i, (i + dz) % NZ) for i in range(NZ)])
    if dz == 0:
        return lax.ppermute(value, "x", [(i, (i + dx) % NX) for i in range(NX)])
    return lax.ppermute(
        value,
        ("z", "x"),
        [(z * NX + x, (z + dz) % NZ * NX + (x + dx) % NX) for z in range(NZ) for x in range(NX)],
    )


def to_sibling(value):
    return lax.ppermute(value, "k", [(0, 1), (1, 0)])


def to_partner(value):
    return lax.ppermute(value, ("y", "k"), [(0, 3), (1, 2), (2, 1), (3, 0)])


def inverse_norms(rows):
    values = rows.astype(jnp.float32)
    return 1.0 / jnp.sqrt(jnp.sum(values * values, axis=-1) + EPSILON)


def lane_sums(values):
    high = values.astype(jnp.bfloat16)
    rest = values - high.astype(jnp.float32)
    middle = rest.astype(jnp.bfloat16)
    low = (rest - middle.astype(jnp.float32)).astype(jnp.bfloat16)
    terms = jnp.concatenate([high, middle, low], axis=1)
    ones = jnp.ones((8, terms.shape[1]), jnp.bfloat16)
    return lax.dot_general(ones, terms, (((1,), (1,)), ((), ())), preferred_element_type=jnp.float32)[:1]


def pair_kernel(news, olds, sizes, first_far, table, *refs):
    arrays, refs = refs[: len(sizes)], refs[len(sizes) :]
    blocks, scale, rows_in, cols_in, norms_in, turn, rows, cols_out, norms, next_turn, held, cols, listed, places, sems = refs
    n_new, n_old, n_set = len(news), len(olds), blocks.shape[0]
    z, x = table[table.shape[0] - 2], table[table.shape[0] - 1]
    copies, first = [], 0
    for a, (array, size) in enumerate(zip(arrays, sizes, strict=True)):
        copies.append((first, pltpu.make_async_copy(array, held.at[pl.ds(first, size)], sems.at[a])))
        first += size
    for _, copy in copies:
        copy.start()
    for g, (dz, dx) in enumerate([*news, *olds]):
        places[g] = lax.rem(z - dz + NZ, NZ) * NX + lax.rem(x - dx + NX, NX)

    def list_pairs(first_guest, last_guest, first_block):
        def list_guest(g, count):
            wanted = table[places[g]]

            def list_pair(r, count):
                listed[0, count] = r
                listed[1, count] = g
                return count + jnp.where(table[NZ * NX + r] == wanted, 1, 0)

            return lax.fori_loop(first_block, n_set, list_pair, count)

        count = lax.fori_loop(first_guest, last_guest, list_guest, 0)
        for u in range(UNROLL):
            listed[0, count + u] = first_block
            listed[1, count + u] = first_guest
        return count

    def run_pairs(count):
        @pl.loop(0, lax.div(count + UNROLL - 1, UNROLL))
        def _(step):
            for u in range(UNROLL):
                at = step * UNROLL + u
                r, g = listed[0, at], listed[1, at]
                keep = jnp.where(at < count, 1.0, 0.0)
                products = lax.dot_general(
                    blocks[r], held[g], (((1,), (1,)), ((), ())), preferred_element_type=jnp.float32
                )
                norm = norms[pl.ds(places[g], 1), :]
                total = rows[r]
                for half in range(BLOCK // LANES):
                    lanes = slice(half * LANES, (half + 1) * LANES)
                    tile = jnp.exp2(products[:, lanes] * scale[r] * norm[:, lanes]) * keep
                    total = total + tile
                    cols[g, :, lanes] += jnp.sum(tile.reshape(BLOCK // 8, 8, LANES), axis=0)
                rows[r] = total

    count = list_pairs(0, n_new, 0)
    cols[...] = jnp.zeros_like(cols)
    rows[...] = rows_in[...]
    cols_out[...] = cols_in[...]
    norms[...] = norms_in[...]
    next_turn[...] = turn[...]
    for first, copy in copies:
        if first < n_new:
            copy.wait()

    @pl.loop(0, n_new)
    def _(g):
        squares = jnp.zeros((BLOCK, LANES), jnp.float32)
        for part in range(held.shape[2] // LANES):
            values = held[g, :, part * LANES : (part + 1) * LANES].astype(jnp.float32)
            squares = squares + values * values
        norms[pl.ds(places[g], 1), :] = 1.0 / jnp.sqrt(lane_sums(squares) + EPSILON)

    run_pairs(count)
    if n_old:
        count = list_pairs(n_new, n_new + n_old, first_far)
        for first, copy in copies:
            if first >= n_new:
                copy.wait()
        run_pairs(count)

    @pl.loop(0, n_new + n_old)
    def _(g):
        cols_out[pl.ds(places[g], 1), :] += jnp.sum(cols[g], axis=0, keepdims=True)


def pairs(table, news, olds, arrays, first_far, blocks, scale, rows, cols, norms, turn):
    n_guest, n_set = len(news) + len(olds), blocks.shape[0]
    sizes = [a.shape[0] for a in arrays]
    smem = pl.BlockSpec(memory_space=pltpu.SMEM)
    vmem = pl.BlockSpec(memory_space=pltpu.VMEM)
    tiles = (len(news) * n_set + len(olds) * (n_set - first_far)) // 3
    return pl.pallas_call(
        functools.partial(pair_kernel, news, olds, sizes, first_far),
        in_specs=[smem] + [pl.BlockSpec(memory_space=pltpu.HBM)] * len(arrays) + [vmem] * 6,
        out_specs=[vmem] * 4,
        out_shape=[jax.ShapeDtypeStruct(v.shape, jnp.float32) for v in (rows, cols, norms, turn)],
        scratch_shapes=[
            pltpu.VMEM((n_guest, *arrays[0].shape[1:]), jnp.bfloat16),
            pltpu.VMEM((n_guest, 8, BLOCK), jnp.float32),
            pltpu.SMEM((2, n_guest * n_set + UNROLL), jnp.int32),
            pltpu.SMEM((n_guest,), jnp.int32),
            pltpu.SemaphoreType.DMA((len(arrays),)),
        ],
        input_output_aliases={1 + len(arrays) + 2 + j: j for j in range(3)},
        compiler_params=pltpu.CompilerParams(vmem_limit_bytes=63 << 20),
        cost_estimate=pl.CostEstimate(
            flops=tiles * 4 * BLOCK * BLOCK * 768, bytes_accessed=tiles * 400000, transcendentals=tiles * BLOCK * BLOCK
        ),
        name="pairs",
    )(table, *arrays, blocks, scale, rows, cols, norms, turn)


def body(home_rows, guest_rows, home_cluster, guest_cluster, pair_mask):
    slots = home_rows.shape[0] // BLOCK
    y, z, x, h, k = (lax.axis_index(a) for a in AXES)

    def device_of(yy, kk):
        return (((yy * NZ + z) * NX + x) * NH + h) * NK + kk

    table = jnp.concatenate([
        lax.dynamic_slice(guest_cluster.reshape(NY, NZ * NX, NH * NK), (y, 0, h * NK + k), (1, NZ * NX, 1)).reshape(-1),
        lax.dynamic_slice_in_dim(home_cluster, device_of(y, 1 - k) * slots, slots),
        lax.dynamic_slice_in_dim(home_cluster, device_of(1 - y, 1 - k) * slots, slots),
        jnp.stack([z, x]),
    ])

    def scaled(blocks):
        return jnp.broadcast_to((inverse_norms(blocks) * EXP2_SCALE)[..., None], (*blocks.shape[:2], LANES))

    def zeros(n):
        return jnp.zeros((n, BLOCK, LANES), jnp.float32)

    stacks = {((0, 0),): guest_rows[None]}

    def one(n):
        for nodes, blocks in stacks.items():
            if n in nodes:
                return blocks[nodes.index(n)]
        raise ValueError(n)

    def send(slot, after):
        sends = [(stacks[p] if p in stacks else jnp.stack([one(n) for n in p]), p, d) for d, p in slot]
        blocks, _ = lax.optimization_barrier((tuple(b for b, _, _ in sends), tuple(after)))
        made = []
        for block, (_, parents, (dz, dx)) in zip(blocks, sends, strict=True):
            made.append(tuple(node(n[0] + dz, n[1] + dx) for n in parents))
            stacks[made[-1]] = shift(block, dz, dx)
        return made

    def flat(groups):
        return [n for nodes in groups for n in nodes]

    far = to_partner(home_rows).reshape(slots, BLOCK, -1)
    near = to_sibling(home_rows).reshape(slots, BLOCK, -1)
    newest = [((0, 0),), *send(SLOTS[0][:3], []), *send(SLOTS[0][3:], [near])]
    blocks, scale, rows = near, scaled(near), zeros(slots)
    cols = norms = jnp.zeros((NZ * NX, BLOCK), jnp.float32)
    turn = jnp.zeros((8, LANES), jnp.float32)
    backlog, done = [], []
    for s in range(1, len(SLOTS) + 1):
        came = tuple(stacks[p] for p in newest)
        coming = send(SLOTS[s], [*came, *done]) if s < len(SLOTS) else []
        if s == IDS_AT:
            home_cluster, guest_cluster, _ = lax.optimization_barrier((home_cluster, guest_cluster, came))
        olds = []
        if s == FAR_FROM:
            far, _ = lax.optimization_barrier((far, came))
            blocks = jnp.concatenate([near, far])
            scale = jnp.concatenate([scale, scaled(far)])
            rows = jnp.concatenate([rows, zeros(slots)])
            olds = backlog
        rows, cols, norms, turn = pairs(
            table, flat(newest), flat(olds), [stacks[p] for p in [*newest, *olds]], slots, blocks, scale, rows, cols, norms,
            turn,
        )
        backlog = backlog + newest
        done = [turn]
        newest = coming
    near_rows, far_rows = rows[:slots], rows[slots:]

    incoming = lax.all_to_all(cols, ("z", "x"), 0, 0, tiled=True)
    guest_density = jnp.sum(incoming, axis=0)
    home_density = to_sibling(jnp.sum(near_rows, axis=-1)) + to_partner(jnp.sum(far_rows, axis=-1))

    home_ids = lax.dynamic_slice_in_dim(home_cluster, device_of(y, k) * slots, slots)
    guest_id = lax.dynamic_slice_in_dim(guest_cluster, device_of(y, k), 1)

    def members(ids):
        count = jnp.sum((home_cluster[None, :] == ids[:, None]).astype(jnp.int32), axis=1)
        count = count + jnp.sum((guest_cluster[None, :] == ids[:, None]).astype(jnp.int32), axis=1)
        return count.astype(jnp.float32)

    home_score = jnp.log(1.0 + home_density) - jnp.log(members(home_ids))[:, None]
    guest_score = jnp.log(1.0 + guest_density) - jnp.log(members(guest_id))
    return home_score.reshape(-1), guest_score


def solution(mesh):
    whole = Mesh(mesh.devices.reshape(NY, NZ, NX, NH, NK), AXES)
    placed = (P(AXES, None), P(AXES, None), P(), P(), P(AXES, None, None))
    return jax.shard_map(
        body, mesh=whole, in_specs=placed, out_specs=(P(AXES), P(AXES)), check_vma=False
    )
```

profile of v0, /device:TPU:1, one launch (start us, length us, event | category | flops | bytes accessed | tf_op | source)
XLA Modules:
  0.0 174.6 jit_solution(1513862137577911378)
XLA Ops:
  0.6 3.3 %collective-permute-start = (bf16[1536,768]{1,0:T(8,128)(2,1)}, bf16[1536,768]{1,0:T(8,128)(2,1)S(1)}, u32[]{:S(2)}, u32[]{:S(2)}) collective-permute-start(bf16[1536,768]{1,0:T(8,128)(2,1)} %param.5), channel_id=1, source_target_pairs={{0,1},{1,0},{2,3},{3,2},{4,5},{5,4},{6,7},{7,6},{8,9},{9,8},{10,11... | collective-permute-start | bytes 7077896 | tf_op jit(solution)/shard_map/ppermute | solution.py:51
  4.0 5.1 %collective-permute-start.2 = (bf16[1,256,768]{2,1,0:T(8,128)(2,1)}, bf16[1,256,768]{2,1,0:T(8,128)(2,1)S(1)}, u32[]{:S(2)}, u32[]{:S(2)}) collective-permute-start(bf16[1,256,768]{2,1,0:T(8,128)(2,1)} %bitcast.12), channel_id=1, source_target_pairs={{0,112},{16,0},{32,16},{48,32},{64,48},{80,64},{96,80},{112,96},{1... | collective-permute-start | bytes 1179656 | tf_op jit(solution)/shard_map/ppermute | solution.py:40
  9.1 1.2 collective-permute-start.3
  10.3 1.5 collective-permute-start.4
  11.8 0.8 reshape.64
  12.6 0.2 dynamic-slice_reduce_fusion
  12.8 0.9 fusion.1
  13.7 0.6 concatenate.12.table
  14.2 0.5 multiply_reduce_fusion.1
  14.8 2.7 %collective-permute-done.2.refs_2_.refs_6_ = bf16[1,256,768]{2,1,0:T(8,128)(2,1)S(1)} collective-permute-done((bf16[1,256,768]{2,1,0:T(8,128)(2,1)}, bf16[1,256,768]{2,1,0:T(8,128)(2,1)S(1)}, u32[]{:S(2)}, u32[]{:S(2)}) %collective-permute-start.2) | collective-permute-done | bytes 393248 | tf_op jit(solution)/shard_map/ppermute | solution.py:40
  17.5 3.1 %collective-permute-done.3.refs_1_.refs_5_ = bf16[1,256,768]{2,1,0:T(8,128)(2,1)S(1)} collective-permute-done((bf16[1,256,768]{2,1,0:T(8,128)(2,1)}, bf16[1,256,768]{2,1,0:T(8,128)(2,1)S(1)}, u32[]{:S(2)}, u32[]{:S(2)}) %collective-permute-start.3) | collective-permute-done | bytes 393248 | tf_op jit(solution)/shard_map/ppermute | solution.py:42
  20.6 2.1 %collective-permute-done.1.refs_4_.refs_8_ = bf16[1,256,768]{2,1,0:T(8,128)(2,1)} collective-permute-done((bf16[1,256,768]{2,1,0:T(8,128)(2,1)}, bf16[1,256,768]{2,1,0:T(8,128)(2,1)}, u32[]{:S(2)}, u32[]{:S(2)}) %collective-permute-start.1) | collective-permute-done | bytes 393248 | tf_op jit(solution)/shard_map/ppermute | solution.py:40
  22.6 2.7 %collective-permute-start.7 = (bf16[1,256,768]{2,1,0:T(8,128)(2,1)}, bf16[1,256,768]{2,1,0:T(8,128)(2,1)}, u32[]{:S(2)}, u32[]{:S(2)}) collective-permute-start(bf16[1,256,768]{2,1,0:T(8,128)(2,1)} %copy-done.7), channel_id=1, source_target_pairs={{0,112},{16,0},{32,16},{48,32},{64,48},{80,64},{96,80},{112,96},{1... | collective-permute-start | bytes 1179656 | tf_op jit(solution)/shard_map/ppermute | solution.py:40
  25.3 2.7 %collective-permute-start.8 = (bf16[1,256,768]{2,1,0:T(8,128)(2,1)}, bf16[1,256,768]{2,1,0:T(8,128)(2,1)}, u32[]{:S(2)}, u32[]{:S(2)}) collective-permute-start(bf16[1,256,768]{2,1,0:T(8,128)(2,1)} %copy-done.7), channel_id=1, source_target_pairs={{0,12},{4,0},{8,4},{12,8},{1,13},{5,1},{9,5},{13,9},{2,14},{6,2},{... | collective-permute-start | bytes 1179656 | tf_op jit(solution)/shard_map/ppermute | solution.py:42
  28.0 1.2 broadcast_in_dim.11.refs_6_.refs_5_
  29.2 0.6 broadcast_in_dim.13.refs_10_
  29.7 0.6 broadcast_in_dim.12.clone.refs_9_
  30.4 0.6 broadcast_in_dim.12.refs_8_
  31.0 0.9 broadcast_4_refs_7_.2.refs_7_
  31.9 7.2 %pairs.6 = (f32[6,256,128]{2,1,0:T(8,128)}, f32[32,256]{1,0:T(8,128)}, f32[32,256]{1,0:T(8,128)}, f32[8,128]{1,0:T(8,128)}) custom-call(s32[46]{0:T(128)} %concatenate.12.table, bf16[1,256,768]{2,1,0:T(8,128)(2,1)} %bitcast.16, bf16[1,256,768]{2,1,0:T(8,128)(2,1)} %copy-done.3, ...), custom_call_target="tpu_custom_call", output_to_operand_aliasing={{0}: (8, {}), {1}: (9, {}), {2}: (10, {})} | custom-call | flops 2013265920 | bytes 4000000 | tf_op jit(solution)/shard_map/pairs/pallas_call | solution.py:160
  39.1 0.1 collective-permute-start.9
  39.2 2.7 %collective-permute-start.10 = (bf16[1,256,768]{2,1,0:T(8,128)(2,1)}, bf16[1,256,768]{2,1,0:T(8,128)(2,1)}, u32[]{:S(2)}, u32[]{:S(2)}) collective-permute-start(bf16[1,256,768]{2,1,0:T(8,128)(2,1)} %collective-permute-done.7.refs_1_.refs_10_), channel_id=1, source_target_pairs={{0,112},{16,0},{32,16},{48,32},{64,48},{80,64},{96,80},{112,96},{1... | collective-permute-start | bytes 1179656 | tf_op jit(solution)/shard_map/ppermute | solution.py:40
  41.9 2.7 %collective-permute-start.12 = (bf16[1,256,768]{2,1,0:T(8,128)(2,1)}, bf16[1,256,768]{2,1,0:T(8,128)(2,1)}, u32[]{:S(2)}, u32[]{:S(2)}) collective-permute-start(bf16[1,256,768]{2,1,0:T(8,128)(2,1)} %collective-permute-done.1.refs_4_.refs_8_), channel_id=1, source_target_pairs={{0,12},{4,0},{8,4},{12,8},{1,13},{5,1},{9,5},{13,9},{2,14},{6,2},{... | collective-permute-start | bytes 1179656 | tf_op jit(solution)/shard_map/ppermute | solution.py:42
  44.6 1.2 pad_maximum_fusion.2
  45.8 6.8 %pairs.7 = (f32[6,256,128]{2,1,0:T(8,128)}, f32[32,256]{1,0:T(8,128)}, f32[32,256]{1,0:T(8,128)}, f32[8,128]{1,0:T(8,128)}) custom-call(s32[46]{0:T(128)} %concatenate.12.table, bf16[1,256,768]{2,1,0:T(8,128)(2,1)} %collective-permute-done.6.refs_0_.refs_9_, ...), custom_call_target="tpu_custom_call", output_to_operand_aliasing={{0}: (7, {}), {1}: (8, {}), {2}: (9, {})} | custom-call | flops 1610612736 | bytes 3200000 | tf_op jit(solution)/shard_map/pairs/pallas_call | solution.py:160
  52.6 2.1 %pad_maximum_fusion.3 = bf16[2,256,768]{2,1,0:T(8,128)(2,1)} fusion(bf16[1,256,768]{2,1,0:T(8,128)(2,1)} %collective-permute-done.10.refs_2_.refs_15_, bf16[1,256,768]{2,1,0:T(8,128)(2,1)} %collective-permute-done.9.refs_3_.refs_16_), kind=kLoop, calls=%fused_computation.5 | loop fusion | flops 393216 | bytes 1572864 | tf_op jit(solution)/shard_map/stack | solution.py:210
  54.7 1.5 collective-permute-start.14
  56.1 1.5 collective-permute-start.16
  57.6 0.6 dynamic_slice.19
  58.2 0.1 dynamic_slice.18
  58.2 6.8 %pairs.8 = (f32[6,256,128]{2,1,0:T(8,128)}, f32[32,256]{1,0:T(8,128)}, f32[32,256]{1,0:T(8,128)}, f32[8,128]{1,0:T(8,128)}) custom-call(s32[46]{0:T(128)} %concatenate.12.table, bf16[1,256,768]{2,1,0:T(8,128)(2,1)} %collective-permute-done.11.refs_0_.refs_13_, ...), custom_call_target="tpu_custom_call", output_to_operand_aliasing={{0}: (7, {}), {1}: (8, {}), {2}: (9, {})} | custom-call | flops 1610612736 | bytes 3200000 | tf_op jit(solution)/shard_map/pairs/pallas_call | solution.py:160
  65.0 2.6 %concatenate.15.refs_19_ = f32[12,256,128]{2,1,0:T(8,128)} pad(f32[6,256,128]{2,1,0:T(8,128)} %get-tuple-element.81, f32[]{:T(128)} %constant.16.clone.1), padding=0_6x0_0x0_0 | pad | bytes 2359300 | tf_op jit(solution)/shard_map/concatenate | solution.py:238
  67.6 1.4 convert_reduce_fusion.1
  69.0 0.2 convert_reduce_fusion.2
  69.2 0.2 convert_reduce_fusion
  69.4 0.1 collective-permute-done.14.refs_2_
  69.5 0.6 collective-permute-done.16.refs_1_
  70.1 2.2 %multiply_reduce_fusion = f32[6,256]{1,0:T(8,128)S(1)} fusion(bf16[6,256,768]{2,1,0:T(8,128)(2,1)} %bitcast.4), kind=kLoop, calls=%fused_computation.1 | loop fusion | flops 3537408 | bytes 2365440 | tf_op jit(solution)/shard_map/reduce_sum | solution.py:60
  72.3 4.3 %pad_maximum_fusion.refs_17_.refs_4_ = bf16[12,256,768]{2,1,0:T(8,128)(2,1)} fusion(bf16[6,256,768]{2,1,0:T(8,128)(2,1)} %bitcast.4, bf16[6,256,768]{2,1,0:T(8,128)(2,1)S(1)} %bitcast.10), kind=kLoop, calls=%fused_computation | loop fusion | flops 2359296 | bytes 9437184 | tf_op jit(solution)/shard_map/concatenate | solution.py:236
  76.6 1.6 collective-permute-start.20
  78.2 0.3 broadcast_in_dim.14
  78.5 1.3 pad_maximum_fusion.1.refs_18_.refs_5_
  79.8 3.7 %collective-permute-start.17 = (bf16[2,256,768]{2,1,0:T(8,128)(2,1)}, bf16[2,256,768]{2,1,0:T(8,128)(2,1)}, u32[]{:S(2)}, u32[]{:S(2)}) collective-permute-start(bf16[2,256,768]{2,1,0:T(8,128)(2,1)} %collective-permute-done.14.refs_2_), channel_id=1, source_target_pairs={{0,16},{16,32},{32,48},{48,64},{64,80},{80,96},{96,112},{112,0},{1... | collective-permute-start | bytes 2359304 | tf_op jit(solution)/shard_map/ppermute | solution.py:40
  83.5 18.5 %pairs.9 = (f32[12,256,128]{2,1,0:T(8,128)}, f32[32,256]{1,0:T(8,128)}, f32[32,256]{1,0:T(8,128)}, f32[8,128]{1,0:T(8,128)}) custom-call(s32[46]{0:T(128)} %concatenate.12.table, bf16[2,256,768]{2,1,0:T(8,128)(2,1)} %collective-permute-done.15.refs_0_, ...), custom_call_target="tpu_custom_call", output_to_operand_aliasing={{0}: (20, {}), {1}: (21, {}), {2}: (22, {})} | custom-call | flops 11676942336 | bytes 23200000 | tf_op jit(solution)/shard_map/pairs/pallas_call | solution.py:160
  102.0 1.0 slice.20
  103.0 0.6 collective-permute-done.18.refs_0_
  103.7 1.8 %slice.21 = bf16[1,256,768]{2,1,0:T(8,128)(2,1)} slice(bf16[2,256,768]{2,1,0:T(8,128)(2,1)} %collective-permute-done.18.refs_0_), slice={[0:1], [0:256], [0:768]} | slice | bytes 786432 | tf_op jit(solution)/shard_map/slice | solution.py:206
  105.4 1.0 slice.22
  106.5 3.5 %collective-permute-start.22 = (bf16[1,256,768]{2,1,0:T(8,128)(2,1)S(1)}, bf16[1,256,768]{2,1,0:T(8,128)(2,1)}, u32[]{:S(2)}, u32[]{:S(2)}) collective-permute-start(bf16[1,256,768]{2,1,0:T(8,128)(2,1)S(1)} %slice.20), channel_id=1, source_target_pairs={{0,4},{4,8},{8,12},{12,0},{1,5},{5,9},{9,13},{13,1},{2,6},{6,10},{... | collective-permute-start | bytes 1179656 | tf_op jit(solution)/shard_map/ppermute | solution.py:42
  110.0 0.3 collective-permute-start.23
  110.3 4.2 %collective-permute-start.24 = (bf16[1,256,768]{2,1,0:T(8,128)(2,1)}, bf16[1,256,768]{2,1,0:T(8,128)(2,1)}, u32[]{:S(2)}, u32[]{:S(2)}) collective-permute-start(bf16[1,256,768]{2,1,0:T(8,128)(2,1)} %collective-permute-done.9.refs_3_.refs_16_), channel_id=1, source_target_pairs={{0,16},{16,32},{32,48},{48,64},{64,80},{80,96},{96,112},{112,0},{1... | collective-permute-start | bytes 1179656 | tf_op jit(solution)/shard_map/ppermute | solution.py:40
  114.5 1.6 collective-permute-start.25
  116.1 12.9 %pairs.10 = (f32[12,256,128]{2,1,0:T(8,128)}, f32[32,256]{1,0:T(8,128)}, f32[32,256]{1,0:T(8,128)}, f32[8,128]{1,0:T(8,128)}) custom-call(s32[46]{0:T(128)} %concatenate.12.table, bf16[2,256,768]{2,1,0:T(8,128)(2,1)} %collective-permute-done.18.refs_0_, ...), custom_call_target="tpu_custom_call", output_to_operand_aliasing={{0}: (7, {}), {1}: (8, {}), {2}: (9, {})} | custom-call | flops 5637144576 | bytes 11200000 | tf_op jit(solution)/shard_map/pairs/pallas_call | solution.py:160
  129.0 9.6 %pairs.11 = (f32[12,256,128]{2,1,0:T(8,128)}, f32[32,256]{1,0:T(8,128)}, f32[32,256]{1,0:T(8,128)}, f32[8,128]{1,0:T(8,128)}) custom-call(s32[46]{0:T(128)} %concatenate.12.table, bf16[1,256,768]{2,1,0:T(8,128)(2,1)} %collective-permute-done.22.refs_0_, ...), custom_call_target="tpu_custom_call", output_to_operand_aliasing={{0}: (7, {}), {1}: (8, {}), {2}: (9, {})} | custom-call | flops 3221225472 | bytes 6400000 | tf_op jit(solution)/shard_map/pairs/pallas_call | solution.py:160
  138.7 1.8 %slice_reduce_fusion = (f32[6,256]{1,0:T(8,128)S(1)}, f32[6,256]{1,0:T(8,128)S(1)}) fusion(f32[12,256,128]{2,1,0:T(8,128)} %get-tuple-element.96), kind=kLoop, calls=%fused_computation.6 | loop fusion | flops 390144 | bytes 1585152 | tf_op jit(solution)/shard_map/reduce_sum | solution.py:251
  140.5 10.1 %collective-permute-start.27 = (f32[6,256]{1,0:T(8,128)S(1)}, f32[6,256]{1,0:T(8,128)S(1)}, u32[]{:S(2)}, u32[]{:S(2)}) collective-permute-start(f32[6,256]{1,0:T(8,128)S(1)} %get-tuple-element.100), channel_id=1, source_target_pairs={{0,129},{1,128},{128,1},{129,0},{2,131},{3,130},{130,3},{131,2},{4... | collective-permute-start | bytes 18440 | tf_op jit(solution)/shard_map/ppermute | solution.py:55
  150.6 1.3 fusion
  153.2 1.4 copy.25
  154.6 10.6 %all-to-all-start = ((f32[32,1,256]{2,1,0:T(1,128)}), f32[32,1,256]{2,1,0:T(1,128)S(1)}, u32[]{:S(2)}, u32[]{:S(2)}) async-start(f32[32,1,256]{2,1,0:T(1,128)} %copy.25), calls=%async_computation | async-start | bytes 65536 | tf_op jit(solution)/shard_map/all_to_all | solution.py:249
  165.3 0.1 log_subtract_fusion
  165.4 0.6 reshape.68
  166.0 8.0 %all-to-all-done = f32[32,1,256]{2,1,0:T(1,128)S(1)} async-done(((f32[32,1,256]{2,1,0:T(1,128)}), f32[32,1,256]{2,1,0:T(1,128)S(1)}, u32[]{:S(2)}, u32[]{:S(2)}) %all-to-all-start) | async-done | bytes 32800 | tf_op jit(solution)/shard_map/all_to_all | solution.py:249
  174.0 0.1 reduce_sum.87
  174.0 0.6 log_subtract_fusion.1
  (52 shorter events, 0.2 us)
Async XLA Ops:
  0.6 11.1 %collective-permute-start = (bf16[1536,768]{1,0:T(8,128)(2,1)}, bf16[1536,768]{1,0:T(8,128)(2,1)S(1)}, u32[]{:S(2)}, u32[]{:S(2)}) collective-permute-start(bf16[1536,768]{1,0:T(8,128)(2,1)} %param.5), channel_id=1, source_target_pairs={{0,1},{1,0},{2,3},{3,2},{4,5},{5,4},{6,7},{7,6},{8,9},{9,8},{10,11... | collective-permute-start | bytes 7077896 | tf_op jit(solution)/shard_map/ppermute | solution.py:51
  4.0 65.4 %collective-permute-start.21 = (bf16[1536,768]{1,0:T(8,128)(2,1)}, bf16[1536,768]{1,0:T(8,128)(2,1)}, u32[]{:S(2)}, u32[]{:S(2)}) collective-permute-start(bf16[1536,768]{1,0:T(8,128)(2,1)} %param.5), channel_id=1, source_target_pairs={{0,129},{1,128},{128,1},{129,0},{2,131},{3,130},{130,3},{131,2},{4... | collective-permute-start | bytes 7077896 | tf_op jit(solution)/shard_map/ppermute | solution.py:55
  4.0 13.5 %collective-permute-start.2 = (bf16[1,256,768]{2,1,0:T(8,128)(2,1)}, bf16[1,256,768]{2,1,0:T(8,128)(2,1)S(1)}, u32[]{:S(2)}, u32[]{:S(2)}) collective-permute-start(bf16[1,256,768]{2,1,0:T(8,128)(2,1)} %bitcast.12), channel_id=1, source_target_pairs={{0,112},{16,0},{32,16},{48,32},{64,48},{80,64},{96,80},{112,96},{1... | collective-permute-start | bytes 1179656 | tf_op jit(solution)/shard_map/ppermute | solution.py:40
  9.1 11.5 %collective-permute-start.3 = (bf16[1,256,768]{2,1,0:T(8,128)(2,1)}, bf16[1,256,768]{2,1,0:T(8,128)(2,1)S(1)}, u32[]{:S(2)}, u32[]{:S(2)}) collective-permute-start(bf16[1,256,768]{2,1,0:T(8,128)(2,1)} %bitcast.13), channel_id=1, source_target_pairs={{0,4},{4,8},{8,12},{12,0},{1,5},{5,9},{9,13},{13,1},{2,6},{6,10},{... | collective-permute-start | bytes 1179656 | tf_op jit(solution)/shard_map/ppermute | solution.py:42
  10.3 10.3 %collective-permute-start.4 = (bf16[1,256,768]{2,1,0:T(8,128)(2,1)}, bf16[1,256,768]{2,1,0:T(8,128)(2,1)}, u32[]{:S(2)}, u32[]{:S(2)}) collective-permute-start(bf16[1,256,768]{2,1,0:T(8,128)(2,1)} %bitcast.14), channel_id=1, source_target_pairs={{0,12},{4,0},{8,4},{12,8},{1,13},{5,1},{9,5},{13,9},{2,14},{6,2},{... | collective-permute-start | bytes 1179656 | tf_op jit(solution)/shard_map/ppermute | solution.py:42
  11.8 2.5 %copy-start = (bf16[1536,768]{1,0:T(8,128)(2,1)}, bf16[1536,768]{1,0:T(8,128)(2,1)S(1)}, u32[]{:S(2)}) copy-start(bf16[1536,768]{1,0:T(8,128)(2,1)S(1)} %collective-permute-done) | copy-start | bytes 7077892
  11.8 10.9 %collective-permute-start.1 = (bf16[1,256,768]{2,1,0:T(8,128)(2,1)}, bf16[1,256,768]{2,1,0:T(8,128)(2,1)}, u32[]{:S(2)}, u32[]{:S(2)}) collective-permute-start(bf16[1,256,768]{2,1,0:T(8,128)(2,1)} %bitcast.15), channel_id=1, source_target_pairs={{0,16},{16,32},{32,48},{48,64},{64,80},{80,96},{96,112},{112,0},{1... | collective-permute-start | bytes 1179656 | tf_op jit(solution)/shard_map/ppermute | solution.py:40
  17.5 3.1 %copy-start.7 = (bf16[1,256,768]{2,1,0:T(8,128)(2,1)}, bf16[1,256,768]{2,1,0:T(8,128)(2,1)S(1)}, u32[]{:S(2)}) copy-start(bf16[1,256,768]{2,1,0:T(8,128)(2,1)S(1)} %collective-permute-done.2.refs_2_.refs_6_) | copy-start | bytes 1179652
  20.5 11.4 %copy-start.3 = (bf16[1,256,768]{2,1,0:T(8,128)(2,1)}, bf16[1,256,768]{2,1,0:T(8,128)(2,1)S(1)}, u32[]{:S(2)}) copy-start(bf16[1,256,768]{2,1,0:T(8,128)(2,1)S(1)} %collective-permute-done.3.refs_1_.refs_5_) | copy-start | bytes 1179652
  22.6 16.5 %collective-permute-start.5 = (bf16[1,256,768]{2,1,0:T(8,128)(2,1)S(1)}, bf16[1,256,768]{2,1,0:T(8,128)(2,1)S(1)}, u32[]{:S(2)}, u32[]{:S(2)}) collective-permute-start(bf16[1,256,768]{2,1,0:T(8,128)(2,1)S(1)} %collective-permute-done.3.refs_1_.refs_5_), channel_id=1, source_target_pairs={{0,4},{4,8},{8,12},{12,0},{1,5},{5,9},{9,13},{13,1},{2,6},{6,10},{... | collective-permute-start | bytes 1179656 | tf_op jit(solution)/shard_map/ppermute | solution.py:42
  22.6 16.5 %collective-permute-start.6 = (bf16[1,256,768]{2,1,0:T(8,128)(2,1)}, bf16[1,256,768]{2,1,0:T(8,128)(2,1)}, u32[]{:S(2)}, u32[]{:S(2)}) collective-permute-start(bf16[1,256,768]{2,1,0:T(8,128)(2,1)} %collective-permute-done.1.refs_4_.refs_8_), channel_id=1, source_target_pairs={{0,16},{16,32},{32,48},{48,64},{64,80},{80,96},{96,112},{112,0},{1... | collective-permute-start | bytes 1179656 | tf_op jit(solution)/shard_map/ppermute | solution.py:40
  22.6 16.5 %collective-permute-start.7 = (bf16[1,256,768]{2,1,0:T(8,128)(2,1)}, bf16[1,256,768]{2,1,0:T(8,128)(2,1)}, u32[]{:S(2)}, u32[]{:S(2)}) collective-permute-start(bf16[1,256,768]{2,1,0:T(8,128)(2,1)} %copy-done.7), channel_id=1, source_target_pairs={{0,112},{16,0},{32,16},{48,32},{64,48},{80,64},{96,80},{112,96},{1... | collective-permute-start | bytes 1179656 | tf_op jit(solution)/shard_map/ppermute | solution.py:40
  25.3 13.8 %collective-permute-start.8 = (bf16[1,256,768]{2,1,0:T(8,128)(2,1)}, bf16[1,256,768]{2,1,0:T(8,128)(2,1)}, u32[]{:S(2)}, u32[]{:S(2)}) collective-permute-start(bf16[1,256,768]{2,1,0:T(8,128)(2,1)} %copy-done.7), channel_id=1, source_target_pairs={{0,12},{4,0},{8,4},{12,8},{1,13},{5,1},{9,5},{13,9},{2,14},{6,2},{... | collective-permute-start | bytes 1179656 | tf_op jit(solution)/shard_map/ppermute | solution.py:42
  39.1 2.8 %copy-start.4 = (bf16[1,256,768]{2,1,0:T(8,128)(2,1)}, bf16[1,256,768]{2,1,0:T(8,128)(2,1)S(1)}, u32[]{:S(2)}) copy-start(bf16[1,256,768]{2,1,0:T(8,128)(2,1)S(1)} %collective-permute-done.5.refs_2_.refs_11_) | copy-start | bytes 1179652
  39.1 13.4 %collective-permute-start.9 = (bf16[1,256,768]{2,1,0:T(8,128)(2,1)}, bf16[1,256,768]{2,1,0:T(8,128)(2,1)}, u32[]{:S(2)}, u32[]{:S(2)}) collective-permute-start(bf16[1,256,768]{2,1,0:T(8,128)(2,1)} %collective-permute-done.6.refs_0_.refs_9_), channel_id=1, source_target_pairs={{0,16},{16,32},{32,48},{48,64},{64,80},{80,96},{96,112},{112,0},{1... | collective-permute-start | bytes 1179656 | tf_op jit(solution)/shard_map/ppermute | solution.py:40
  39.2 13.3 %collective-permute-start.10 = (bf16[1,256,768]{2,1,0:T(8,128)(2,1)}, bf16[1,256,768]{2,1,0:T(8,128)(2,1)}, u32[]{:S(2)}, u32[]{:S(2)}) collective-permute-start(bf16[1,256,768]{2,1,0:T(8,128)(2,1)} %collective-permute-done.7.refs_1_.refs_10_), channel_id=1, source_target_pairs={{0,112},{16,0},{32,16},{48,32},{64,48},{80,64},{96,80},{112,96},{1... | collective-permute-start | bytes 1179656 | tf_op jit(solution)/shard_map/ppermute | solution.py:40
  41.9 12.7 %collective-permute-start.11 = (bf16[1,256,768]{2,1,0:T(8,128)(2,1)}, bf16[1,256,768]{2,1,0:T(8,128)(2,1)}, u32[]{:S(2)}, u32[]{:S(2)}) collective-permute-start(bf16[1,256,768]{2,1,0:T(8,128)(2,1)} %collective-permute-done.6.refs_0_.refs_9_), channel_id=1, source_target_pairs={{0,4},{4,8},{8,12},{12,0},{1,5},{5,9},{9,13},{13,1},{2,6},{6,10},{... | collective-permute-start | bytes 1179656 | tf_op jit(solution)/shard_map/ppermute | solution.py:42
  41.9 12.7 %collective-permute-start.12 = (bf16[1,256,768]{2,1,0:T(8,128)(2,1)}, bf16[1,256,768]{2,1,0:T(8,128)(2,1)}, u32[]{:S(2)}, u32[]{:S(2)}) collective-permute-start(bf16[1,256,768]{2,1,0:T(8,128)(2,1)} %collective-permute-done.1.refs_4_.refs_8_), channel_id=1, source_target_pairs={{0,12},{4,0},{8,4},{12,8},{1,13},{5,1},{9,5},{13,9},{2,14},{6,2},{... | collective-permute-start | bytes 1179656 | tf_op jit(solution)/shard_map/ppermute | solution.py:42
  45.8 11.8 %copy-start.6 = (s32[256]{0:T(256)S(1)}, s32[256]{0:T(256)}, u32[]{:S(2)}) copy-start(s32[256]{0:T(256)} %param.8) | copy-start | bytes 3076
  45.8 12.4 %copy-start.5 = (s32[1536]{0:T(1024)S(1)}, s32[1536]{0:T(1024)}, u32[]{:S(2)}) copy-start(s32[1536]{0:T(1024)} %param.7) | copy-start | bytes 18436
  54.6 14.8 %collective-permute-start.13 = (bf16[2,256,768]{2,1,0:T(8,128)(2,1)}, bf16[2,256,768]{2,1,0:T(8,128)(2,1)}, u32[]{:S(2)}, u32[]{:S(2)}) collective-permute-start(bf16[2,256,768]{2,1,0:T(8,128)(2,1)} %pad_maximum_fusion.3), channel_id=1, source_target_pairs={{0,12},{4,0},{8,4},{12,8},{1,13},{5,1},{9,5},{13,9},{2,14},{6,2},{... | collective-permute-start | bytes 2359304 | tf_op jit(solution)/shard_map/ppermute | solution.py:42
  54.7 14.8 %collective-permute-start.14 = (bf16[2,256,768]{2,1,0:T(8,128)(2,1)}, bf16[2,256,768]{2,1,0:T(8,128)(2,1)}, u32[]{:S(2)}, u32[]{:S(2)}) collective-permute-start(bf16[2,256,768]{2,1,0:T(8,128)(2,1)} %pad_maximum_fusion.3), channel_id=1, source_target_pairs={{0,4},{4,8},{8,12},{12,0},{1,5},{5,9},{9,13},{13,1},{2,6},{6,10},{... | collective-permute-start | bytes 2359304 | tf_op jit(solution)/shard_map/ppermute | solution.py:42
  56.1 13.4 %collective-permute-start.15 = (bf16[2,256,768]{2,1,0:T(8,128)(2,1)S(1)}, bf16[2,256,768]{2,1,0:T(8,128)(2,1)}, u32[]{:S(2)}, u32[]{:S(2)}) collective-permute-start(bf16[2,256,768]{2,1,0:T(8,128)(2,1)S(1)} %pad_maximum_fusion.2), channel_id=1, source_target_pairs={{0,112},{16,0},{32,16},{48,32},{64,48},{80,64},{96,80},{112,96},{1... | collective-permute-start | bytes 2359304 | tf_op jit(solution)/shard_map/ppermute | solution.py:40
  56.1 14.0 %collective-permute-start.16 = (bf16[2,256,768]{2,1,0:T(8,128)(2,1)S(1)}, bf16[2,256,768]{2,1,0:T(8,128)(2,1)}, u32[]{:S(2)}, u32[]{:S(2)}) collective-permute-start(bf16[2,256,768]{2,1,0:T(8,128)(2,1)S(1)} %pad_maximum_fusion.2), channel_id=1, source_target_pairs={{0,16},{16,32},{32,48},{48,64},{64,80},{80,96},{96,112},{112,0},{1... | collective-permute-start | bytes 2359304 | tf_op jit(solution)/shard_map/ppermute | solution.py:40
  65.0 7.3 %copy-start.1 = (bf16[1536,768]{1,0:T(8,128)(2,1)S(1)}, bf16[1536,768]{1,0:T(8,128)(2,1)}, u32[]{:S(2)}) copy-start(bf16[1536,768]{1,0:T(8,128)(2,1)} %copy-done) | copy-start | bytes 7077892
  72.3 6.1 %copy-start.2 = (f32[6,256,128]{2,1,0:T(8,128)S(1)}, f32[6,256,128]{2,1,0:T(8,128)}, u32[]{:S(2)}) copy-start(f32[6,256,128]{2,1,0:T(8,128)} %broadcast_in_dim.11.refs_6_.refs_5_) | copy-start | bytes 2359300
  76.6 29.8 %collective-permute-start.20 = (bf16[1,256,768]{2,1,0:T(8,128)(2,1)}, bf16[1,256,768]{2,1,0:T(8,128)(2,1)}, u32[]{:S(2)}, u32[]{:S(2)}) collective-permute-start(bf16[1,256,768]{2,1,0:T(8,128)(2,1)} %collective-permute-done.7.refs_1_.refs_10_), channel_id=1, source_target_pairs={{0,12},{4,0},{8,4},{12,8},{1,13},{5,1},{9,5},{13,9},{2,14},{6,2},{... | collective-permute-start | bytes 1179656 | tf_op jit(solution)/shard_map/ppermute | solution.py:42
  79.8 22.2 %collective-permute-start.17 = (bf16[2,256,768]{2,1,0:T(8,128)(2,1)}, bf16[2,256,768]{2,1,0:T(8,128)(2,1)}, u32[]{:S(2)}, u32[]{:S(2)}) collective-permute-start(bf16[2,256,768]{2,1,0:T(8,128)(2,1)} %collective-permute-done.14.refs_2_), channel_id=1, source_target_pairs={{0,16},{16,32},{32,48},{48,64},{64,80},{80,96},{96,112},{112,0},{1... | collective-permute-start | bytes 2359304 | tf_op jit(solution)/shard_map/ppermute | solution.py:40
  83.4 20.2 %collective-permute-start.18 = (bf16[2,256,768]{2,1,0:T(8,128)(2,1)}, bf16[2,256,768]{2,1,0:T(8,128)(2,1)}, u32[]{:S(2)}, u32[]{:S(2)}) collective-permute-start(bf16[2,256,768]{2,1,0:T(8,128)(2,1)} %collective-permute-done.13.refs_3_), channel_id=1, source_target_pairs={{0,112},{16,0},{32,16},{48,32},{64,48},{80,64},{96,80},{112,96},{1... | collective-permute-start | bytes 2359304 | tf_op jit(solution)/shard_map/ppermute | solution.py:40
  83.5 22.0 %collective-permute-start.19 = (bf16[2,256,768]{2,1,0:T(8,128)(2,1)}, bf16[2,256,768]{2,1,0:T(8,128)(2,1)}, u32[]{:S(2)}, u32[]{:S(2)}) collective-permute-start(bf16[2,256,768]{2,1,0:T(8,128)(2,1)} %collective-permute-done.14.refs_2_), channel_id=1, source_target_pairs={{0,4},{4,8},{8,12},{12,0},{1,5},{5,9},{9,13},{13,1},{2,6},{6,10},{... | collective-permute-start | bytes 2359304 | tf_op jit(solution)/shard_map/ppermute | solution.py:42
  106.5 22.5 %collective-permute-start.22 = (bf16[1,256,768]{2,1,0:T(8,128)(2,1)S(1)}, bf16[1,256,768]{2,1,0:T(8,128)(2,1)}, u32[]{:S(2)}, u32[]{:S(2)}) collective-permute-start(bf16[1,256,768]{2,1,0:T(8,128)(2,1)S(1)} %slice.20), channel_id=1, source_target_pairs={{0,4},{4,8},{8,12},{12,0},{1,5},{5,9},{9,13},{13,1},{2,6},{6,10},{... | collective-permute-start | bytes 1179656 | tf_op jit(solution)/shard_map/ppermute | solution.py:42
  110.0 19.0 %collective-permute-start.23 = (bf16[1,256,768]{2,1,0:T(8,128)(2,1)}, bf16[1,256,768]{2,1,0:T(8,128)(2,1)}, u32[]{:S(2)}, u32[]{:S(2)}) collective-permute-start(bf16[1,256,768]{2,1,0:T(8,128)(2,1)} %slice.21), channel_id=1, source_target_pairs={{0,12},{4,0},{8,4},{12,8},{1,13},{5,1},{9,5},{13,9},{2,14},{6,2},{... | collective-permute-start | bytes 1179656 | tf_op jit(solution)/shard_map/ppermute | solution.py:42
  110.3 18.7 %collective-permute-start.24 = (bf16[1,256,768]{2,1,0:T(8,128)(2,1)}, bf16[1,256,768]{2,1,0:T(8,128)(2,1)}, u32[]{:S(2)}, u32[]{:S(2)}) collective-permute-start(bf16[1,256,768]{2,1,0:T(8,128)(2,1)} %collective-permute-done.9.refs_3_.refs_16_), channel_id=1, source_target_pairs={{0,16},{16,32},{32,48},{48,64},{64,80},{80,96},{96,112},{112,0},{1... | collective-permute-start | bytes 1179656 | tf_op jit(solution)/shard_map/ppermute | solution.py:40
  114.5 14.5 %collective-permute-start.25 = (bf16[1,256,768]{2,1,0:T(8,128)(2,1)S(1)}, bf16[1,256,768]{2,1,0:T(8,128)(2,1)}, u32[]{:S(2)}, u32[]{:S(2)}) collective-permute-start(bf16[1,256,768]{2,1,0:T(8,128)(2,1)S(1)} %slice.22), channel_id=1, source_target_pairs={{0,112},{16,0},{32,16},{48,32},{64,48},{80,64},{96,80},{112,96},{1... | collective-permute-start | bytes 1179656 | tf_op jit(solution)/shard_map/ppermute | solution.py:40
  140.5 24.8 %collective-permute-start.27 = (f32[6,256]{1,0:T(8,128)S(1)}, f32[6,256]{1,0:T(8,128)S(1)}, u32[]{:S(2)}, u32[]{:S(2)}) collective-permute-start(f32[6,256]{1,0:T(8,128)S(1)} %get-tuple-element.100), channel_id=1, source_target_pairs={{0,129},{1,128},{128,1},{129,0},{2,131},{3,130},{130,3},{131,2},{4... | collective-permute-start | bytes 18440 | tf_op jit(solution)/shard_map/ppermute | solution.py:55
  150.6 14.7 %collective-permute-start.26 = (f32[6,256]{1,0:T(8,128)S(1)}, f32[6,256]{1,0:T(8,128)S(1)}, u32[]{:S(2)}, u32[]{:S(2)}) collective-permute-start(f32[6,256]{1,0:T(8,128)S(1)} %get-tuple-element.101), channel_id=1, source_target_pairs={{0,1},{1,0},{2,3},{3,2},{4,5},{5,4},{6,7},{7,6},{8,9},{9,8},{10,11... | collective-permute-start | bytes 18440 | tf_op jit(solution)/shard_map/ppermute | solution.py:51
  154.6 19.3 %all-to-all-start = ((f32[32,1,256]{2,1,0:T(1,128)}), f32[32,1,256]{2,1,0:T(1,128)S(1)}, u32[]{:S(2)}, u32[]{:S(2)}) async-start(f32[32,1,256]{2,1,0:T(1,128)} %copy.25), calls=%async_computation | async-start | bytes 65536 | tf_op jit(solution)/shard_map/all_to_all | solution.py:249
where the time goes:
time: 175 us
  Pallas kernels  61.8 us (35%)
  starting transfers between devices  60.4 us (35%)
  waiting for transfers between devices  17.2 us (10%)
  other arithmetic  17.1 us (10%)
  local copies, waits for them, and re-layouts  15.7 us (9%)
  between operations  2.37 us (1%)
    pallas_call x6, Pallas kernels, pairs(): pl.pallas_call(functools.partial(pair_kernel, news, olds, sizes, first_fa...  61.8 us
    ppermute x12, starting transfers between devices, shift(): return lax.ppermute(value, 'z', [(i, (i + dz) % NZ) for i in range(NZ)])  21.4 us
    ppermute x12, starting transfers between devices, shift(): return lax.ppermute(value, 'x', [(i, (i + dx) % NX) for i in range(NX)])  15 us
    all_to_all x1, starting transfers between devices, body(): incoming = lax.all_to_all(cols, ('z', 'x'), 0, 0, tiled=True)  10.6 us
    ppermute x2, starting transfers between devices, to_partner(): return lax.ppermute(value, ('y', 'k'), [(0, 3), (1, 2), (2, 1), (3, 0)])  10.1 us
    all_to_all x1, waiting for transfers between devices, body(): incoming = lax.all_to_all(cols, ('z', 'x'), 0, 0, tiled=True)  8 us
    ppermute x12, waiting for transfers between devices, shift(): return lax.ppermute(value, 'z', [(i, (i + dz) % NZ) for i in range(NZ)])  5.98 us
    concatenate x1, other arithmetic, body(): blocks = jnp.concatenate([near, far])  4.28 us
  transfers between devices with their start and end apart: 29, of which 7 were waited for; matrix products, arithmetic and copies ran while one was open for 14% of the time, Pallas kernels for 30%

commit v1 on v0

--- a/solution.py
+++ b/solution.py
@@ -15,6 +15,7 @@
 EPSILON = 1e-06
 EXP2_SCALE = SHARPNESS / math.log(2.0)
 UNROLL = 4
+VMEM_MIB = 63
 FAR_FROM = 4
 IDS_AT = 3
 
@@ -55,32 +56,55 @@
     return lax.ppermute(value, ("y", "k"), [(0, 3), (1, 2), (2, 1), (3, 0)])
 
 
-def inverse_norms(rows):
-    values = rows.astype(jnp.float32)
-    return 1.0 / jnp.sqrt(jnp.sum(values * values, axis=-1) + EPSILON)
-
-
-def lane_sums(values):
+def three_terms(values):
     high = values.astype(jnp.bfloat16)
     rest = values - high.astype(jnp.float32)
     middle = rest.astype(jnp.bfloat16)
-    low = (rest - middle.astype(jnp.float32)).astype(jnp.bfloat16)
-    terms = jnp.concatenate([high, middle, low], axis=1)
+    return high, middle, (rest - middle.astype(jnp.float32)).astype(jnp.bfloat16)
+
+
+def lane_sums(values):
+    terms = jnp.concatenate(three_terms(values), axis=1)
     ones = jnp.ones((8, terms.shape[1]), jnp.bfloat16)
     return lax.dot_general(ones, terms, (((1,), (1,)), ((), ())), preferred_element_type=jnp.float32)[:1]
 
 
-def pair_kernel(news, olds, sizes, first_far, table, *refs):
+def as_column(row):
+    at = lax.broadcasted_iota(jnp.int32, (16, row.shape[1]), 0)
+    terms = jnp.zeros((16, row.shape[1]), jnp.float32)
+    for i, term in enumerate(three_terms(row)):
+        terms = jnp.where(at == i, term.astype(jnp.float32), terms)
+    ones = jnp.ones((16, LANES), jnp.bfloat16)
+    return lax.dot_general(
+        terms.astype(jnp.bfloat16), ones, (((0,), (0,)), ((), ())), preferred_element_type=jnp.float32
+    )
+
+
+def pair_kernel(news, olds, sizes, n_sets, first, table, *refs):
     arrays, refs = refs[: len(sizes)], refs[len(sizes) :]
-    blocks, scale, rows_in, cols_in, norms_in, turn, rows, cols_out, norms, next_turn, held, cols, listed, places, sems = refs
-    n_new, n_old, n_set = len(news), len(olds), blocks.shape[0]
+    sets, refs = refs[:n_sets], refs[n_sets:]
+    before, refs = ((), refs) if first else (refs[:5], refs[5:])
+    rows, cols, norms, scale, next_turn, held, blocks, columns, sums, listed, places, sems = refs
+    n_new, n_guest = len(news), len(news) + len(olds)
+    n_set, n_each = blocks.shape[0], sets[0].shape[0]
     z, x = table[table.shape[0] - 2], table[table.shape[0] - 1]
-    copies, first = [], 0
+
+    guest_copies, at = [], 0
     for a, (array, size) in enumerate(zip(arrays, sizes, strict=True)):
-        copies.append((first, pltpu.make_async_copy(array, held.at[pl.ds(first, size)], sems.at[a])))
-        first += size
-    for _, copy in copies:
+        guest_copies.append((at, pltpu.make_async_copy(array, held.at[pl.ds(at, size)], sems.at[a])))
+        at += size
+    set_copies = [
+        pltpu.make_async_copy(one, blocks.at[pl.ds(j * n_each, n_each)], sems.at[len(sizes) + j])
+        for j, one in enumerate(sets)
+    ]
+    for at, copy in guest_copies:
+        if at < n_new:
+            copy.start()
+    for copy in set_copies:
         copy.start()
+    for at, copy in guest_copies:
+        if at >= n_new:
+            copy.start()
     for g, (dz, dx) in enumerate([*news, *olds]):
         places[g] = lax.rem(z - dz + NZ, NZ) * NX + lax.rem(x - dx + NX, NX)
 
@@ -109,73 +133,91 @@
                 r, g = listed[0, at], listed[1, at]
                 keep = jnp.where(at < count, 1.0, 0.0)
                 products = lax.dot_general(
-                    blocks[r], held[g], (((1,), (1,)), ((), ())), preferred_element_type=jnp.float32
+                    held[g], blocks[r], (((1,), (1,)), ((), ())), preferred_element_type=jnp.float32
                 )
-                norm = norms[pl.ds(places[g], 1), :]
-                total = rows[r]
+                across, down = scale[pl.ds(r, 1), :], columns[g]
+                total = sums[g]
                 for half in range(BLOCK // LANES):
                     lanes = slice(half * LANES, (half + 1) * LANES)
-                    tile = jnp.exp2(products[:, lanes] * scale[r] * norm[:, lanes]) * keep
+                    tile = jnp.exp2(products[:, lanes] * down * across[:, lanes]) * keep
                     total = total + tile
-                    cols[g, :, lanes] += jnp.sum(tile.reshape(BLOCK // 8, 8, LANES), axis=0)
-                rows[r] = total
+                    rows[r, :, lanes] += jnp.sum(tile.reshape(BLOCK // 8, 8, LANES), axis=0)
+                sums[g] = total
 
     count = list_pairs(0, n_new, 0)
-    cols[...] = jnp.zeros_like(cols)
-    rows[...] = rows_in[...]
-    cols_out[...] = cols_in[...]
-    norms[...] = norms_in[...]
-    next_turn[...] = turn[...]
-    for first, copy in copies:
-        if first < n_new:
+    if first:
+        for out in (rows, cols, norms, scale, next_turn):
+            out[...] = jnp.zeros_like(out)
+    else:
+        for out, value in zip((rows, cols, norms, scale, next_turn), before, strict=True):
+            out[...] = value[...]
+    sums[...] = jnp.zeros_like(sums)
+    for at, copy in guest_copies:
+        if at < n_new:
             copy.wait()
+
+    def inverse_norms(block):
+        squares = jnp.zeros((BLOCK, LANES), jnp.float32)
+        for part in range(block.shape[1] // LANES):
+            values = block[:, part * LANES : (part + 1) * LANES].astype(jnp.float32)
+            squares = squares + values * values
+        return 1.0 / jnp.sqrt(lane_sums(squares) + EPSILON)
 
     @pl.loop(0, n_new)
     def _(g):
-        squares = jnp.zeros((BLOCK, LANES), jnp.float32)
-        for part in range(held.shape[2] // LANES):
-            values = held[g, :, part * LANES : (part + 1) * LANES].astype(jnp.float32)
-            squares = squares + values * values
-        norms[pl.ds(places[g], 1), :] = 1.0 / jnp.sqrt(lane_sums(squares) + EPSILON)
+        norms[pl.ds(places[g], 1), :] = inverse_norms(held.at[g])
+
+    @pl.loop(0, n_guest)
+    def _(g):
+        columns[g] = as_column(norms[pl.ds(places[g], 1), :])
+
+    for copy in set_copies:
+        copy.wait()
+    if first or olds:
+
+        @pl.loop(n_set - n_each, n_set)
+        def _(r):
+            scale[pl.ds(r, 1), :] = inverse_norms(blocks.at[r]) * EXP2_SCALE
 
     run_pairs(count)
-    if n_old:
-        count = list_pairs(n_new, n_new + n_old, first_far)
-        for first, copy in copies:
-            if first >= n_new:
+    if olds:
+        count = list_pairs(n_new, n_guest, n_set - n_each)
+        for at, copy in guest_copies:
+            if at >= n_new:
                 copy.wait()
         run_pairs(count)
 
-    @pl.loop(0, n_new + n_old)
+    @pl.loop(0, n_guest)
     def _(g):
-        cols_out[pl.ds(places[g], 1), :] += jnp.sum(cols[g], axis=0, keepdims=True)
-
-
-def pairs(table, news, olds, arrays, first_far, blocks, scale, rows, cols, norms, turn):
-    n_guest, n_set = len(news) + len(olds), blocks.shape[0]
-    sizes = [a.shape[0] for a in arrays]
-    smem = pl.BlockSpec(memory_space=pltpu.SMEM)
-    vmem = pl.BlockSpec(memory_space=pltpu.VMEM)
-    tiles = (len(news) * n_set + len(olds) * (n_set - first_far)) // 3
+        cols[pl.ds(places[g], 1), :] += lane_sums(sums[g])
+
+
+def pairs(table, news, olds, arrays, sets, running):
+    n_guest, n_set = len(news) + len(olds), sum(one.shape[0] for one in sets)
+    smem, vmem, hbm = (pl.BlockSpec(memory_space=m) for m in (pltpu.SMEM, pltpu.VMEM, pltpu.HBM))
+    first = running is None
+    tiles = (len(news) * n_set + len(olds) * sets[-1].shape[0]) // 3
+    shapes = [(2 * sets[0].shape[0], 8, BLOCK), (NZ * NX, BLOCK), (NZ * NX, BLOCK), (16, BLOCK), (8, LANES)]
     return pl.pallas_call(
-        functools.partial(pair_kernel, news, olds, sizes, first_far),
-        in_specs=[smem] + [pl.BlockSpec(memory_space=pltpu.HBM)] * len(arrays) + [vmem] * 6,
-        out_specs=[vmem] * 4,
-        out_shape=[jax.ShapeDtypeStruct(v.shape, jnp.float32) for v in (rows, cols, norms, turn)],
+        functools.partial(pair_kernel, news, olds, [a.shape[0] for a in arrays], len(sets), first),
+        in_specs=[smem] + [hbm] * (len(arrays) + len(sets)) + [vmem] * (0 if first else 5),
+        out_specs=[vmem] * 5,
+        out_shape=[jax.ShapeDtypeStruct(shape, jnp.float32) for shape in shapes],
         scratch_shapes=[
             pltpu.VMEM((n_guest, *arrays[0].shape[1:]), jnp.bfloat16),
-            pltpu.VMEM((n_guest, 8, BLOCK), jnp.float32),
+            pltpu.VMEM((n_set, *arrays[0].shape[1:]), jnp.bfloat16),
+            pltpu.VMEM((n_guest, BLOCK, LANES), jnp.float32),
+            pltpu.VMEM((n_guest, BLOCK, LANES), jnp.float32),
             pltpu.SMEM((2, n_guest * n_set + UNROLL), jnp.int32),
             pltpu.SMEM((n_guest,), jnp.int32),
-            pltpu.SemaphoreType.DMA((len(arrays),)),
+            pltpu.SemaphoreType.DMA((len(arrays) + len(sets),)),
         ],
-        input_output_aliases={1 + len(arrays) + 2 + j: j for j in range(3)},
-        compiler_params=pltpu.CompilerParams(vmem_limit_bytes=63 << 20),
+        compiler_params=pltpu.CompilerParams(vmem_limit_bytes=VMEM_MIB << 20),
         cost_estimate=pl.CostEstimate(
             flops=tiles * 4 * BLOCK * BLOCK * 768, bytes_accessed=tiles * 400000, transcendentals=tiles * BLOCK * BLOCK
         ),
         name="pairs",
-    )(table, *arrays, blocks, scale, rows, cols, norms, turn)
+    )(table, *arrays, *sets, *([] if first else running))
 
 
 def body(home_rows, guest_rows, home_cluster, guest_cluster, pair_mask):
@@ -191,12 +233,6 @@
         lax.dynamic_slice_in_dim(home_cluster, device_of(1 - y, 1 - k) * slots, slots),
         jnp.stack([z, x]),
     ])
-
-    def scaled(blocks):
-        return jnp.broadcast_to((inverse_norms(blocks) * EXP2_SCALE)[..., None], (*blocks.shape[:2], LANES))
-
-    def zeros(n):
-        return jnp.zeros((n, BLOCK, LANES), jnp.float32)
 
     stacks = {((0, 0),): guest_rows[None]}
 
@@ -221,9 +257,7 @@
     far = to_partner(home_rows).reshape(slots, BLOCK, -1)
     near = to_sibling(home_rows).reshape(slots, BLOCK, -1)
     newest = [((0, 0),), *send(SLOTS[0][:3], []), *send(SLOTS[0][3:], [near])]
-    blocks, scale, rows = near, scaled(near), zeros(slots)
-    cols = norms = jnp.zeros((NZ * NX, BLOCK), jnp.float32)
-    turn = jnp.zeros((8, LANES), jnp.float32)
+    sets, running = [near], None
     backlog, done = [], []
     for s in range(1, len(SLOTS) + 1):
         came = tuple(stacks[p] for p in newest)
@@ -233,22 +267,17 @@
         olds = []
         if s == FAR_FROM:
             far, _ = lax.optimization_barrier((far, came))
-            blocks = jnp.concatenate([near, far])
-            scale = jnp.concatenate([scale, scaled(far)])
-            rows = jnp.concatenate([rows, zeros(slots)])
+            sets = [near, far]
             olds = backlog
-        rows, cols, norms, turn = pairs(
-            table, flat(newest), flat(olds), [stacks[p] for p in [*newest, *olds]], slots, blocks, scale, rows, cols, norms,
-            turn,
-        )
+        running = pairs(table, flat(newest), flat(olds), [stacks[p] for p in [*newest, *olds]], sets, running)
         backlog = backlog + newest
-        done = [turn]
+        done = [running[4]]
         newest = coming
-    near_rows, far_rows = rows[:slots], rows[slots:]
+    rows, cols = jnp.sum(running[0], axis=1), running[1]
 
     incoming = lax.all_to_all(cols, ("z", "x"), 0, 0, tiled=True)
     guest_density = jnp.sum(incoming, axis=0)
-    home_density = to_sibling(jnp.sum(near_rows, axis=-1)) + to_partner(jnp.sum(far_rows, axis=-1))
+    home_density = to_sibling(rows[:slots]) + to_partner(rows[slots:])
 
     home_ids = lax.dynamic_slice_in_dim(home_cluster, device_of(y, k) * slots, slots)
     guest_id = lax.dynamic_slice_in_dim(guest_cluster, device_of(y, k), 1)

time: 175 us -> 171 us (0.977); the launches traced: 175 us -> 168 us
  other arithmetic: 17.1 us -> 7.83 us
  Pallas kernels: 61.8 us -> 68.9 us
  local copies, waits for them, and re-layouts: 15.7 us -> 9.03 us
  waiting for transfers between devices: 17.2 us -> 23 us
  starting transfers between devices: 60.4 us -> 57.5 us
    ppermute x2, starting transfers between devices: 3.33 us -> 16.9 us  [to_sibling(): return lax.ppermute(value, 'k', [(0, 1), (1, 0)])]
    ppermute x2, starting transfers between devices: 10.1 us -> 2.83 us  [to_partner(): return lax.ppermute(value, ('y', 'k'), [(0, 3), (1, 2), (2, 1), (3, 0)])]
    pallas_call x6, Pallas kernels: 61.8 us -> 68.9 us  [pairs(): pl.pallas_call(functools.partial(pair_kernel, news, olds, [a.shape[0] for...]
    ppermute x12, waiting for transfers between devices: 3.2 us -> 9.04 us  [shift(): return lax.ppermute(value, 'x', [(i, (i + dx) % NX) for i in range(NX)])]
    concatenate x2 -> x0, other arithmetic: 5.59 us -> none  [the longest x1 4.28 us: body(): blocks = jnp.concatenate([near, far])]
    all_to_all x1, starting transfers between devices: 10.6 us -> 5.78 us  [body(): incoming = lax.all_to_all(cols, ('z', 'x'), 0, 0, tiled=True)]
    ppermute x12, starting transfers between devices: 21.4 us -> 17 us  [shift(): return lax.ppermute(value, 'z', [(i, (i + dz) % NZ) for i in range(NZ)])]
    reduce_sum x3 -> x1, other arithmetic: 4.57 us -> 0.92 us  [body(): rows, cols = (jnp.sum(running[0], axis=1), running[1])]
  transfers between devices with their start and end apart: 29 -> 29, of which waited for: 7 -> 8; matrix products, arithmetic and copies ran while one was open for 14% -> 9% of each run, Pallas kernels for 30% -> 36%
where the time goes in v1:
time: 171 us; the launch traced here: 168 us
  Pallas kernels  68.9 us (40%)
  starting transfers between devices  57.5 us (34%)
  waiting for transfers between devices  23 us (13%)
  local copies, waits for them, and re-layouts  9.03 us (5%)
  other arithmetic  7.83 us (5%)
  between operations  2.22 us (1%)
    pallas_call x6, Pallas kernels, pairs(): pl.pallas_call(functools.partial(pair_kernel, news, olds, [a.shape[0] for...  68.9 us
    ppermute x12, starting transfers between devices, shift(): return lax.ppermute(value, 'z', [(i, (i + dz) % NZ) for i in range(NZ)])  17 us
    ppermute x2, starting transfers between devices, to_sibling(): return lax.ppermute(value, 'k', [(0, 1), (1, 0)])  16.9 us
    ppermute x12, starting transfers between devices, shift(): return lax.ppermute(value, 'x', [(i, (i + dx) % NX) for i in range(NX)])  15 us
    ppermute x12, waiting for transfers between devices, shift(): return lax.ppermute(value, 'x', [(i, (i + dx) % NX) for i in range(NX)])  9.04 us
    all_to_all x1, waiting for transfers between devices, body(): incoming = lax.all_to_all(cols, ('z', 'x'), 0, 0, tiled=True)  8 us
    ppermute x12, waiting for transfers between devices, shift(): return lax.ppermute(value, 'z', [(i, (i + dz) % NZ) for i in range(NZ)])  5.93 us
    all_to_all x1, starting transfers between devices, body(): incoming = lax.all_to_all(cols, ('z', 'x'), 0, 0, tiled=True)  5.78 us
  transfers between devices with their start and end apart: 29, of which 8 were waited for; matrix products, arithmetic and copies ran while one was open for 9% of the time, Pallas kernels for 36%

profile of v1, /device:TPU:1, one launch (start us, length us, event | category | flops | bytes accessed | tf_op | source)
XLA Modules:
  0.0 168.5 jit_solution(15260912353747517259)
XLA Ops:
  0.6 3.3 %collective-permute-start = (bf16[1536,768]{1,0:T(8,128)(2,1)}, bf16[1536,768]{1,0:T(8,128)(2,1)S(1)}, u32[]{:S(2)}, u32[]{:S(2)}) collective-permute-start(bf16[1536,768]{1,0:T(8,128)(2,1)} %param.5), channel_id=1, source_target_pairs={{0,1},{1,0},{2,3},{3,2},{4,5},{5,4},{6,7},{7,6},{8,9},{9,8},{10,11... | collective-permute-start | bytes 7077896 | tf_op jit(solution)/shard_map/ppermute | solution.py:52
  4.0 0.0 collective-permute-start.21
  4.0 0.8 collective-permute-start.3
  4.7 5.6 %collective-permute-start.2 = (bf16[1,256,768]{2,1,0:T(8,128)(2,1)}, bf16[1,256,768]{2,1,0:T(8,128)(2,1)}, u32[]{:S(2)}, u32[]{:S(2)}) collective-permute-start(bf16[1,256,768]{2,1,0:T(8,128)(2,1)} %bitcast.15), channel_id=1, source_target_pairs={{0,112},{16,0},{32,16},{48,32},{64,48},{80,64},{96,80},{112,96},{1... | collective-permute-start | bytes 1179656 | tf_op jit(solution)/shard_map/ppermute | solution.py:41
  10.3 1.5 collective-permute-start.4
  11.8 4.1 %collective-permute-done.3.refs_1_.refs_5_ = bf16[1,256,768]{2,1,0:T(8,128)(2,1)S(1)} collective-permute-done((bf16[1,256,768]{2,1,0:T(8,128)(2,1)}, bf16[1,256,768]{2,1,0:T(8,128)(2,1)S(1)}, u32[]{:S(2)}, u32[]{:S(2)}) %collective-permute-start.3) | collective-permute-done | bytes 393248 | tf_op jit(solution)/shard_map/ppermute | solution.py:43
  15.9 2.4 %collective-permute-done.2.refs_2_.refs_6_ = bf16[1,256,768]{2,1,0:T(8,128)(2,1)} collective-permute-done((bf16[1,256,768]{2,1,0:T(8,128)(2,1)}, bf16[1,256,768]{2,1,0:T(8,128)(2,1)}, u32[]{:S(2)}, u32[]{:S(2)}) %collective-permute-start.2) | collective-permute-done | bytes 393248 | tf_op jit(solution)/shard_map/ppermute | solution.py:41
  18.4 1.9 %collective-permute-done.4.refs_3_.refs_7_ = bf16[1,256,768]{2,1,0:T(8,128)(2,1)S(1)} collective-permute-done((bf16[1,256,768]{2,1,0:T(8,128)(2,1)}, bf16[1,256,768]{2,1,0:T(8,128)(2,1)S(1)}, u32[]{:S(2)}, u32[]{:S(2)}) %collective-permute-start.4) | collective-permute-done | bytes 393248 | tf_op jit(solution)/shard_map/ppermute | solution.py:43
  20.2 2.4 %collective-permute-done.1.refs_4_.refs_8_ = bf16[1,256,768]{2,1,0:T(8,128)(2,1)} collective-permute-done((bf16[1,256,768]{2,1,0:T(8,128)(2,1)}, bf16[1,256,768]{2,1,0:T(8,128)(2,1)}, u32[]{:S(2)}, u32[]{:S(2)}) %collective-permute-start.1) | collective-permute-done | bytes 393248 | tf_op jit(solution)/shard_map/ppermute | solution.py:41
  22.6 0.0 collective-permute-start.5
  22.6 1.4 collective-permute-start.7
  24.0 0.1 collective-permute-start.6
  24.1 2.7 %collective-permute-start.8 = (bf16[1,256,768]{2,1,0:T(8,128)(2,1)}, bf16[1,256,768]{2,1,0:T(8,128)(2,1)}, u32[]{:S(2)}, u32[]{:S(2)}) collective-permute-start(bf16[1,256,768]{2,1,0:T(8,128)(2,1)} %collective-permute-done.2.refs_2_.refs_6_), channel_id=1, source_target_pairs={{0,12},{4,0},{8,4},{12,8},{1,13},{5,1},{9,5},{13,9},{2,14},{6,2},{... | collective-permute-start | bytes 1179656 | tf_op jit(solution)/shard_map/ppermute | solution.py:43
  26.8 0.8 reshape.45
  27.6 0.2 dynamic-slice_reduce_fusion
  27.7 0.9 fusion.2
  28.6 0.7 concatenate.3.table
  29.3 8.9 %pairs.6 = (f32[12,8,256]{2,1,0:T(8,128)}, f32[32,256]{1,0:T(8,128)}, f32[32,256]{1,0:T(8,128)}, f32[16,256]{1,0:T(8,128)}, f32[8,128]{1,0:T(8,128)}) custom-call(s32[46]{0:T(128)} %concatenate.3.table, bf16[1,256,768]{2,1,0:T(8,128)(2,1)} %bitcast.18, bf16[1,256,768]{2,1,0:T(8,128)(2,1)} %copy-done, ...), custom_call_target="tpu_custom_call" | custom-call | flops 2013265920 | bytes 4000000 | tf_op jit(solution)/shard_map/pairs/pallas_call | solution.py:201
  38.1 0.0 collective-permute-done.5.refs_2_.refs_11_
  38.1 0.0 collective-permute-done.7.refs_1_.refs_10_
  38.2 2.0 %collective-permute-start.10 = (bf16[1,256,768]{2,1,0:T(8,128)(2,1)}, bf16[1,256,768]{2,1,0:T(8,128)(2,1)}, u32[]{:S(2)}, u32[]{:S(2)}) collective-permute-start(bf16[1,256,768]{2,1,0:T(8,128)(2,1)} %collective-permute-done.7.refs_1_.refs_10_), channel_id=1, source_target_pairs={{0,112},{16,0},{32,16},{48,32},{64,48},{80,64},{96,80},{112,96},{1... | collective-permute-start | bytes 1179656 | tf_op jit(solution)/shard_map/ppermute | solution.py:41
  40.1 0.0 collective-permute-start.9
  40.1 0.2 collective-permute-start.11
  40.3 2.5 %collective-permute-start.12 = (bf16[1,256,768]{2,1,0:T(8,128)(2,1)}, bf16[1,256,768]{2,1,0:T(8,128)(2,1)}, u32[]{:S(2)}, u32[]{:S(2)}) collective-permute-start(bf16[1,256,768]{2,1,0:T(8,128)(2,1)} %collective-permute-done.1.refs_4_.refs_8_), channel_id=1, source_target_pairs={{0,12},{4,0},{8,4},{12,8},{1,13},{5,1},{9,5},{13,9},{2,14},{6,2},{... | collective-permute-start | bytes 1179656 | tf_op jit(solution)/shard_map/ppermute | solution.py:43
  42.8 1.2 pad_maximum_fusion
  44.0 0.0 copy-start.3
  44.0 0.0 copy-start.2
  44.0 7.1 %pairs.7 = (f32[12,8,256]{2,1,0:T(8,128)}, f32[32,256]{1,0:T(8,128)}, f32[32,256]{1,0:T(8,128)}, f32[16,256]{1,0:T(8,128)}, f32[8,128]{1,0:T(8,128)}) custom-call(s32[46]{0:T(128)} %concatenate.3.table, bf16[1,256,768]{2,1,0:T(8,128)(2,1)} %collective-permute-done.6.refs_0_.refs_9_, bf16[1,256,768]{2,1,0:T(8,128)(2,1)} %collective-permute-done.7.refs_1_.refs_10_, ...), custom_call_target="tpu_custom_call" | custom-call | flops 1610612736 | bytes 3200000 | tf_op jit(solution)/shard_map/pairs/pallas_call | solution.py:201
  51.2 2.1 %pad_maximum_fusion.1 = bf16[2,256,768]{2,1,0:T(8,128)(2,1)} fusion(bf16[1,256,768]{2,1,0:T(8,128)(2,1)} %collective-permute-done.10.refs_2_.refs_15_, bf16[1,256,768]{2,1,0:T(8,128)(2,1)} %collective-permute-done.9.refs_3_.refs_16_), kind=kLoop, calls=%fused_computation.1 | loop fusion | flops 393216 | bytes 1572864 | tf_op jit(solution)/shard_map/stack | solution.py:246
  53.2 0.9 collective-permute-start.13
  54.2 0.6 collective-permute-start.14
  54.7 2.7 %collective-permute-start.15 = (bf16[2,256,768]{2,1,0:T(8,128)(2,1)S(1)}, bf16[2,256,768]{2,1,0:T(8,128)(2,1)}, u32[]{:S(2)}, u32[]{:S(2)}) collective-permute-start(bf16[2,256,768]{2,1,0:T(8,128)(2,1)S(1)} %pad_maximum_fusion), channel_id=1, source_target_pairs={{0,112},{16,0},{32,16},{48,32},{64,48},{80,64},{96,80},{112,96},{1... | collective-permute-start | bytes 2359304 | tf_op jit(solution)/shard_map/ppermute | solution.py:41
  57.4 0.6 dynamic_slice.19
  58.0 0.1 dynamic_slice.18
  58.1 1.3 convert_reduce_fusion.1
  59.3 0.2 convert_reduce_fusion.2
  59.5 0.2 convert_reduce_fusion
  59.7 6.9 %pairs.8 = (f32[12,8,256]{2,1,0:T(8,128)}, f32[32,256]{1,0:T(8,128)}, f32[32,256]{1,0:T(8,128)}, f32[16,256]{1,0:T(8,128)}, f32[8,128]{1,0:T(8,128)}) custom-call(s32[46]{0:T(128)} %concatenate.3.table, bf16[1,256,768]{2,1,0:T(8,128)(2,1)} %collective-permute-done.11.refs_0_.refs_13_, bf16[1,256,768]{2,1,0:T(8,128)(2,1)} %collective-permute-done.12.refs_1_.refs_14_, ...), custom_call_target="tpu_custom_call" | custom-call | flops 1610612736 | bytes 3200000 | tf_op jit(solution)/shard_map/pairs/pallas_call | solution.py:201
  66.7 0.1 collective-permute-done.13.refs_3_
  66.7 2.9 %collective-permute-done.14.refs_2_ = bf16[2,256,768]{2,1,0:T(8,128)(2,1)} collective-permute-done((bf16[2,256,768]{2,1,0:T(8,128)(2,1)}, bf16[2,256,768]{2,1,0:T(8,128)(2,1)}, u32[]{:S(2)}, u32[]{:S(2)}) %collective-permute-start.14) | collective-permute-done | bytes 786464 | tf_op jit(solution)/shard_map/ppermute | solution.py:43
  69.7 1.1 collective-permute-done.16.refs_1_
  70.7 2.7 %collective-permute-start.18 = (bf16[2,256,768]{2,1,0:T(8,128)(2,1)}, bf16[2,256,768]{2,1,0:T(8,128)(2,1)}, u32[]{:S(2)}, u32[]{:S(2)}) collective-permute-start(bf16[2,256,768]{2,1,0:T(8,128)(2,1)} %collective-permute-done.13.refs_3_), channel_id=1, source_target_pairs={{0,112},{16,0},{32,16},{48,32},{64,48},{80,64},{96,80},{112,96},{1... | collective-permute-start | bytes 2359304 | tf_op jit(solution)/shard_map/ppermute | solution.py:41
  73.4 0.3 collective-permute-start.19
  73.7 2.9 %collective-permute-start.20 = (bf16[1,256,768]{2,1,0:T(8,128)(2,1)}, bf16[1,256,768]{2,1,0:T(8,128)(2,1)}, u32[]{:S(2)}, u32[]{:S(2)}) collective-permute-start(bf16[1,256,768]{2,1,0:T(8,128)(2,1)} %collective-permute-done.7.refs_1_.refs_10_), channel_id=1, source_target_pairs={{0,12},{4,0},{8,4},{12,8},{1,13},{5,1},{9,5},{13,9},{2,14},{6,2},{... | collective-permute-start | bytes 1179656 | tf_op jit(solution)/shard_map/ppermute | solution.py:43
  76.6 26.5 %pairs.9 = (f32[12,8,256]{2,1,0:T(8,128)}, f32[32,256]{1,0:T(8,128)}, f32[32,256]{1,0:T(8,128)}, f32[16,256]{1,0:T(8,128)}, f32[8,128]{1,0:T(8,128)}) custom-call(s32[46]{0:T(128)} %concatenate.3.table, bf16[2,256,768]{2,1,0:T(8,128)(2,1)} %collective-permute-done.15.refs_0_, bf16[2,256,768]{2,1,0:T(8,128)(2,1)} %collective-permute-done.16.refs_1_, ...), custom_call_target="tpu_custom_call" | custom-call | flops 11676942336 | bytes 23200000 | tf_op jit(solution)/shard_map/pairs/pallas_call | solution.py:201
  103.2 1.0 slice.20
  104.2 1.8 %slice.21 = bf16[1,256,768]{2,1,0:T(8,128)(2,1)} slice(bf16[2,256,768]{2,1,0:T(8,128)(2,1)} %collective-permute-done.18.refs_0_), slice={[0:1], [0:256], [0:768]} | slice | bytes 786432 | tf_op jit(solution)/shard_map/slice | solution.py:242
  106.0 1.0 slice.22
  107.1 1.2 collective-permute-start.22
  108.2 1.6 collective-permute-start.23
  109.8 2.7 %collective-permute-start.25 = (bf16[1,256,768]{2,1,0:T(8,128)(2,1)S(1)}, bf16[1,256,768]{2,1,0:T(8,128)(2,1)}, u32[]{:S(2)}, u32[]{:S(2)}) collective-permute-start(bf16[1,256,768]{2,1,0:T(8,128)(2,1)S(1)} %slice.22), channel_id=1, source_target_pairs={{0,112},{16,0},{32,16},{48,32},{64,48},{80,64},{96,80},{112,96},{1... | collective-permute-start | bytes 1179656 | tf_op jit(solution)/shard_map/ppermute | solution.py:41
  112.5 11.9 %pairs.10 = (f32[12,8,256]{2,1,0:T(8,128)}, f32[32,256]{1,0:T(8,128)}, f32[32,256]{1,0:T(8,128)}, f32[16,256]{1,0:T(8,128)}, f32[8,128]{1,0:T(8,128)}) custom-call(s32[46]{0:T(128)} %concatenate.3.table, bf16[2,256,768]{2,1,0:T(8,128)(2,1)} %collective-permute-done.18.refs_0_, bf16[2,256,768]{2,1,0:T(8,128)(2,1)} %collective-permute-done.19.refs_1_, ...), custom_call_target="tpu_custom_call" | custom-call | flops 5637144576 | bytes 11200000 | tf_op jit(solution)/shard_map/pairs/pallas_call | solution.py:201
  124.5 7.6 %pairs.11 = (f32[12,8,256]{2,1,0:T(8,128)}, f32[32,256]{1,0:T(8,128)}, f32[32,256]{1,0:T(8,128)}, f32[16,256]{1,0:T(8,128)}, f32[8,128]{1,0:T(8,128)}) custom-call(s32[46]{0:T(128)} %concatenate.3.table, bf16[1,256,768]{2,1,0:T(8,128)(2,1)} %collective-permute-done.22.refs_0_, bf16[1,256,768]{2,1,0:T(8,128)(2,1)} %collective-permute-done.23.refs_1_, ...), custom_call_target="tpu_custom_call" | custom-call | flops 3221225472 | bytes 6400000 | tf_op jit(solution)/shard_map/pairs/pallas_call | solution.py:201
  132.1 0.9 reduce_sum.54
  133.0 13.5 %collective-permute-start.26 = (f32[6,256]{1,0:T(8,128)S(1)}, f32[6,256]{1,0:T(8,128)S(1)}, u32[]{:S(2)}, u32[]{:S(2)}) collective-permute-start(f32[6,256]{1,0:T(8,128)S(1)} %get-tuple-element.111), channel_id=1, source_target_pairs={{0,1},{1,0},{2,3},{3,2},{4,5},{5,4},{6,7},{7,6},{8,9},{9,8},{10,11... | collective-permute-start | bytes 18440 | tf_op jit(solution)/shard_map/ppermute | solution.py:52
  146.6 2.8 %collective-permute-start.27 = (f32[6,256]{1,0:T(8,128)S(1)}, f32[6,256]{1,0:T(8,128)S(1)}, u32[]{:S(2)}, u32[]{:S(2)}) collective-permute-start(f32[6,256]{1,0:T(8,128)S(1)} %get-tuple-element.110), channel_id=1, source_target_pairs={{0,129},{1,128},{128,1},{129,0},{2,131},{3,130},{130,3},{131,2},{4... | collective-permute-start | bytes 18440 | tf_op jit(solution)/shard_map/ppermute | solution.py:56
  149.4 1.3 fusion
  152.0 1.4 copy.7
  153.4 5.8 %all-to-all-start = ((f32[32,1,256]{2,1,0:T(1,128)}), f32[32,1,256]{2,1,0:T(1,128)S(1)}, u32[]{:S(2)}, u32[]{:S(2)}) async-start(f32[32,1,256]{2,1,0:T(1,128)} %copy.7), calls=%async_computation | async-start | bytes 65536 | tf_op jit(solution)/shard_map/all_to_all | solution.py:278
  159.2 0.1 log_subtract_fusion
  159.2 0.6 reshape.49
  159.8 8.0 %all-to-all-done = f32[32,1,256]{2,1,0:T(1,128)S(1)} async-done(((f32[32,1,256]{2,1,0:T(1,128)}), f32[32,1,256]{2,1,0:T(1,128)S(1)}, u32[]{:S(2)}, u32[]{:S(2)}) %all-to-all-start) | async-done | bytes 32800 | tf_op jit(solution)/shard_map/all_to_all | solution.py:278
  167.8 0.1 reduce_sum.57
  167.9 0.6 log_subtract_fusion.1
  (35 shorter events, 0.1 us)
Async XLA Ops:
  0.6 11.1 %collective-permute-start = (bf16[1536,768]{1,0:T(8,128)(2,1)}, bf16[1536,768]{1,0:T(8,128)(2,1)S(1)}, u32[]{:S(2)}, u32[]{:S(2)}) collective-permute-start(bf16[1536,768]{1,0:T(8,128)(2,1)} %param.5), channel_id=1, source_target_pairs={{0,1},{1,0},{2,3},{3,2},{4,5},{5,4},{6,7},{7,6},{8,9},{9,8},{10,11... | collective-permute-start | bytes 7077896 | tf_op jit(solution)/shard_map/ppermute | solution.py:52
  4.0 62.7 %collective-permute-start.21 = (bf16[1536,768]{1,0:T(8,128)(2,1)}, bf16[1536,768]{1,0:T(8,128)(2,1)}, u32[]{:S(2)}, u32[]{:S(2)}) collective-permute-start(bf16[1536,768]{1,0:T(8,128)(2,1)} %param.5), channel_id=1, source_target_pairs={{0,129},{1,128},{128,1},{129,0},{2,131},{3,130},{130,3},{131,2},{4... | collective-permute-start | bytes 7077896 | tf_op jit(solution)/shard_map/ppermute | solution.py:56
  4.0 12.0 %collective-permute-start.3 = (bf16[1,256,768]{2,1,0:T(8,128)(2,1)}, bf16[1,256,768]{2,1,0:T(8,128)(2,1)S(1)}, u32[]{:S(2)}, u32[]{:S(2)}) collective-permute-start(bf16[1,256,768]{2,1,0:T(8,128)(2,1)} %bitcast.14), channel_id=1, source_target_pairs={{0,4},{4,8},{8,12},{12,0},{1,5},{5,9},{9,13},{13,1},{2,6},{6,10},{... | collective-permute-start | bytes 1179656 | tf_op jit(solution)/shard_map/ppermute | solution.py:43
  4.7 13.6 %collective-permute-start.2 = (bf16[1,256,768]{2,1,0:T(8,128)(2,1)}, bf16[1,256,768]{2,1,0:T(8,128)(2,1)}, u32[]{:S(2)}, u32[]{:S(2)}) collective-permute-start(bf16[1,256,768]{2,1,0:T(8,128)(2,1)} %bitcast.15), channel_id=1, source_target_pairs={{0,112},{16,0},{32,16},{48,32},{64,48},{80,64},{96,80},{112,96},{1... | collective-permute-start | bytes 1179656 | tf_op jit(solution)/shard_map/ppermute | solution.py:41
  10.3 9.9 %collective-permute-start.4 = (bf16[1,256,768]{2,1,0:T(8,128)(2,1)}, bf16[1,256,768]{2,1,0:T(8,128)(2,1)S(1)}, u32[]{:S(2)}, u32[]{:S(2)}) collective-permute-start(bf16[1,256,768]{2,1,0:T(8,128)(2,1)} %bitcast.16), channel_id=1, source_target_pairs={{0,12},{4,0},{8,4},{12,8},{1,13},{5,1},{9,5},{13,9},{2,14},{6,2},{... | collective-permute-start | bytes 1179656 | tf_op jit(solution)/shard_map/ppermute | solution.py:43
  11.8 8.5 %copy-start.4 = (bf16[1536,768]{1,0:T(8,128)(2,1)}, bf16[1536,768]{1,0:T(8,128)(2,1)S(1)}, u32[]{:S(2)}) copy-start(bf16[1536,768]{1,0:T(8,128)(2,1)S(1)} %collective-permute-done) | copy-start | bytes 7077892
  11.8 10.9 %collective-permute-start.1 = (bf16[1,256,768]{2,1,0:T(8,128)(2,1)}, bf16[1,256,768]{2,1,0:T(8,128)(2,1)}, u32[]{:S(2)}, u32[]{:S(2)}) collective-permute-start(bf16[1,256,768]{2,1,0:T(8,128)(2,1)} %bitcast.17), channel_id=1, source_target_pairs={{0,16},{16,32},{32,48},{48,64},{64,80},{80,96},{96,112},{112,0},{1... | collective-permute-start | bytes 1179656 | tf_op jit(solution)/shard_map/ppermute | solution.py:41
  15.9 13.3 %copy-start = (bf16[1,256,768]{2,1,0:T(8,128)(2,1)}, bf16[1,256,768]{2,1,0:T(8,128)(2,1)S(1)}, u32[]{:S(2)}) copy-start(bf16[1,256,768]{2,1,0:T(8,128)(2,1)S(1)} %collective-permute-done.3.refs_1_.refs_5_) | copy-start | bytes 1179652
  20.2 2.4 %copy-start.5 = (bf16[1,256,768]{2,1,0:T(8,128)(2,1)}, bf16[1,256,768]{2,1,0:T(8,128)(2,1)S(1)}, u32[]{:S(2)}) copy-start(bf16[1,256,768]{2,1,0:T(8,128)(2,1)S(1)} %collective-permute-done.4.refs_3_.refs_7_) | copy-start | bytes 1179652
  22.6 15.5 %collective-permute-start.5 = (bf16[1,256,768]{2,1,0:T(8,128)(2,1)S(1)}, bf16[1,256,768]{2,1,0:T(8,128)(2,1)S(1)}, u32[]{:S(2)}, u32[]{:S(2)}) collective-permute-start(bf16[1,256,768]{2,1,0:T(8,128)(2,1)S(1)} %collective-permute-done.3.refs_1_.refs_5_), channel_id=1, source_target_pairs={{0,4},{4,8},{8,12},{12,0},{1,5},{5,9},{9,13},{13,1},{2,6},{6,10},{... | collective-permute-start | bytes 1179656 | tf_op jit(solution)/shard_map/ppermute | solution.py:43
  22.6 15.5 %collective-permute-start.7 = (bf16[1,256,768]{2,1,0:T(8,128)(2,1)}, bf16[1,256,768]{2,1,0:T(8,128)(2,1)}, u32[]{:S(2)}, u32[]{:S(2)}) collective-permute-start(bf16[1,256,768]{2,1,0:T(8,128)(2,1)} %collective-permute-done.2.refs_2_.refs_6_), channel_id=1, source_target_pairs={{0,112},{16,0},{32,16},{48,32},{64,48},{80,64},{96,80},{112,96},{1... | collective-permute-start | bytes 1179656 | tf_op jit(solution)/shard_map/ppermute | solution.py:41
  24.0 14.1 %collective-permute-start.6 = (bf16[1,256,768]{2,1,0:T(8,128)(2,1)}, bf16[1,256,768]{2,1,0:T(8,128)(2,1)}, u32[]{:S(2)}, u32[]{:S(2)}) collective-permute-start(bf16[1,256,768]{2,1,0:T(8,128)(2,1)} %collective-permute-done.1.refs_4_.refs_8_), channel_id=1, source_target_pairs={{0,16},{16,32},{32,48},{48,64},{64,80},{80,96},{96,112},{112,0},{1... | collective-permute-start | bytes 1179656 | tf_op jit(solution)/shard_map/ppermute | solution.py:41
  24.1 14.1 %collective-permute-start.8 = (bf16[1,256,768]{2,1,0:T(8,128)(2,1)}, bf16[1,256,768]{2,1,0:T(8,128)(2,1)}, u32[]{:S(2)}, u32[]{:S(2)}) collective-permute-start(bf16[1,256,768]{2,1,0:T(8,128)(2,1)} %collective-permute-done.2.refs_2_.refs_6_), channel_id=1, source_target_pairs={{0,12},{4,0},{8,4},{12,8},{1,13},{5,1},{9,5},{13,9},{2,14},{6,2},{... | collective-permute-start | bytes 1179656 | tf_op jit(solution)/shard_map/ppermute | solution.py:43
  38.1 2.2 %copy-start.1 = (bf16[1,256,768]{2,1,0:T(8,128)(2,1)}, bf16[1,256,768]{2,1,0:T(8,128)(2,1)S(1)}, u32[]{:S(2)}) copy-start(bf16[1,256,768]{2,1,0:T(8,128)(2,1)S(1)} %collective-permute-done.5.refs_2_.refs_11_) | copy-start | bytes 1179652
  38.2 13.0 %collective-permute-start.10 = (bf16[1,256,768]{2,1,0:T(8,128)(2,1)}, bf16[1,256,768]{2,1,0:T(8,128)(2,1)}, u32[]{:S(2)}, u32[]{:S(2)}) collective-permute-start(bf16[1,256,768]{2,1,0:T(8,128)(2,1)} %collective-permute-done.7.refs_1_.refs_10_), channel_id=1, source_target_pairs={{0,112},{16,0},{32,16},{48,32},{64,48},{80,64},{96,80},{112,96},{1... | collective-permute-start | bytes 1179656 | tf_op jit(solution)/shard_map/ppermute | solution.py:41
  40.1 11.0 %collective-permute-start.9 = (bf16[1,256,768]{2,1,0:T(8,128)(2,1)}, bf16[1,256,768]{2,1,0:T(8,128)(2,1)}, u32[]{:S(2)}, u32[]{:S(2)}) collective-permute-start(bf16[1,256,768]{2,1,0:T(8,128)(2,1)} %collective-permute-done.6.refs_0_.refs_9_), channel_id=1, source_target_pairs={{0,16},{16,32},{32,48},{48,64},{64,80},{80,96},{96,112},{112,0},{1... | collective-permute-start | bytes 1179656 | tf_op jit(solution)/shard_map/ppermute | solution.py:41
  40.1 13.1 %collective-permute-start.11 = (bf16[1,256,768]{2,1,0:T(8,128)(2,1)}, bf16[1,256,768]{2,1,0:T(8,128)(2,1)}, u32[]{:S(2)}, u32[]{:S(2)}) collective-permute-start(bf16[1,256,768]{2,1,0:T(8,128)(2,1)} %collective-permute-done.6.refs_0_.refs_9_), channel_id=1, source_target_pairs={{0,4},{4,8},{8,12},{12,0},{1,5},{5,9},{9,13},{13,1},{2,6},{6,10},{... | collective-permute-start | bytes 1179656 | tf_op jit(solution)/shard_map/ppermute | solution.py:43
  40.3 12.9 %collective-permute-start.12 = (bf16[1,256,768]{2,1,0:T(8,128)(2,1)}, bf16[1,256,768]{2,1,0:T(8,128)(2,1)}, u32[]{:S(2)}, u32[]{:S(2)}) collective-permute-start(bf16[1,256,768]{2,1,0:T(8,128)(2,1)} %collective-permute-done.1.refs_4_.refs_8_), channel_id=1, source_target_pairs={{0,12},{4,0},{8,4},{12,8},{1,13},{5,1},{9,5},{13,9},{2,14},{6,2},{... | collective-permute-start | bytes 1179656 | tf_op jit(solution)/shard_map/ppermute | solution.py:43
  44.0 13.4 %copy-start.3 = (s32[256]{0:T(256)S(1)}, s32[256]{0:T(256)}, u32[]{:S(2)}) copy-start(s32[256]{0:T(256)} %param.8) | copy-start | bytes 3076
  44.0 14.0 %copy-start.2 = (s32[1536]{0:T(1024)S(1)}, s32[1536]{0:T(1024)}, u32[]{:S(2)}) copy-start(s32[1536]{0:T(1024)} %param.7) | copy-start | bytes 18436
  53.2 13.5 %collective-permute-start.13 = (bf16[2,256,768]{2,1,0:T(8,128)(2,1)}, bf16[2,256,768]{2,1,0:T(8,128)(2,1)}, u32[]{:S(2)}, u32[]{:S(2)}) collective-permute-start(bf16[2,256,768]{2,1,0:T(8,128)(2,1)} %pad_maximum_fusion.1), channel_id=1, source_target_pairs={{0,12},{4,0},{8,4},{12,8},{1,13},{5,1},{9,5},{13,9},{2,14},{6,2},{... | collective-permute-start | bytes 2359304 | tf_op jit(solution)/shard_map/ppermute | solution.py:43
  54.2 15.5 %collective-permute-start.14 = (bf16[2,256,768]{2,1,0:T(8,128)(2,1)}, bf16[2,256,768]{2,1,0:T(8,128)(2,1)}, u32[]{:S(2)}, u32[]{:S(2)}) collective-permute-start(bf16[2,256,768]{2,1,0:T(8,128)(2,1)} %pad_maximum_fusion.1), channel_id=1, source_target_pairs={{0,4},{4,8},{8,12},{12,0},{1,5},{5,9},{9,13},{13,1},{2,6},{6,10},{... | collective-permute-start | bytes 2359304 | tf_op jit(solution)/shard_map/ppermute | solution.py:43
  54.7 15.0 %collective-permute-start.15 = (bf16[2,256,768]{2,1,0:T(8,128)(2,1)S(1)}, bf16[2,256,768]{2,1,0:T(8,128)(2,1)}, u32[]{:S(2)}, u32[]{:S(2)}) collective-permute-start(bf16[2,256,768]{2,1,0:T(8,128)(2,1)S(1)} %pad_maximum_fusion), channel_id=1, source_target_pairs={{0,112},{16,0},{32,16},{48,32},{64,48},{80,64},{96,80},{112,96},{1... | collective-permute-start | bytes 2359304 | tf_op jit(solution)/shard_map/ppermute | solution.py:41
  57.4 13.4 %collective-permute-start.16 = (bf16[2,256,768]{2,1,0:T(8,128)(2,1)S(1)}, bf16[2,256,768]{2,1,0:T(8,128)(2,1)}, u32[]{:S(2)}, u32[]{:S(2)}) collective-permute-start(bf16[2,256,768]{2,1,0:T(8,128)(2,1)S(1)} %pad_maximum_fusion), channel_id=1, source_target_pairs={{0,16},{16,32},{32,48},{48,64},{64,80},{80,96},{96,112},{112,0},{1... | collective-permute-start | bytes 2359304 | tf_op jit(solution)/shard_map/ppermute | solution.py:41
  70.7 32.4 %collective-permute-start.17 = (bf16[2,256,768]{2,1,0:T(8,128)(2,1)}, bf16[2,256,768]{2,1,0:T(8,128)(2,1)}, u32[]{:S(2)}, u32[]{:S(2)}) collective-permute-start(bf16[2,256,768]{2,1,0:T(8,128)(2,1)} %collective-permute-done.14.refs_2_), channel_id=1, source_target_pairs={{0,16},{16,32},{32,48},{48,64},{64,80},{80,96},{96,112},{112,0},{1... | collective-permute-start | bytes 2359304 | tf_op jit(solution)/shard_map/ppermute | solution.py:41
  70.7 33.4 %collective-permute-start.18 = (bf16[2,256,768]{2,1,0:T(8,128)(2,1)}, bf16[2,256,768]{2,1,0:T(8,128)(2,1)}, u32[]{:S(2)}, u32[]{:S(2)}) collective-permute-start(bf16[2,256,768]{2,1,0:T(8,128)(2,1)} %collective-permute-done.13.refs_3_), channel_id=1, source_target_pairs={{0,112},{16,0},{32,16},{48,32},{64,48},{80,64},{96,80},{112,96},{1... | collective-permute-start | bytes 2359304 | tf_op jit(solution)/shard_map/ppermute | solution.py:41
  73.4 32.6 %collective-permute-start.19 = (bf16[2,256,768]{2,1,0:T(8,128)(2,1)}, bf16[2,256,768]{2,1,0:T(8,128)(2,1)}, u32[]{:S(2)}, u32[]{:S(2)}) collective-permute-start(bf16[2,256,768]{2,1,0:T(8,128)(2,1)} %collective-permute-done.14.refs_2_), channel_id=1, source_target_pairs={{0,4},{4,8},{8,12},{12,0},{1,5},{5,9},{9,13},{13,1},{2,6},{6,10},{... | collective-permute-start | bytes 2359304 | tf_op jit(solution)/shard_map/ppermute | solution.py:43
  73.7 33.3 %collective-permute-start.20 = (bf16[1,256,768]{2,1,0:T(8,128)(2,1)}, bf16[1,256,768]{2,1,0:T(8,128)(2,1)}, u32[]{:S(2)}, u32[]{:S(2)}) collective-permute-start(bf16[1,256,768]{2,1,0:T(8,128)(2,1)} %collective-permute-done.7.refs_1_.refs_10_), channel_id=1, source_target_pairs={{0,12},{4,0},{8,4},{12,8},{1,13},{5,1},{9,5},{13,9},{2,14},{6,2},{... | collective-permute-start | bytes 1179656 | tf_op jit(solution)/shard_map/ppermute | solution.py:43
  107.1 17.4 %collective-permute-start.22 = (bf16[1,256,768]{2,1,0:T(8,128)(2,1)S(1)}, bf16[1,256,768]{2,1,0:T(8,128)(2,1)}, u32[]{:S(2)}, u32[]{:S(2)}) collective-permute-start(bf16[1,256,768]{2,1,0:T(8,128)(2,1)S(1)} %slice.20), channel_id=1, source_target_pairs={{0,4},{4,8},{8,12},{12,0},{1,5},{5,9},{9,13},{13,1},{2,6},{6,10},{... | collective-permute-start | bytes 1179656 | tf_op jit(solution)/shard_map/ppermute | solution.py:43
  108.2 16.2 %collective-permute-start.23 = (bf16[1,256,768]{2,1,0:T(8,128)(2,1)}, bf16[1,256,768]{2,1,0:T(8,128)(2,1)}, u32[]{:S(2)}, u32[]{:S(2)}) collective-permute-start(bf16[1,256,768]{2,1,0:T(8,128)(2,1)} %slice.21), channel_id=1, source_target_pairs={{0,12},{4,0},{8,4},{12,8},{1,13},{5,1},{9,5},{13,9},{2,14},{6,2},{... | collective-permute-start | bytes 1179656 | tf_op jit(solution)/shard_map/ppermute | solution.py:43
  109.8 14.6 %collective-permute-start.24 = (bf16[1,256,768]{2,1,0:T(8,128)(2,1)}, bf16[1,256,768]{2,1,0:T(8,128)(2,1)}, u32[]{:S(2)}, u32[]{:S(2)}) collective-permute-start(bf16[1,256,768]{2,1,0:T(8,128)(2,1)} %collective-permute-done.9.refs_3_.refs_16_), channel_id=1, source_target_pairs={{0,16},{16,32},{32,48},{48,64},{64,80},{80,96},{96,112},{112,0},{1... | collective-permute-start | bytes 1179656 | tf_op jit(solution)/shard_map/ppermute | solution.py:41
  109.8 14.6 %collective-permute-start.25 = (bf16[1,256,768]{2,1,0:T(8,128)(2,1)S(1)}, bf16[1,256,768]{2,1,0:T(8,128)(2,1)}, u32[]{:S(2)}, u32[]{:S(2)}) collective-permute-start(bf16[1,256,768]{2,1,0:T(8,128)(2,1)S(1)} %slice.22), channel_id=1, source_target_pairs={{0,112},{16,0},{32,16},{48,32},{64,48},{80,64},{96,80},{112,96},{1... | collective-permute-start | bytes 1179656 | tf_op jit(solution)/shard_map/ppermute | solution.py:41
  133.0 26.1 %collective-permute-start.26 = (f32[6,256]{1,0:T(8,128)S(1)}, f32[6,256]{1,0:T(8,128)S(1)}, u32[]{:S(2)}, u32[]{:S(2)}) collective-permute-start(f32[6,256]{1,0:T(8,128)S(1)} %get-tuple-element.111), channel_id=1, source_target_pairs={{0,1},{1,0},{2,3},{3,2},{4,5},{5,4},{6,7},{7,6},{8,9},{9,8},{10,11... | collective-permute-start | bytes 18440 | tf_op jit(solution)/shard_map/ppermute | solution.py:52
  146.6 12.6 %collective-permute-start.27 = (f32[6,256]{1,0:T(8,128)S(1)}, f32[6,256]{1,0:T(8,128)S(1)}, u32[]{:S(2)}, u32[]{:S(2)}) collective-permute-start(f32[6,256]{1,0:T(8,128)S(1)} %get-tuple-element.110), channel_id=1, source_target_pairs={{0,129},{1,128},{128,1},{129,0},{2,131},{3,130},{130,3},{131,2},{4... | collective-permute-start | bytes 18440 | tf_op jit(solution)/shard_map/ppermute | solution.py:56
  153.4 14.5 %all-to-all-start = ((f32[32,1,256]{2,1,0:T(1,128)}), f32[32,1,256]{2,1,0:T(1,128)S(1)}, u32[]{:S(2)}, u32[]{:S(2)}) async-start(f32[32,1,256]{2,1,0:T(1,128)} %copy.7), calls=%async_computation | async-start | bytes 65536 | tf_op jit(solution)/shard_map/all_to_all | solution.py:278

commit v2 on v1

--- a/solution.py
+++ b/solution.py
@@ -14,7 +14,9 @@
 SHARPNESS = 30.0
 EPSILON = 1e-06
 EXP2_SCALE = SHARPNESS / math.log(2.0)
-UNROLL = 4
+UNROLL = 6
+GROUP = 4
+AHEAD = 6
 VMEM_MIB = 63
 FAR_FROM = 4
 IDS_AT = 3
@@ -23,12 +25,12 @@
 AXES = ("y", "z", "x", "h", "k")
 
 SLOTS = (
-    ( ((0, 1), ((0, 0),)), ((-1, 0), ((0, 0),)), ((0, -1), ((0, 0),)), ((1, 0), ((0, 0),)) ),
-    ( ((1, 0), ((1, 0),)), ((-1, 0), ((-1, 0),)), ((0, 1), ((0, 1),)), ((0, -1), ((-1, 0),)) ),
-    ( ((0, 1), ((2, 0),)), ((0, -1), ((1, 0),)), ((-1, 0), ((-2, 0),)), ((1, 0), ((2, 0),)) ),
-    ( ((-1, 0), ((0, 2), (0, 1),)), ((1, 0), ((0, 2), (0, 1),)), ((0, 1), ((3, 0), (-3, 0),)), ((0, -1), ((3, 0), (-3, 0),)) ),
-    ( ((-1, 0), ((3, -1), (-3, -1),)), ((0, 1), ((3, 1), (-3, 1),)), ((0, -1), ((-2, 0),)), ((1, 0), ((3, 1), (-3, 1),)) ),
-    ( ((0, 1), ((-2, 1),)), ((0, -1), ((2, -1),)), ((1, 0), ((3, 0),)), ((-1, 0), ((-3, 2),)) ),
+    ( ((0, -1), ((0, 0),)), ((-1, 0), ((0, 0),)), ((1, 0), ((0, 0),)), ((0, 1), ((0, 0),)) ),
+    ( ((-1, 0), ((-1, 0),)), ((1, 0), ((1, 0),)), ((0, -1), ((-1, 0),)), ((0, 1), ((0, 1),)) ),
+    ( ((1, 0), ((0, 2),)), ((0, 1), ((2, 0),)), ((0, -1), ((2, 0),)), ((-1, 0), ((-2, 0),)) ),
+    ( ((-1, 0), ((2, 1), (2, -1),)), ((0, -1), ((-3, 0), (-2, 0),)), ((1, 0), ((2, 1), (2, -1),)), ((0, 1), ((-3, 0), (-2, 0),)) ),
+    ( ((1, 0), ((3, 1), (3, -1),)), ((0, 1), ((3, 1), (3, -1),)), ((-1, 0), ((0, 1), (-3, 0),)), ((0, -1), ((-3, -1), (-2, -1),)) ),
+    ( ((-1, 0), ((0, 2),)), ((0, -1), ((2, -1),)), ((1, 0), ((3, 2),)) ),
 )
 
 
@@ -69,22 +71,25 @@
     return lax.dot_general(ones, terms, (((1,), (1,)), ((), ())), preferred_element_type=jnp.float32)[:1]
 
 
-def as_column(row):
-    at = lax.broadcasted_iota(jnp.int32, (16, row.shape[1]), 0)
-    terms = jnp.zeros((16, row.shape[1]), jnp.float32)
-    for i, term in enumerate(three_terms(row)):
-        terms = jnp.where(at == i, term.astype(jnp.float32), terms)
-    ones = jnp.ones((16, LANES), jnp.bfloat16)
-    return lax.dot_general(
-        terms.astype(jnp.bfloat16), ones, (((0,), (0,)), ((), ())), preferred_element_type=jnp.float32
-    )
+def lane_totals(values):
+    terms = jnp.concatenate(three_terms(values), axis=1)
+    ones = jnp.ones((terms.shape[1], LANES), jnp.bfloat16)
+    return lax.dot_general(terms, ones, (((1,), (0,)), ((), ())), preferred_element_type=jnp.float32)
+
+
+def squares(block):
+    total = None
+    for part in range(block.shape[1] // LANES):
+        values = block[:, part * LANES : (part + 1) * LANES].astype(jnp.float32)
+        total = values * values if total is None else total + values * values
+    return total
 
 
 def pair_kernel(news, olds, sizes, n_sets, first, table, *refs):
     arrays, refs = refs[: len(sizes)], refs[len(sizes) :]
     sets, refs = refs[:n_sets], refs[n_sets:]
-    before, refs = ((), refs) if first else (refs[:5], refs[5:])
-    rows, cols, norms, scale, next_turn, held, blocks, columns, sums, listed, places, sems = refs
+    before, refs = ((), refs) if first else (refs[:4], refs[4:])
+    rows, cols, scale, next_turn, held, blocks, columns, sums, added, listed, places, sems, set_sems = refs
     n_new, n_guest = len(news), len(news) + len(olds)
     n_set, n_each = blocks.shape[0], sets[0].shape[0]
     z, x = table[table.shape[0] - 2], table[table.shape[0] - 1]
@@ -93,41 +98,47 @@
     for a, (array, size) in enumerate(zip(arrays, sizes, strict=True)):
         guest_copies.append((at, pltpu.make_async_copy(array, held.at[pl.ds(at, size)], sems.at[a])))
         at += size
-    set_copies = [
-        pltpu.make_async_copy(one, blocks.at[pl.ds(j * n_each, n_each)], sems.at[len(sizes) + j])
-        for j, one in enumerate(sets)
-    ]
+    def start_block(r):
+        for j in range(n_sets):
+
+            @pl.when((r >= j * n_each) & (r < (j + 1) * n_each))
+            def _(j=j):
+                pltpu.make_async_copy(sets[j].at[r - j * n_each], blocks.at[r], set_sems.at[r]).start()
+
     for at, copy in guest_copies:
         if at < n_new:
             copy.start()
-    for copy in set_copies:
-        copy.start()
-    for at, copy in guest_copies:
-        if at >= n_new:
-            copy.start()
     for g, (dz, dx) in enumerate([*news, *olds]):
         places[g] = lax.rem(z - dz + NZ, NZ) * NX + lax.rem(x - dx + NX, NX)
 
     def list_pairs(first_guest, last_guest, first_block):
-        def list_guest(g, count):
-            wanted = table[places[g]]
-
-            def list_pair(r, count):
+        def list_block(r, count):
+            own = table[NZ * NX + r]
+            for g in range(first_guest, last_guest):
                 listed[0, count] = r
                 listed[1, count] = g
-                return count + jnp.where(table[NZ * NX + r] == wanted, 1, 0)
-
-            return lax.fori_loop(first_block, n_set, list_pair, count)
-
-        count = lax.fori_loop(first_guest, last_guest, list_guest, 0)
+                count = count + jnp.where(table[places[g]] == own, 1, 0)
+            return count
+
+        count = lax.fori_loop(first_block, n_set, list_block, 0)
         for u in range(UNROLL):
             listed[0, count + u] = first_block
             listed[1, count + u] = first_guest
         return count
 
-    def run_pairs(count):
-        @pl.loop(0, lax.div(count + UNROLL - 1, UNROLL))
-        def _(step):
+    def wait_blocks(start, stop):
+        def wait_block(r, _):
+            pltpu.make_async_copy(sets[0].at[0], blocks.at[r], set_sems.at[r]).wait()
+            start_block(r + AHEAD)
+            return 0
+
+        lax.fori_loop(start, stop, wait_block, 0)
+        return jnp.maximum(start, stop)
+
+    def run_pairs(count, waited):
+        def run_step(step, waited):
+            last = jnp.minimum(step * UNROLL + UNROLL, count) - 1
+            waited = wait_blocks(waited, listed[0, last] + 1)
             for u in range(UNROLL):
                 at = step * UNROLL + u
                 r, g = listed[0, at], listed[1, at]
@@ -143,53 +154,59 @@
                     total = total + tile
                     rows[r, :, lanes] += jnp.sum(tile.reshape(BLOCK // 8, 8, LANES), axis=0)
                 sums[g] = total
+            return waited
+
+        return lax.fori_loop(0, lax.div(count + UNROLL - 1, UNROLL), run_step, waited)
+
+    def in_groups(start, stop, task):
+        size = min(GROUP, stop - start)
+
+        @pl.loop(0, -(-(stop - start) // size))
+        def _(step):
+            for u in range(size):
+                task(jnp.minimum(start + step * size + u, stop - 1))
+
+    def set_column(g):
+        columns[g] = 1.0 / jnp.sqrt(lane_totals(squares(held.at[g])) + EPSILON)
+
+    def set_scale(r):
+        scale[pl.ds(r, 1), :] = EXP2_SCALE / jnp.sqrt(lane_sums(squares(blocks.at[r])) + EPSILON)
+
+    def set_col_sums(g):
+        cols[places[g]] = added[places[g]] + lane_sums(sums[g])
 
     count = list_pairs(0, n_new, 0)
     if first:
-        for out in (rows, cols, norms, scale, next_turn):
+        for out in (rows, cols, scale, next_turn):
             out[...] = jnp.zeros_like(out)
     else:
-        for out, value in zip((rows, cols, norms, scale, next_turn), before, strict=True):
+        for out, value in zip((rows, cols, scale, next_turn), before, strict=True):
             out[...] = value[...]
     sums[...] = jnp.zeros_like(sums)
     for at, copy in guest_copies:
         if at < n_new:
             copy.wait()
-
-    def inverse_norms(block):
-        squares = jnp.zeros((BLOCK, LANES), jnp.float32)
-        for part in range(block.shape[1] // LANES):
-            values = block[:, part * LANES : (part + 1) * LANES].astype(jnp.float32)
-            squares = squares + values * values
-        return 1.0 / jnp.sqrt(lane_sums(squares) + EPSILON)
-
-    @pl.loop(0, n_new)
-    def _(g):
-        norms[pl.ds(places[g], 1), :] = inverse_norms(held.at[g])
-
-    @pl.loop(0, n_guest)
-    def _(g):
-        columns[g] = as_column(norms[pl.ds(places[g], 1), :])
-
-    for copy in set_copies:
-        copy.wait()
+    for r in range(AHEAD):
+        start_block(r)
+    for at, copy in guest_copies:
+        if at >= n_new:
+            copy.start()
+    in_groups(0, n_new, set_column)
+    waited = 0
     if first or olds:
-
-        @pl.loop(n_set - n_each, n_set)
-        def _(r):
-            scale[pl.ds(r, 1), :] = inverse_norms(blocks.at[r]) * EXP2_SCALE
-
-    run_pairs(count)
+        waited = wait_blocks(0, n_set)
+        in_groups(n_set - n_each, n_set, set_scale)
+    waited = run_pairs(count, waited)
     if olds:
         count = list_pairs(n_new, n_guest, n_set - n_each)
         for at, copy in guest_copies:
             if at >= n_new:
                 copy.wait()
-        run_pairs(count)
-
-    @pl.loop(0, n_guest)
-    def _(g):
-        cols[pl.ds(places[g], 1), :] += lane_sums(sums[g])
+        in_groups(n_new, n_guest, set_column)
+        waited = run_pairs(count, waited)
+    wait_blocks(waited, n_set)
+    added[...] = cols[...]
+    in_groups(0, n_guest, set_col_sums)
 
 
 def pairs(table, news, olds, arrays, sets, running):
@@ -197,20 +214,22 @@
     smem, vmem, hbm = (pl.BlockSpec(memory_space=m) for m in (pltpu.SMEM, pltpu.VMEM, pltpu.HBM))
     first = running is None
     tiles = (len(news) * n_set + len(olds) * sets[-1].shape[0]) // 3
-    shapes = [(2 * sets[0].shape[0], 8, BLOCK), (NZ * NX, BLOCK), (NZ * NX, BLOCK), (16, BLOCK), (8, LANES)]
+    shapes = [(2 * sets[0].shape[0], 8, BLOCK), (NZ * NX, 1, BLOCK), (16, BLOCK), (8, LANES)]
     return pl.pallas_call(
         functools.partial(pair_kernel, news, olds, [a.shape[0] for a in arrays], len(sets), first),
-        in_specs=[smem] + [hbm] * (len(arrays) + len(sets)) + [vmem] * (0 if first else 5),
-        out_specs=[vmem] * 5,
+        in_specs=[smem] + [hbm] * (len(arrays) + len(sets)) + [vmem] * (0 if first else 4),
+        out_specs=[vmem] * 4,
         out_shape=[jax.ShapeDtypeStruct(shape, jnp.float32) for shape in shapes],
         scratch_shapes=[
             pltpu.VMEM((n_guest, *arrays[0].shape[1:]), jnp.bfloat16),
             pltpu.VMEM((n_set, *arrays[0].shape[1:]), jnp.bfloat16),
             pltpu.VMEM((n_guest, BLOCK, LANES), jnp.float32),
             pltpu.VMEM((n_guest, BLOCK, LANES), jnp.float32),
+            pltpu.VMEM(shapes[1], jnp.float32),
             pltpu.SMEM((2, n_guest * n_set + UNROLL), jnp.int32),
             pltpu.SMEM((n_guest,), jnp.int32),
-            pltpu.SemaphoreType.DMA((len(arrays) + len(sets),)),
+            pltpu.SemaphoreType.DMA((len(arrays),)),
+            pltpu.SemaphoreType.DMA((n_set,)),
         ],
         compiler_params=pltpu.CompilerParams(vmem_limit_bytes=VMEM_MIB << 20),
         cost_estimate=pl.CostEstimate(
@@ -271,12 +290,12 @@
             olds = backlog
         running = pairs(table, flat(newest), flat(olds), [stacks[p] for p in [*newest, *olds]], sets, running)
         backlog = backlog + newest
-        done = [running[4]]
+        done = [running[3]]
         newest = coming
     rows, cols = jnp.sum(running[0], axis=1), running[1]
 
     incoming = lax.all_to_all(cols, ("z", "x"), 0, 0, tiled=True)
-    guest_density = jnp.sum(incoming, axis=0)
+    guest_density = jnp.sum(incoming, axis=(0, 1))
     home_density = to_sibling(rows[:slots]) + to_partner(rows[slots:])
 
     home_ids = lax.dynamic_slice_in_dim(home_cluster, device_of(y, k) * slots, slots)

time: 171 us -> 158 us (0.924); the launches traced: 168 us -> 158 us
  Pallas kernels: 68.9 us -> 60.3 us
  starting transfers between devices: 57.5 us -> 53.4 us
  waiting for transfers between devices: 23 us -> 27.1 us
  local copies, waits for them, and re-layouts: 9.03 us -> 6.22 us
    pallas_call x6, Pallas kernels: 68.9 us -> 60.3 us  [pairs(): pl.pallas_call(functools.partial(pair_kernel, news, olds, [a.shape[0] for...]
    ppermute x2, starting transfers between devices: 16.9 us -> 9.05 us  [to_sibling(): return lax.ppermute(value, 'k', [(0, 1), (1, 0)])]
    ppermute x12, waiting for transfers between devices: 5.93 us -> 13.7 us  [shift(): return lax.ppermute(value, 'z', [(i, (i + dz) % NZ) for i in range(NZ)])]
    all_to_all x1, starting transfers between devices: 5.78 us -> 12.1 us  [body(): incoming = lax.all_to_all(cols, ('z', 'x'), 0, 0, tiled=True)]
    ppermute x12 -> x11, waiting for transfers between devices: 9.04 us -> 5.52 us  [shift(): return lax.ppermute(value, 'x', [(i, (i + dx) % NX) for i in range(NX)])]
    slice x3 -> x1, local copies, waits for them, and re-layouts: 3.86 us -> 1.02 us  [one(): return blocks[nodes.index(n)]]
    ppermute x12 -> x11, starting transfers between devices: 15 us -> 12.9 us  [shift(): return lax.ppermute(value, 'x', [(i, (i + dx) % NX) for i in range(NX)])]
  transfers between devices with their start and end apart: 29 -> 28, of which waited for: 8 -> 7; matrix products, arithmetic and copies ran while one was open for 9% -> 7% of each run, Pallas kernels for 36% -> 33%
where the time goes in v2:
time: 158 us
  Pallas kernels  60.3 us (38%)
  starting transfers between devices  53.4 us (34%)
  waiting for transfers between devices  27.1 us (17%)
  other arithmetic  8.51 us (5%)
  local copies, waits for them, and re-layouts  6.22 us (4%)
  between operations  2.22 us (1%)
    pallas_call x6, Pallas kernels, pairs(): pl.pallas_call(functools.partial(pair_kernel, news, olds, [a.shape[0] for...  60.3 us
    ppermute x12, starting transfers between devices, shift(): return lax.ppermute(value, 'z', [(i, (i + dz) % NZ) for i in range(NZ)])  16.2 us
    ppermute x12, waiting for transfers between devices, shift(): return lax.ppermute(value, 'z', [(i, (i + dz) % NZ) for i in range(NZ)])  13.7 us
    ppermute x11, starting transfers between devices, shift(): return lax.ppermute(value, 'x', [(i, (i + dx) % NX) for i in range(NX)])  12.9 us
    all_to_all x1, starting transfers between devices, body(): incoming = lax.all_to_all(cols, ('z', 'x'), 0, 0, tiled=True)  12.1 us
    ppermute x2, starting transfers between devices, to_sibling(): return lax.ppermute(value, 'k', [(0, 1), (1, 0)])  9.05 us
    all_to_all x1, waiting for transfers between devices, body(): incoming = lax.all_to_all(cols, ('z', 'x'), 0, 0, tiled=True)  7.91 us
    ppermute x11, waiting for transfers between devices, shift(): return lax.ppermute(value, 'x', [(i, (i + dx) % NX) for i in range(NX)])  5.52 us
  transfers between devices with their start and end apart: 28, of which 7 were waited for; matrix products, arithmetic and copies ran while one was open for 7% of the time, Pallas kernels for 33%

profile of v2, /device:TPU:1, one launch (start us, length us, event | category | flops | bytes accessed | tf_op | source)
XLA Modules:
  0.0 157.8 jit_solution(12484269558545706393)
XLA Ops:
  0.6 3.3 %collective-permute-start.2 = (bf16[1536,768]{1,0:T(8,128)(2,1)}, bf16[1536,768]{1,0:T(8,128)(2,1)S(1)}, u32[]{:S(2)}, u32[]{:S(2)}) collective-permute-start(bf16[1536,768]{1,0:T(8,128)(2,1)} %param.5), channel_id=1, source_target_pairs={{0,1},{1,0},{2,3},{3,2},{4,5},{5,4},{6,7},{7,6},{8,9},{9,8},{10,11... | collective-permute-start | bytes 7077896 | tf_op jit(solution)/shard_map/ppermute | solution.py:54
  4.0 0.0 collective-permute-start.21
  4.0 5.1 %collective-permute-start = (bf16[1,256,768]{2,1,0:T(8,128)(2,1)}, bf16[1,256,768]{2,1,0:T(8,128)(2,1)S(1)}, u32[]{:S(2)}, u32[]{:S(2)}) collective-permute-start(bf16[1,256,768]{2,1,0:T(8,128)(2,1)} %bitcast.12), channel_id=1, source_target_pairs={{0,112},{16,0},{32,16},{48,32},{64,48},{80,64},{96,80},{112,96},{1... | collective-permute-start | bytes 1179656 | tf_op jit(solution)/shard_map/ppermute | solution.py:43
  9.1 0.0 collective-permute-start.1
  9.1 2.5 %collective-permute-start.4 = (bf16[1,256,768]{2,1,0:T(8,128)(2,1)}, bf16[1,256,768]{2,1,0:T(8,128)(2,1)S(1)}, u32[]{:S(2)}, u32[]{:S(2)}) collective-permute-start(bf16[1,256,768]{2,1,0:T(8,128)(2,1)} %bitcast.14), channel_id=1, source_target_pairs={{0,12},{4,0},{8,4},{12,8},{1,13},{5,1},{9,5},{13,9},{2,14},{6,2},{... | collective-permute-start | bytes 1179656 | tf_op jit(solution)/shard_map/ppermute | solution.py:45
  11.6 0.0 collective-permute-done.2
  11.6 5.9 %collective-permute-done.refs_2_.refs_6_ = bf16[1,256,768]{2,1,0:T(8,128)(2,1)S(1)} collective-permute-done((bf16[1,256,768]{2,1,0:T(8,128)(2,1)}, bf16[1,256,768]{2,1,0:T(8,128)(2,1)S(1)}, u32[]{:S(2)}, u32[]{:S(2)}) %collective-permute-start) | collective-permute-done | bytes 393248 | tf_op jit(solution)/shard_map/ppermute | solution.py:43
  17.5 3.1 %collective-permute-done.1.refs_3_.refs_7_ = bf16[1,256,768]{2,1,0:T(8,128)(2,1)} collective-permute-done((bf16[1,256,768]{2,1,0:T(8,128)(2,1)}, bf16[1,256,768]{2,1,0:T(8,128)(2,1)}, u32[]{:S(2)}, u32[]{:S(2)}) %collective-permute-start.1) | collective-permute-done | bytes 393248 | tf_op jit(solution)/shard_map/ppermute | solution.py:43
  20.5 0.0 collective-permute-done.4.refs_1_.refs_5_
  20.6 2.1 %collective-permute-done.3.refs_4_.refs_8_ = bf16[1,256,768]{2,1,0:T(8,128)(2,1)S(1)} collective-permute-done((bf16[1,256,768]{2,1,0:T(8,128)(2,1)}, bf16[1,256,768]{2,1,0:T(8,128)(2,1)S(1)}, u32[]{:S(2)}, u32[]{:S(2)}) %collective-permute-start.3) | collective-permute-done | bytes 393248 | tf_op jit(solution)/shard_map/ppermute | solution.py:45
  22.6 0.0 collective-permute-start.5
  22.6 2.5 %collective-permute-start.7 = (bf16[1,256,768]{2,1,0:T(8,128)(2,1)S(1)}, bf16[1,256,768]{2,1,0:T(8,128)(2,1)}, u32[]{:S(2)}, u32[]{:S(2)}) collective-permute-start(bf16[1,256,768]{2,1,0:T(8,128)(2,1)S(1)} %collective-permute-done.refs_2_.refs_6_), channel_id=1, source_target_pairs={{0,112},{16,0},{32,16},{48,32},{64,48},{80,64},{96,80},{112,96},{1... | collective-permute-start | bytes 1179656 | tf_op jit(solution)/shard_map/ppermute | solution.py:43
  25.1 2.6 %collective-permute-start.8 = (bf16[1,256,768]{2,1,0:T(8,128)(2,1)S(1)}, bf16[1,256,768]{2,1,0:T(8,128)(2,1)}, u32[]{:S(2)}, u32[]{:S(2)}) collective-permute-start(bf16[1,256,768]{2,1,0:T(8,128)(2,1)S(1)} %collective-permute-done.refs_2_.refs_6_), channel_id=1, source_target_pairs={{0,12},{4,0},{8,4},{12,8},{1,13},{5,1},{9,5},{13,9},{2,14},{6,2},{... | collective-permute-start | bytes 1179656 | tf_op jit(solution)/shard_map/ppermute | solution.py:45
  27.7 0.8 reshape.43
  28.5 0.2 dynamic-slice_reduce_fusion
  28.7 0.9 fusion.2
  29.5 0.6 concatenate.3.table
  30.1 8.8 %pairs.6 = (f32[12,8,256]{2,1,0:T(8,128)}, f32[32,1,256]{2,1,0:T(1,128)}, f32[16,256]{1,0:T(8,128)}, f32[8,128]{1,0:T(8,128)}) custom-call(s32[46]{0:T(128)} %concatenate.3.table, bf16[1,256,768]{2,1,0:T(8,128)(2,1)} %bitcast.16, bf16[1,256,768]{2,1,0:T(8,128)(2,1)} %copy-done.6, bf16[1,256,768]{2,1,0:T(8,128)(2,1)} %copy-done.5, ...), custom_call_target="tpu_custom_call" | custom-call | flops 2013265920 | bytes 4000000 | tf_op jit(solution)/shard_map/pairs/pallas_call | solution.py:218
  38.9 0.0 collective-permute-done.7.refs_0_.refs_9_
  38.9 0.0 collective-permute-done.6.refs_1_.refs_10_
  39.0 0.1 collective-permute-start.10
  39.1 2.7 %collective-permute-start.9 = (bf16[1,256,768]{2,1,0:T(8,128)(2,1)}, bf16[1,256,768]{2,1,0:T(8,128)(2,1)}, u32[]{:S(2)}, u32[]{:S(2)}) collective-permute-start(bf16[1,256,768]{2,1,0:T(8,128)(2,1)} %collective-permute-done.6.refs_1_.refs_10_), channel_id=1, source_target_pairs={{0,12},{4,0},{8,4},{12,8},{1,13},{5,1},{9,5},{13,9},{2,14},{6,2},{... | collective-permute-start | bytes 1179656 | tf_op jit(solution)/shard_map/ppermute | solution.py:45
  41.7 1.8 %collective-permute-start.11 = (bf16[1,256,768]{2,1,0:T(8,128)(2,1)}, bf16[1,256,768]{2,1,0:T(8,128)(2,1)}, u32[]{:S(2)}, u32[]{:S(2)}) collective-permute-start(bf16[1,256,768]{2,1,0:T(8,128)(2,1)} %collective-permute-done.7.refs_0_.refs_9_), channel_id=1, source_target_pairs={{0,112},{16,0},{32,16},{48,32},{64,48},{80,64},{96,80},{112,96},{1... | collective-permute-start | bytes 1179656 | tf_op jit(solution)/shard_map/ppermute | solution.py:43
  43.5 0.0 collective-permute-start.12
  43.5 6.4 %pairs.7 = (f32[12,8,256]{2,1,0:T(8,128)}, f32[32,1,256]{2,1,0:T(1,128)}, f32[16,256]{1,0:T(8,128)}, f32[8,128]{1,0:T(8,128)}) custom-call(s32[46]{0:T(128)} %concatenate.3.table, bf16[1,256,768]{2,1,0:T(8,128)(2,1)} %collective-permute-done.7.refs_0_.refs_9_, bf16[1,256,768]{2,1,0:T(8,128)(2,1)} %collective-permute-done.6.refs_1_.refs_10_, ...), custom_call_target="tpu_custom_call" | custom-call | flops 1610612736 | bytes 3200000 | tf_op jit(solution)/shard_map/pairs/pallas_call | solution.py:218
  50.0 0.0 copy-start.3
  50.0 0.0 copy-start.2
  50.0 0.0 collective-permute-done.10.refs_1_.refs_14_
  50.0 0.8 copy-done
  50.8 1.2 pad_maximum_fusion
  52.0 0.0 collective-permute-done.11.refs_3_.refs_16_
  52.0 2.7 %pad_maximum_fusion.2 = (bf16[2,256,768]{2,1,0:T(8,128)(2,1)}, bf16[2,256,768]{2,1,0:T(8,128)(2,1)}) fusion(bf16[1,256,768]{2,1,0:T(8,128)(2,1)} %collective-permute-done.11.refs_3_.refs_16_, bf16[1,256,768]{2,1,0:T(8,128)(2,1)} %copy-done.1, bf16[1,256,768]{2,1,0:T(8,128)(2,1)} %collective-permute-done.7.refs_0_.refs_9_), kind=kLoop, calls=%fused_computation.2 | loop fusion | flops 786432 | bytes 2752512 | tf_op jit(solution)/shard_map/stack | solution.py:265
  54.7 0.7 collective-permute-start.14
  55.4 2.6 %collective-permute-start.15 = (bf16[2,256,768]{2,1,0:T(8,128)(2,1)S(1)}, bf16[2,256,768]{2,1,0:T(8,128)(2,1)}, u32[]{:S(2)}, u32[]{:S(2)}) collective-permute-start(bf16[2,256,768]{2,1,0:T(8,128)(2,1)S(1)} %pad_maximum_fusion), channel_id=1, source_target_pairs={{0,112},{16,0},{32,16},{48,32},{64,48},{80,64},{96,80},{112,96},{1... | collective-permute-start | bytes 2359304 | tf_op jit(solution)/shard_map/ppermute | solution.py:43
  58.0 0.8 collective-permute-start.16
  58.9 0.6 dynamic_slice.19
  59.5 0.1 dynamic_slice.18
  59.5 1.3 convert_reduce_fusion.1
  60.8 0.2 convert_reduce_fusion.2
  61.0 0.2 convert_reduce_fusion
  61.2 4.9 %pairs.8 = (f32[12,8,256]{2,1,0:T(8,128)}, f32[32,1,256]{2,1,0:T(1,128)}, f32[16,256]{1,0:T(8,128)}, f32[8,128]{1,0:T(8,128)}) custom-call(s32[46]{0:T(128)} %concatenate.3.table, bf16[1,256,768]{2,1,0:T(8,128)(2,1)} %collective-permute-done.12.refs_0_.refs_13_, bf16[1,256,768]{2,1,0:T(8,128)(2,1)} %copy-done, ...), custom_call_target="tpu_custom_call" | custom-call | flops 1610612736 | bytes 3200000 | tf_op jit(solution)/shard_map/pairs/pallas_call | solution.py:218
  66.1 4.6 %collective-permute-done.13.refs_2_ = bf16[2,256,768]{2,1,0:T(8,128)(2,1)} collective-permute-done((bf16[2,256,768]{2,1,0:T(8,128)(2,1)S(1)}, bf16[2,256,768]{2,1,0:T(8,128)(2,1)}, u32[]{:S(2)}, u32[]{:S(2)}) %collective-permute-start.13) | collective-permute-done | bytes 786464 | tf_op jit(solution)/shard_map/ppermute | solution.py:43
  70.7 0.2 collective-permute-done.15.refs_0_
  70.8 3.4 %collective-permute-done.16.refs_3_ = bf16[2,256,768]{2,1,0:T(8,128)(2,1)} collective-permute-done((bf16[2,256,768]{2,1,0:T(8,128)(2,1)}, bf16[2,256,768]{2,1,0:T(8,128)(2,1)}, u32[]{:S(2)}, u32[]{:S(2)}) %collective-permute-start.16) | collective-permute-done | bytes 786464 | tf_op jit(solution)/shard_map/ppermute | solution.py:45
  74.3 2.7 %collective-permute-start.19 = (bf16[2,256,768]{2,1,0:T(8,128)(2,1)}, bf16[2,256,768]{2,1,0:T(8,128)(2,1)}, u32[]{:S(2)}, u32[]{:S(2)}) collective-permute-start(bf16[2,256,768]{2,1,0:T(8,128)(2,1)} %get-tuple-element.77), channel_id=1, source_target_pairs={{0,112},{16,0},{32,16},{48,32},{64,48},{80,64},{96,80},{112,96},{1... | collective-permute-start | bytes 2359304 | tf_op jit(solution)/shard_map/ppermute | solution.py:43
  77.0 2.7 %collective-permute-start.20 = (bf16[2,256,768]{2,1,0:T(8,128)(2,1)}, bf16[2,256,768]{2,1,0:T(8,128)(2,1)}, u32[]{:S(2)}, u32[]{:S(2)}) collective-permute-start(bf16[2,256,768]{2,1,0:T(8,128)(2,1)} %collective-permute-done.14.refs_1_), channel_id=1, source_target_pairs={{0,12},{4,0},{8,4},{12,8},{1,13},{5,1},{9,5},{13,9},{2,14},{6,2},{... | collective-permute-start | bytes 2359304 | tf_op jit(solution)/shard_map/ppermute | solution.py:45
  79.7 21.9 %pairs.9 = (f32[12,8,256]{2,1,0:T(8,128)}, f32[32,1,256]{2,1,0:T(1,128)}, f32[16,256]{1,0:T(8,128)}, f32[8,128]{1,0:T(8,128)}) custom-call(s32[46]{0:T(128)} %concatenate.3.table, bf16[2,256,768]{2,1,0:T(8,128)(2,1)} %collective-permute-done.15.refs_0_, bf16[2,256,768]{2,1,0:T(8,128)(2,1)} %collective-permute-done.14.refs_1_, ...), custom_call_target="tpu_custom_call" | custom-call | flops 11676942336 | bytes 23200000 | tf_op jit(solution)/shard_map/pairs/pallas_call | solution.py:218
  101.5 1.0 slice.12
  102.6 1.0 collective-permute-start.22
  103.6 0.9 collective-permute-start.23
  104.5 0.6 collective-permute-start.24
  105.1 10.8 %pairs.10 = (f32[12,8,256]{2,1,0:T(8,128)}, f32[32,1,256]{2,1,0:T(1,128)}, f32[16,256]{1,0:T(8,128)}, f32[8,128]{1,0:T(8,128)}) custom-call(s32[46]{0:T(128)} %concatenate.3.table, bf16[2,256,768]{2,1,0:T(8,128)(2,1)} %collective-permute-done.18.refs_0_, bf16[2,256,768]{2,1,0:T(8,128)(2,1)} %collective-permute-done.17.refs_1_, ...), custom_call_target="tpu_custom_call" | custom-call | flops 6442450944 | bytes 12800000 | tf_op jit(solution)/shard_map/pairs/pallas_call | solution.py:218
  115.9 0.7 copy-done.7
  116.6 7.5 %pairs.11 = (f32[12,8,256]{2,1,0:T(8,128)}, f32[32,1,256]{2,1,0:T(1,128)}, f32[16,256]{1,0:T(8,128)}, f32[8,128]{1,0:T(8,128)}) custom-call(s32[46]{0:T(128)} %concatenate.3.table, bf16[1,256,768]{2,1,0:T(8,128)(2,1)} %copy-done.7, bf16[1,256,768]{2,1,0:T(8,128)(2,1)} %collective-permute-done.23.refs_1_, ...), custom_call_target="tpu_custom_call" | custom-call | flops 2415919104 | bytes 4800000 | tf_op jit(solution)/shard_map/pairs/pallas_call | solution.py:218
  124.1 0.9 reduce_sum.54
  125.1 5.7 %collective-permute-start.25 = (f32[6,256]{1,0:T(8,128)S(1)}, f32[6,256]{1,0:T(8,128)S(1)}, u32[]{:S(2)}, u32[]{:S(2)}) collective-permute-start(f32[6,256]{1,0:T(8,128)S(1)} %get-tuple-element.101), channel_id=1, source_target_pairs={{0,1},{1,0},{2,3},{3,2},{4,5},{5,4},{6,7},{7,6},{8,9},{9,8},{10,11... | collective-permute-start | bytes 18440 | tf_op jit(solution)/shard_map/ppermute | solution.py:54
  130.8 3.1 %collective-permute-start.26 = (f32[6,256]{1,0:T(8,128)S(1)}, f32[6,256]{1,0:T(8,128)S(1)}, u32[]{:S(2)}, u32[]{:S(2)}) collective-permute-start(f32[6,256]{1,0:T(8,128)S(1)} %get-tuple-element.100), channel_id=1, source_target_pairs={{0,129},{1,128},{128,1},{129,0},{2,131},{3,130},{130,3},{131,2},{4... | collective-permute-start | bytes 18440 | tf_op jit(solution)/shard_map/ppermute | solution.py:58
  133.9 1.3 fusion
  136.4 12.1 %all-to-all-start = ((f32[32,1,256]{2,1,0:T(1,128)}), f32[32,1,256]{2,1,0:T(1,128)S(1)}, u32[]{:S(2)}, u32[]{:S(2)}) async-start(f32[32,1,256]{2,1,0:T(1,128)} %get-tuple-element.97), calls=%async_computation | async-start | bytes 65536 | tf_op jit(solution)/shard_map/all_to_all | solution.py:297
  148.6 0.1 log_subtract_fusion
  148.7 0.6 reshape.47
  149.3 7.9 %all-to-all-done = f32[32,1,256]{2,1,0:T(1,128)S(1)} async-done(((f32[32,1,256]{2,1,0:T(1,128)}), f32[32,1,256]{2,1,0:T(1,128)S(1)}, u32[]{:S(2)}, u32[]{:S(2)}) %all-to-all-start) | async-done | bytes 32800 | tf_op jit(solution)/shard_map/all_to_all | solution.py:297
  157.2 0.1 reduce_sum.57
  157.2 0.6 log_subtract_fusion.1
  (34 shorter events, 0.1 us)
Async XLA Ops:
  0.6 10.9 %collective-permute-start.2 = (bf16[1536,768]{1,0:T(8,128)(2,1)}, bf16[1536,768]{1,0:T(8,128)(2,1)S(1)}, u32[]{:S(2)}, u32[]{:S(2)}) collective-permute-start(bf16[1536,768]{1,0:T(8,128)(2,1)} %param.5), channel_id=1, source_target_pairs={{0,1},{1,0},{2,3},{3,2},{4,5},{5,4},{6,7},{7,6},{8,9},{9,8},{10,11... | collective-permute-start | bytes 7077896 | tf_op jit(solution)/shard_map/ppermute | solution.py:54
  4.0 62.2 %collective-permute-start.21 = (bf16[1536,768]{1,0:T(8,128)(2,1)}, bf16[1536,768]{1,0:T(8,128)(2,1)}, u32[]{:S(2)}, u32[]{:S(2)}) collective-permute-start(bf16[1536,768]{1,0:T(8,128)(2,1)} %param.5), channel_id=1, source_target_pairs={{0,129},{1,128},{128,1},{129,0},{2,131},{3,130},{130,3},{131,2},{4... | collective-permute-start | bytes 7077896 | tf_op jit(solution)/shard_map/ppermute | solution.py:58
  4.0 13.5 %collective-permute-start = (bf16[1,256,768]{2,1,0:T(8,128)(2,1)}, bf16[1,256,768]{2,1,0:T(8,128)(2,1)S(1)}, u32[]{:S(2)}, u32[]{:S(2)}) collective-permute-start(bf16[1,256,768]{2,1,0:T(8,128)(2,1)} %bitcast.12), channel_id=1, source_target_pairs={{0,112},{16,0},{32,16},{48,32},{64,48},{80,64},{96,80},{112,96},{1... | collective-permute-start | bytes 1179656 | tf_op jit(solution)/shard_map/ppermute | solution.py:43
  9.1 11.5 %collective-permute-start.1 = (bf16[1,256,768]{2,1,0:T(8,128)(2,1)}, bf16[1,256,768]{2,1,0:T(8,128)(2,1)}, u32[]{:S(2)}, u32[]{:S(2)}) collective-permute-start(bf16[1,256,768]{2,1,0:T(8,128)(2,1)} %bitcast.13), channel_id=1, source_target_pairs={{0,16},{16,32},{32,48},{48,64},{64,80},{80,96},{96,112},{112,0},{1... | collective-permute-start | bytes 1179656 | tf_op jit(solution)/shard_map/ppermute | solution.py:43
  9.1 11.5 %collective-permute-start.4 = (bf16[1,256,768]{2,1,0:T(8,128)(2,1)}, bf16[1,256,768]{2,1,0:T(8,128)(2,1)S(1)}, u32[]{:S(2)}, u32[]{:S(2)}) collective-permute-start(bf16[1,256,768]{2,1,0:T(8,128)(2,1)} %bitcast.14), channel_id=1, source_target_pairs={{0,12},{4,0},{8,4},{12,8},{1,13},{5,1},{9,5},{13,9},{2,14},{6,2},{... | collective-permute-start | bytes 1179656 | tf_op jit(solution)/shard_map/ppermute | solution.py:45
  11.6 11.0 %copy-start.4 = (bf16[1536,768]{1,0:T(8,128)(2,1)}, bf16[1536,768]{1,0:T(8,128)(2,1)S(1)}, u32[]{:S(2)}) copy-start(bf16[1536,768]{1,0:T(8,128)(2,1)S(1)} %collective-permute-done.2) | copy-start | bytes 7077892
  11.6 11.0 %collective-permute-start.3 = (bf16[1,256,768]{2,1,0:T(8,128)(2,1)}, bf16[1,256,768]{2,1,0:T(8,128)(2,1)S(1)}, u32[]{:S(2)}, u32[]{:S(2)}) collective-permute-start(bf16[1,256,768]{2,1,0:T(8,128)(2,1)} %bitcast.15), channel_id=1, source_target_pairs={{0,4},{4,8},{8,12},{12,0},{1,5},{5,9},{9,13},{13,1},{2,6},{6,10},{... | collective-permute-start | bytes 1179656 | tf_op jit(solution)/shard_map/ppermute | solution.py:45
  17.5 12.7 %copy-start.5 = (bf16[1,256,768]{2,1,0:T(8,128)(2,1)}, bf16[1,256,768]{2,1,0:T(8,128)(2,1)S(1)}, u32[]{:S(2)}) copy-start(bf16[1,256,768]{2,1,0:T(8,128)(2,1)S(1)} %collective-permute-done.refs_2_.refs_6_) | copy-start | bytes 1179652
  20.6 4.5 %copy-start.6 = (bf16[1,256,768]{2,1,0:T(8,128)(2,1)}, bf16[1,256,768]{2,1,0:T(8,128)(2,1)S(1)}, u32[]{:S(2)}) copy-start(bf16[1,256,768]{2,1,0:T(8,128)(2,1)S(1)} %collective-permute-done.4.refs_1_.refs_5_) | copy-start | bytes 1179652
  22.6 7.5 %copy-start.1 = (bf16[1,256,768]{2,1,0:T(8,128)(2,1)}, bf16[1,256,768]{2,1,0:T(8,128)(2,1)S(1)}, u32[]{:S(2)}) copy-start(bf16[1,256,768]{2,1,0:T(8,128)(2,1)S(1)} %collective-permute-done.3.refs_4_.refs_8_) | copy-start | bytes 1179652
  22.6 16.3 %collective-permute-start.5 = (bf16[1,256,768]{2,1,0:T(8,128)(2,1)S(1)}, bf16[1,256,768]{2,1,0:T(8,128)(2,1)}, u32[]{:S(2)}, u32[]{:S(2)}) collective-permute-start(bf16[1,256,768]{2,1,0:T(8,128)(2,1)S(1)} %collective-permute-done.3.refs_4_.refs_8_), channel_id=1, source_target_pairs={{0,4},{4,8},{8,12},{12,0},{1,5},{5,9},{9,13},{13,1},{2,6},{6,10},{... | collective-permute-start | bytes 1179656 | tf_op jit(solution)/shard_map/ppermute | solution.py:45
  22.6 16.3 %collective-permute-start.7 = (bf16[1,256,768]{2,1,0:T(8,128)(2,1)S(1)}, bf16[1,256,768]{2,1,0:T(8,128)(2,1)}, u32[]{:S(2)}, u32[]{:S(2)}) collective-permute-start(bf16[1,256,768]{2,1,0:T(8,128)(2,1)S(1)} %collective-permute-done.refs_2_.refs_6_), channel_id=1, source_target_pairs={{0,112},{16,0},{32,16},{48,32},{64,48},{80,64},{96,80},{112,96},{1... | collective-permute-start | bytes 1179656 | tf_op jit(solution)/shard_map/ppermute | solution.py:43
  25.1 13.9 %collective-permute-start.6 = (bf16[1,256,768]{2,1,0:T(8,128)(2,1)}, bf16[1,256,768]{2,1,0:T(8,128)(2,1)}, u32[]{:S(2)}, u32[]{:S(2)}) collective-permute-start(bf16[1,256,768]{2,1,0:T(8,128)(2,1)} %collective-permute-done.1.refs_3_.refs_7_), channel_id=1, source_target_pairs={{0,16},{16,32},{32,48},{48,64},{64,80},{80,96},{96,112},{112,0},{1... | collective-permute-start | bytes 1179656 | tf_op jit(solution)/shard_map/ppermute | solution.py:43
  25.1 13.9 %collective-permute-start.8 = (bf16[1,256,768]{2,1,0:T(8,128)(2,1)S(1)}, bf16[1,256,768]{2,1,0:T(8,128)(2,1)}, u32[]{:S(2)}, u32[]{:S(2)}) collective-permute-start(bf16[1,256,768]{2,1,0:T(8,128)(2,1)S(1)} %collective-permute-done.refs_2_.refs_6_), channel_id=1, source_target_pairs={{0,12},{4,0},{8,4},{12,8},{1,13},{5,1},{9,5},{13,9},{2,14},{6,2},{... | collective-permute-start | bytes 1179656 | tf_op jit(solution)/shard_map/ppermute | solution.py:45
  39.0 11.0 %collective-permute-start.10 = (bf16[1,256,768]{2,1,0:T(8,128)(2,1)}, bf16[1,256,768]{2,1,0:T(8,128)(2,1)S(1)}, u32[]{:S(2)}, u32[]{:S(2)}) collective-permute-start(bf16[1,256,768]{2,1,0:T(8,128)(2,1)} %collective-permute-done.6.refs_1_.refs_10_), channel_id=1, source_target_pairs={{0,4},{4,8},{8,12},{12,0},{1,5},{5,9},{9,13},{13,1},{2,6},{6,10},{... | collective-permute-start | bytes 1179656 | tf_op jit(solution)/shard_map/ppermute | solution.py:45
  39.1 11.7 %collective-permute-start.9 = (bf16[1,256,768]{2,1,0:T(8,128)(2,1)}, bf16[1,256,768]{2,1,0:T(8,128)(2,1)}, u32[]{:S(2)}, u32[]{:S(2)}) collective-permute-start(bf16[1,256,768]{2,1,0:T(8,128)(2,1)} %collective-permute-done.6.refs_1_.refs_10_), channel_id=1, source_target_pairs={{0,12},{4,0},{8,4},{12,8},{1,13},{5,1},{9,5},{13,9},{2,14},{6,2},{... | collective-permute-start | bytes 1179656 | tf_op jit(solution)/shard_map/ppermute | solution.py:45
  41.7 10.3 %collective-permute-start.11 = (bf16[1,256,768]{2,1,0:T(8,128)(2,1)}, bf16[1,256,768]{2,1,0:T(8,128)(2,1)}, u32[]{:S(2)}, u32[]{:S(2)}) collective-permute-start(bf16[1,256,768]{2,1,0:T(8,128)(2,1)} %collective-permute-done.7.refs_0_.refs_9_), channel_id=1, source_target_pairs={{0,112},{16,0},{32,16},{48,32},{64,48},{80,64},{96,80},{112,96},{1... | collective-permute-start | bytes 1179656 | tf_op jit(solution)/shard_map/ppermute | solution.py:43
  43.5 11.2 %collective-permute-start.12 = (bf16[1,256,768]{2,1,0:T(8,128)(2,1)}, bf16[1,256,768]{2,1,0:T(8,128)(2,1)}, u32[]{:S(2)}, u32[]{:S(2)}) collective-permute-start(bf16[1,256,768]{2,1,0:T(8,128)(2,1)} %collective-permute-done.5.refs_3_.refs_12_), channel_id=1, source_target_pairs={{0,16},{16,32},{32,48},{48,64},{64,80},{80,96},{96,112},{112,0},{1... | collective-permute-start | bytes 1179656 | tf_op jit(solution)/shard_map/ppermute | solution.py:43
  50.0 8.9 %copy-start.3 = (s32[256]{0:T(256)S(1)}, s32[256]{0:T(256)}, u32[]{:S(2)}) copy-start(s32[256]{0:T(256)} %param.8) | copy-start | bytes 3076
  50.0 9.5 %copy-start.2 = (s32[1536]{0:T(1024)S(1)}, s32[1536]{0:T(1024)}, u32[]{:S(2)}) copy-start(s32[1536]{0:T(1024)} %param.7) | copy-start | bytes 18436
  50.0 0.8 copy-start
  54.7 16.0 %collective-permute-start.13 = (bf16[2,256,768]{2,1,0:T(8,128)(2,1)S(1)}, bf16[2,256,768]{2,1,0:T(8,128)(2,1)}, u32[]{:S(2)}, u32[]{:S(2)}) collective-permute-start(bf16[2,256,768]{2,1,0:T(8,128)(2,1)S(1)} %pad_maximum_fusion), channel_id=1, source_target_pairs={{0,16},{16,32},{32,48},{48,64},{64,80},{80,96},{96,112},{112,0},{1... | collective-permute-start | bytes 2359304 | tf_op jit(solution)/shard_map/ppermute | solution.py:43
  54.7 16.0 %collective-permute-start.14 = (bf16[2,256,768]{2,1,0:T(8,128)(2,1)}, bf16[2,256,768]{2,1,0:T(8,128)(2,1)}, u32[]{:S(2)}, u32[]{:S(2)}) collective-permute-start(bf16[2,256,768]{2,1,0:T(8,128)(2,1)} %get-tuple-element.70), channel_id=1, source_target_pairs={{0,12},{4,0},{8,4},{12,8},{1,13},{5,1},{9,5},{13,9},{2,14},{6,2},{... | collective-permute-start | bytes 2359304 | tf_op jit(solution)/shard_map/ppermute | solution.py:45
  55.4 15.4 %collective-permute-start.15 = (bf16[2,256,768]{2,1,0:T(8,128)(2,1)S(1)}, bf16[2,256,768]{2,1,0:T(8,128)(2,1)}, u32[]{:S(2)}, u32[]{:S(2)}) collective-permute-start(bf16[2,256,768]{2,1,0:T(8,128)(2,1)S(1)} %pad_maximum_fusion), channel_id=1, source_target_pairs={{0,112},{16,0},{32,16},{48,32},{64,48},{80,64},{96,80},{112,96},{1... | collective-permute-start | bytes 2359304 | tf_op jit(solution)/shard_map/ppermute | solution.py:43
  58.0 16.3 %collective-permute-start.16 = (bf16[2,256,768]{2,1,0:T(8,128)(2,1)}, bf16[2,256,768]{2,1,0:T(8,128)(2,1)}, u32[]{:S(2)}, u32[]{:S(2)}) collective-permute-start(bf16[2,256,768]{2,1,0:T(8,128)(2,1)} %get-tuple-element.70), channel_id=1, source_target_pairs={{0,4},{4,8},{8,12},{12,0},{1,5},{5,9},{9,13},{13,1},{2,6},{6,10},{... | collective-permute-start | bytes 2359304 | tf_op jit(solution)/shard_map/ppermute | solution.py:45
  74.3 27.2 %collective-permute-start.17 = (bf16[2,256,768]{2,1,0:T(8,128)(2,1)}, bf16[2,256,768]{2,1,0:T(8,128)(2,1)}, u32[]{:S(2)}, u32[]{:S(2)}) collective-permute-start(bf16[2,256,768]{2,1,0:T(8,128)(2,1)} %collective-permute-done.13.refs_2_), channel_id=1, source_target_pairs={{0,4},{4,8},{8,12},{12,0},{1,5},{5,9},{9,13},{13,1},{2,6},{6,10},{... | collective-permute-start | bytes 2359304 | tf_op jit(solution)/shard_map/ppermute | solution.py:45
  74.3 28.3 %collective-permute-start.18 = (bf16[2,256,768]{2,1,0:T(8,128)(2,1)}, bf16[2,256,768]{2,1,0:T(8,128)(2,1)}, u32[]{:S(2)}, u32[]{:S(2)}) collective-permute-start(bf16[2,256,768]{2,1,0:T(8,128)(2,1)} %collective-permute-done.13.refs_2_), channel_id=1, source_target_pairs={{0,16},{16,32},{32,48},{48,64},{64,80},{80,96},{96,112},{112,0},{1... | collective-permute-start | bytes 2359304 | tf_op jit(solution)/shard_map/ppermute | solution.py:43
  74.3 28.3 %collective-permute-start.19 = (bf16[2,256,768]{2,1,0:T(8,128)(2,1)}, bf16[2,256,768]{2,1,0:T(8,128)(2,1)}, u32[]{:S(2)}, u32[]{:S(2)}) collective-permute-start(bf16[2,256,768]{2,1,0:T(8,128)(2,1)} %get-tuple-element.77), channel_id=1, source_target_pairs={{0,112},{16,0},{32,16},{48,32},{64,48},{80,64},{96,80},{112,96},{1... | collective-permute-start | bytes 2359304 | tf_op jit(solution)/shard_map/ppermute | solution.py:43
  77.0 25.6 %collective-permute-start.20 = (bf16[2,256,768]{2,1,0:T(8,128)(2,1)}, bf16[2,256,768]{2,1,0:T(8,128)(2,1)}, u32[]{:S(2)}, u32[]{:S(2)}) collective-permute-start(bf16[2,256,768]{2,1,0:T(8,128)(2,1)} %collective-permute-done.14.refs_1_), channel_id=1, source_target_pairs={{0,12},{4,0},{8,4},{12,8},{1,13},{5,1},{9,5},{13,9},{2,14},{6,2},{... | collective-permute-start | bytes 2359304 | tf_op jit(solution)/shard_map/ppermute | solution.py:45
  102.6 13.3 %collective-permute-start.22 = (bf16[1,256,768]{2,1,0:T(8,128)(2,1)}, bf16[1,256,768]{2,1,0:T(8,128)(2,1)S(1)}, u32[]{:S(2)}, u32[]{:S(2)}) collective-permute-start(bf16[1,256,768]{2,1,0:T(8,128)(2,1)} %collective-permute-done.5.refs_3_.refs_12_), channel_id=1, source_target_pairs={{0,112},{16,0},{32,16},{48,32},{64,48},{80,64},{96,80},{112,96},{1... | collective-permute-start | bytes 1179656 | tf_op jit(solution)/shard_map/ppermute | solution.py:43
  103.6 12.3 %collective-permute-start.23 = (bf16[1,256,768]{2,1,0:T(8,128)(2,1)}, bf16[1,256,768]{2,1,0:T(8,128)(2,1)}, u32[]{:S(2)}, u32[]{:S(2)}) collective-permute-start(bf16[1,256,768]{2,1,0:T(8,128)(2,1)} %collective-permute-done.9.refs_2_.refs_15_), channel_id=1, source_target_pairs={{0,12},{4,0},{8,4},{12,8},{1,13},{5,1},{9,5},{13,9},{2,14},{6,2},{... | collective-permute-start | bytes 1179656 | tf_op jit(solution)/shard_map/ppermute | solution.py:45
  104.5 11.4 %collective-permute-start.24 = (bf16[1,256,768]{2,1,0:T(8,128)(2,1)S(1)}, bf16[1,256,768]{2,1,0:T(8,128)(2,1)}, u32[]{:S(2)}, u32[]{:S(2)}) collective-permute-start(bf16[1,256,768]{2,1,0:T(8,128)(2,1)S(1)} %slice.12), channel_id=1, source_target_pairs={{0,16},{16,32},{32,48},{48,64},{64,80},{80,96},{96,112},{112,0},{1... | collective-permute-start | bytes 1179656 | tf_op jit(solution)/shard_map/ppermute | solution.py:43
  115.9 0.7 copy-start.7
  125.1 23.5 %collective-permute-start.25 = (f32[6,256]{1,0:T(8,128)S(1)}, f32[6,256]{1,0:T(8,128)S(1)}, u32[]{:S(2)}, u32[]{:S(2)}) collective-permute-start(f32[6,256]{1,0:T(8,128)S(1)} %get-tuple-element.101), channel_id=1, source_target_pairs={{0,1},{1,0},{2,3},{3,2},{4,5},{5,4},{6,7},{7,6},{8,9},{9,8},{10,11... | collective-permute-start | bytes 18440 | tf_op jit(solution)/shard_map/ppermute | solution.py:54
  130.8 17.8 %collective-permute-start.26 = (f32[6,256]{1,0:T(8,128)S(1)}, f32[6,256]{1,0:T(8,128)S(1)}, u32[]{:S(2)}, u32[]{:S(2)}) collective-permute-start(f32[6,256]{1,0:T(8,128)S(1)} %get-tuple-element.100), channel_id=1, source_target_pairs={{0,129},{1,128},{128,1},{129,0},{2,131},{3,130},{130,3},{131,2},{4... | collective-permute-start | bytes 18440 | tf_op jit(solution)/shard_map/ppermute | solution.py:58
  136.4 20.7 %all-to-all-start = ((f32[32,1,256]{2,1,0:T(1,128)}), f32[32,1,256]{2,1,0:T(1,128)S(1)}, u32[]{:S(2)}, u32[]{:S(2)}) async-start(f32[32,1,256]{2,1,0:T(1,128)} %get-tuple-element.97), calls=%async_computation | async-start | bytes 65536 | tf_op jit(solution)/shard_map/all_to_all | solution.py:297

commit v3 on v2

--- a/solution.py
+++ b/solution.py
@@ -18,8 +18,8 @@
 GROUP = 4
 AHEAD = 6
 VMEM_MIB = 63
-FAR_FROM = 4
-IDS_AT = 3
+FAR_FROM = 3
+IDS_AT = 4
 
 NY, NZ, NX, NH, NK = 2, 8, 4, 2, 2
 AXES = ("y", "z", "x", "h", "k")
@@ -85,11 +85,12 @@
     return total
 
 
-def pair_kernel(news, olds, sizes, n_sets, first, table, *refs):
+def pair_kernel(news, olds, sizes, n_sets, first, last, table, *refs):
     arrays, refs = refs[: len(sizes)], refs[len(sizes) :]
     sets, refs = refs[:n_sets], refs[n_sets:]
-    before, refs = ((), refs) if first else (refs[:4], refs[4:])
-    rows, cols, scale, next_turn, held, blocks, columns, sums, added, listed, places, sems, set_sems = refs
+    n_before = 0 if first else 3 if last else 4
+    before, refs = refs[:n_before], refs[n_before:]
+    rows, scale, next_turn, cols, held, blocks, columns, sums, added, listed, places, sems, set_sems = refs
     n_new, n_guest = len(news), len(news) + len(olds)
     n_set, n_each = blocks.shape[0], sets[0].shape[0]
     z, x = table[table.shape[0] - 2], table[table.shape[0] - 1]
@@ -173,14 +174,17 @@
         scale[pl.ds(r, 1), :] = EXP2_SCALE / jnp.sqrt(lane_sums(squares(blocks.at[r])) + EPSILON)
 
     def set_col_sums(g):
-        cols[places[g]] = added[places[g]] + lane_sums(sums[g])
+        if last:
+            cols[g] = lane_sums(sums[g])
+        else:
+            cols[places[g]] = added[places[g]] + lane_sums(sums[g])
 
     count = list_pairs(0, n_new, 0)
     if first:
-        for out in (rows, cols, scale, next_turn):
+        for out in (rows, scale, next_turn, cols):
             out[...] = jnp.zeros_like(out)
     else:
-        for out, value in zip((rows, cols, scale, next_turn), before, strict=True):
+        for out, value in zip((rows, scale, next_turn, cols)[:n_before], before, strict=True):
             out[...] = value[...]
     sums[...] = jnp.zeros_like(sums)
     for at, copy in guest_copies:
@@ -205,19 +209,20 @@
         in_groups(n_new, n_guest, set_column)
         waited = run_pairs(count, waited)
     wait_blocks(waited, n_set)
-    added[...] = cols[...]
+    if not last:
+        added[...] = cols[...]
     in_groups(0, n_guest, set_col_sums)
 
 
-def pairs(table, news, olds, arrays, sets, running):
+def pairs(table, news, olds, arrays, sets, running, last):
     n_guest, n_set = len(news) + len(olds), sum(one.shape[0] for one in sets)
     smem, vmem, hbm = (pl.BlockSpec(memory_space=m) for m in (pltpu.SMEM, pltpu.VMEM, pltpu.HBM))
     first = running is None
     tiles = (len(news) * n_set + len(olds) * sets[-1].shape[0]) // 3
-    shapes = [(2 * sets[0].shape[0], 8, BLOCK), (NZ * NX, 1, BLOCK), (16, BLOCK), (8, LANES)]
+    shapes = [(2 * sets[0].shape[0], 8, BLOCK), (16, BLOCK), (8, LANES), (n_guest if last else NZ * NX, 1, BLOCK)]
     return pl.pallas_call(
-        functools.partial(pair_kernel, news, olds, [a.shape[0] for a in arrays], len(sets), first),
-        in_specs=[smem] + [hbm] * (len(arrays) + len(sets)) + [vmem] * (0 if first else 4),
+        functools.partial(pair_kernel, news, olds, [a.shape[0] for a in arrays], len(sets), first, last),
+        in_specs=[smem] + [hbm] * (len(arrays) + len(sets)) + [vmem] * (0 if first else 3 if last else 4),
         out_specs=[vmem] * 4,
         out_shape=[jax.ShapeDtypeStruct(shape, jnp.float32) for shape in shapes],
         scratch_shapes=[
@@ -225,7 +230,7 @@
             pltpu.VMEM((n_set, *arrays[0].shape[1:]), jnp.bfloat16),
             pltpu.VMEM((n_guest, BLOCK, LANES), jnp.float32),
             pltpu.VMEM((n_guest, BLOCK, LANES), jnp.float32),
-            pltpu.VMEM(shapes[1], jnp.float32),
+            pltpu.VMEM(shapes[3], jnp.float32),
             pltpu.SMEM((2, n_guest * n_set + UNROLL), jnp.int32),
             pltpu.SMEM((n_guest,), jnp.int32),
             pltpu.SemaphoreType.DMA((len(arrays),)),
@@ -236,7 +241,7 @@
             flops=tiles * 4 * BLOCK * BLOCK * 768, bytes_accessed=tiles * 400000, transcendentals=tiles * BLOCK * BLOCK
         ),
         name="pairs",
-    )(table, *arrays, *sets, *([] if first else running))
+    )(table, *arrays, *sets, *([] if first else running[:3] if last else running))
 
 
 def body(home_rows, guest_rows, home_cluster, guest_cluster, pair_mask):
@@ -277,7 +282,7 @@
     near = to_sibling(home_rows).reshape(slots, BLOCK, -1)
     newest = [((0, 0),), *send(SLOTS[0][:3], []), *send(SLOTS[0][3:], [near])]
     sets, running = [near], None
-    backlog, done = [], []
+    backlog, done = [], [table]
     for s in range(1, len(SLOTS) + 1):
         came = tuple(stacks[p] for p in newest)
         coming = send(SLOTS[s], [*came, *done]) if s < len(SLOTS) else []
@@ -288,14 +293,19 @@
             far, _ = lax.optimization_barrier((far, came))
             sets = [near, far]
             olds = backlog
-        running = pairs(table, flat(newest), flat(olds), [stacks[p] for p in [*newest, *olds]], sets, running)
+        last = s == len(SLOTS)
+        if last:
+            incoming = lax.all_to_all(running[3], ("z", "x"), 0, 0, tiled=True)
+        running = pairs(table, flat(newest), flat(olds), [stacks[p] for p in [*newest, *olds]], sets, running, last)
+        if last:
+            incoming, _ = lax.optimization_barrier((incoming, running[3]))
+            late = [shift(running[3][i], -dz, -dx) for i, (dz, dx) in enumerate(flat(newest))]
         backlog = backlog + newest
-        done = [running[3]]
+        done = [running[2]]
         newest = coming
-    rows, cols = jnp.sum(running[0], axis=1), running[1]
-
-    incoming = lax.all_to_all(cols, ("z", "x"), 0, 0, tiled=True)
-    guest_density = jnp.sum(incoming, axis=(0, 1))
+    rows = jnp.sum(running[0], axis=1)
+
+    guest_density = jnp.sum(incoming, axis=(0, 1)) + sum(part[0] for part in late)
     home_density = to_sibling(rows[:slots]) + to_partner(rows[slots:])
 
     home_ids = lax.dynamic_slice_in_dim(home_cluster, device_of(y, k) * slots, slots)

time: 158 us -> 155 us (0.981)
  waiting for transfers between devices: 27.1 us -> 15.9 us
  starting transfers between devices: 53.4 us -> 62.1 us
  Pallas kernels: 60.3 us -> 57.5 us
    ppermute x0 -> x3, starting transfers between devices: none -> 11.5 us  [shift(): lax.ppermute(value, ('z', 'x'), [(z * NX + x, (z + dz) % NZ * NX + (x + d...]
    all_to_all x1, waiting for transfers between devices: 7.91 us -> 0.01 us  [body(): incoming = lax.all_to_all(running[3], ('z', 'x'), 0, 0, tiled=True)]
    ppermute x12, starting transfers between devices: 16.2 us -> 23.3 us  [shift(): return lax.ppermute(value, 'z', [(i, (i + dz) % NZ) for i in range(NZ)])]
    ppermute x2, starting transfers between devices: 9.05 us -> 3.33 us  [to_sibling(): return lax.ppermute(value, 'k', [(0, 1), (1, 0)])]
    ppermute x12, waiting for transfers between devices: 13.7 us -> 10.2 us  [shift(): return lax.ppermute(value, 'z', [(i, (i + dz) % NZ) for i in range(NZ)])]
    all_to_all x1, starting transfers between devices: 12.1 us -> 8.94 us  [body(): incoming = lax.all_to_all(running[3], ('z', 'x'), 0, 0, tiled=True)]
    pallas_call x6, Pallas kernels: 60.3 us -> 57.5 us  [pairs(): pl.pallas_call(functools.partial(pair_kernel, news, olds, [a.shape[0] for...]
    ppermute x11, starting transfers between devices: 12.9 us -> 10.4 us  [shift(): return lax.ppermute(value, 'x', [(i, (i + dx) % NX) for i in range(NX)])]
  transfers between devices with their start and end apart: 28 -> 31, of which waited for: 7 -> 7; matrix products, arithmetic and copies ran while one was open for 7% -> 6% of each run, Pallas kernels for 33% -> 37%
where the time goes in v3:
time: 155 us; the launch traced here: 154 us
  starting transfers between devices  62.1 us (40%)
  Pallas kernels  57.5 us (37%)
  waiting for transfers between devices  15.9 us (10%)
  other arithmetic  8.6 us (6%)
  local copies, waits for them, and re-layouts  7.64 us (5%)
  between operations  2.29 us (1%)
    pallas_call x6, Pallas kernels, pairs(): pl.pallas_call(functools.partial(pair_kernel, news, olds, [a.shape[0] for...  57.5 us
    ppermute x12, starting transfers between devices, shift(): return lax.ppermute(value, 'z', [(i, (i + dz) % NZ) for i in range(NZ)])  23.3 us
    ppermute x3, starting transfers between devices, shift(): lax.ppermute(value, ('z', 'x'), [(z * NX + x, (z + dz) % NZ * NX + (x + d...  11.5 us
    ppermute x11, starting transfers between devices, shift(): return lax.ppermute(value, 'x', [(i, (i + dx) % NX) for i in range(NX)])  10.4 us
    ppermute x12, waiting for transfers between devices, shift(): return lax.ppermute(value, 'z', [(i, (i + dz) % NZ) for i in range(NZ)])  10.2 us
    all_to_all x1, starting transfers between devices, body(): incoming = lax.all_to_all(running[3], ('z', 'x'), 0, 0, tiled=True)  8.94 us
    ppermute x2, starting transfers between devices, to_partner(): return lax.ppermute(value, ('y', 'k'), [(0, 3), (1, 2), (2, 1), (3, 0)])  4.68 us
    ppermute x11, waiting for transfers between devices, shift(): return lax.ppermute(value, 'x', [(i, (i + dx) % NX) for i in range(NX)])  4.31 us
  transfers between devices with their start and end apart: 31, of which 7 were waited for; matrix products, arithmetic and copies ran while one was open for 6% of the time, Pallas kernels for 37%

profile of v3, /device:TPU:1, one launch (start us, length us, event | category | flops | bytes accessed | tf_op | source)
XLA Modules:
  0.0 154.0 jit_solution(8474552128241382568)
XLA Ops:
  0.6 3.3 %collective-permute-start.2 = (bf16[1536,768]{1,0:T(8,128)(2,1)}, bf16[1536,768]{1,0:T(8,128)(2,1)S(1)}, u32[]{:S(2)}, u32[]{:S(2)}) collective-permute-start(bf16[1536,768]{1,0:T(8,128)(2,1)} %param.5), channel_id=1, source_target_pairs={{0,1},{1,0},{2,3},{3,2},{4,5},{5,4},{6,7},{7,6},{8,9},{9,8},{10,11... | collective-permute-start | bytes 7077896 | tf_op jit(solution)/shard_map/ppermute | solution.py:54
  4.0 0.0 collective-permute-start.17
  4.0 5.1 %collective-permute-start = (bf16[1,256,768]{2,1,0:T(8,128)(2,1)}, bf16[1,256,768]{2,1,0:T(8,128)(2,1)S(1)}, u32[]{:S(2)}, u32[]{:S(2)}) collective-permute-start(bf16[1,256,768]{2,1,0:T(8,128)(2,1)} %bitcast.20), channel_id=1, source_target_pairs={{0,112},{16,0},{32,16},{48,32},{64,48},{80,64},{96,80},{112,96},{1... | collective-permute-start | bytes 1179656 | tf_op jit(solution)/shard_map/ppermute | solution.py:43
  9.1 0.0 collective-permute-start.1
  9.1 2.5 %collective-permute-start.4 = (bf16[1,256,768]{2,1,0:T(8,128)(2,1)}, bf16[1,256,768]{2,1,0:T(8,128)(2,1)S(1)}, u32[]{:S(2)}, u32[]{:S(2)}) collective-permute-start(bf16[1,256,768]{2,1,0:T(8,128)(2,1)} %bitcast.22), channel_id=1, source_target_pairs={{0,12},{4,0},{8,4},{12,8},{1,13},{5,1},{9,5},{13,9},{2,14},{6,2},{... | collective-permute-start | bytes 1179656 | tf_op jit(solution)/shard_map/ppermute | solution.py:45
  11.6 1.4 copy-done.5
  13.0 0.0 collective-permute-start.3
  13.0 0.8 reshape.45
  13.8 0.2 dynamic-slice_reduce_fusion
  14.0 0.9 fusion.2
  14.8 0.6 concatenate.3.table
  15.4 2.0 %collective-permute-done.refs_2_.refs_6_ = bf16[1,256,768]{2,1,0:T(8,128)(2,1)S(1)} collective-permute-done((bf16[1,256,768]{2,1,0:T(8,128)(2,1)}, bf16[1,256,768]{2,1,0:T(8,128)(2,1)S(1)}, u32[]{:S(2)}, u32[]{:S(2)}) %collective-permute-start) | collective-permute-done | bytes 393248 | tf_op jit(solution)/shard_map/ppermute | solution.py:43
  17.5 3.1 %collective-permute-done.1.refs_3_.refs_7_ = bf16[1,256,768]{2,1,0:T(8,128)(2,1)} collective-permute-done((bf16[1,256,768]{2,1,0:T(8,128)(2,1)}, bf16[1,256,768]{2,1,0:T(8,128)(2,1)}, u32[]{:S(2)}, u32[]{:S(2)}) %collective-permute-start.1) | collective-permute-done | bytes 393248 | tf_op jit(solution)/shard_map/ppermute | solution.py:43
  20.5 0.0 collective-permute-done.4.refs_1_.refs_5_
  20.6 3.5 %collective-permute-done.3.refs_4_.refs_8_ = bf16[1,256,768]{2,1,0:T(8,128)(2,1)S(1)} collective-permute-done((bf16[1,256,768]{2,1,0:T(8,128)(2,1)}, bf16[1,256,768]{2,1,0:T(8,128)(2,1)S(1)}, u32[]{:S(2)}, u32[]{:S(2)}) %collective-permute-start.3) | collective-permute-done | bytes 393248 | tf_op jit(solution)/shard_map/ppermute | solution.py:45
  24.1 2.7 %collective-permute-start.7 = (bf16[1,256,768]{2,1,0:T(8,128)(2,1)S(1)}, bf16[1,256,768]{2,1,0:T(8,128)(2,1)}, u32[]{:S(2)}, u32[]{:S(2)}) collective-permute-start(bf16[1,256,768]{2,1,0:T(8,128)(2,1)S(1)} %collective-permute-done.refs_2_.refs_6_), channel_id=1, source_target_pairs={{0,112},{16,0},{32,16},{48,32},{64,48},{80,64},{96,80},{112,96},{1... | collective-permute-start | bytes 1179656 | tf_op jit(solution)/shard_map/ppermute | solution.py:43
  26.7 2.7 %collective-permute-start.8 = (bf16[1,256,768]{2,1,0:T(8,128)(2,1)S(1)}, bf16[1,256,768]{2,1,0:T(8,128)(2,1)}, u32[]{:S(2)}, u32[]{:S(2)}) collective-permute-start(bf16[1,256,768]{2,1,0:T(8,128)(2,1)S(1)} %collective-permute-done.refs_2_.refs_6_), channel_id=1, source_target_pairs={{0,12},{4,0},{8,4},{12,8},{1,13},{5,1},{9,5},{13,9},{2,14},{6,2},{... | collective-permute-start | bytes 1179656 | tf_op jit(solution)/shard_map/ppermute | solution.py:45
  29.4 7.9 %pairs.6 = (f32[12,8,256]{2,1,0:T(8,128)}, f32[16,256]{1,0:T(8,128)}, f32[8,128]{1,0:T(8,128)}, f32[32,1,256]{2,1,0:T(1,128)}) custom-call(s32[46]{0:T(128)} %concatenate.3.table, bf16[1,256,768]{2,1,0:T(8,128)(2,1)} %bitcast.24, bf16[1,256,768]{2,1,0:T(8,128)(2,1)} %copy-done.7, bf16[1,256,768]{2,1,0:T(8,128)(2,1)} %copy-done.6, ...), custom_call_target="tpu_custom_call" | custom-call | flops 2013265920 | bytes 4000000 | tf_op jit(solution)/shard_map/pairs/pallas_call | solution.py:223
  37.3 0.0 collective-permute-done.5.refs_3_.refs_12_
  37.4 0.0 collective-permute-done.7.refs_0_.refs_9_
  37.4 0.0 collective-permute-done.8.refs_2_.refs_11_
  37.4 1.2 collective-permute-start.9
  38.6 0.3 collective-permute-start.10
  38.9 1.2 collective-permute-start.11
  40.1 0.3 collective-permute-start.12
  40.4 6.2 %pairs.7 = (f32[12,8,256]{2,1,0:T(8,128)}, f32[16,256]{1,0:T(8,128)}, f32[8,128]{1,0:T(8,128)}, f32[32,1,256]{2,1,0:T(1,128)}) custom-call(s32[46]{0:T(128)} %concatenate.3.table, bf16[1,256,768]{2,1,0:T(8,128)(2,1)} %collective-permute-done.7.refs_0_.refs_9_, bf16[1,256,768]{2,1,0:T(8,128)(2,1)} %collective-permute-done.6.refs_1_.refs_10_, ...), custom_call_target="tpu_custom_call" | custom-call | flops 1610612736 | bytes 3200000 | tf_op jit(solution)/shard_map/pairs/pallas_call | solution.py:223
  46.6 0.8 copy-done
  47.4 1.2 pad_maximum_fusion
  48.6 0.0 collective-permute-done.11.refs_3_
  48.6 2.7 %pad_maximum_fusion.2 = (bf16[2,256,768]{2,1,0:T(8,128)(2,1)}, bf16[2,256,768]{2,1,0:T(8,128)(2,1)}) fusion(bf16[1,256,768]{2,1,0:T(8,128)(2,1)} %collective-permute-done.11.refs_3_, bf16[1,256,768]{2,1,0:T(8,128)(2,1)} %copy-done.2, bf16[1,256,768]{2,1,0:T(8,128)(2,1)} %collective-permute-done.7.refs_0_.refs_9_), kind=kLoop, calls=%fused_computation.2 | loop fusion | flops 786432 | bytes 2752512 | tf_op jit(solution)/shard_map/stack | solution.py:270
  51.3 0.3 collective-permute-start.13
  51.6 2.5 %collective-permute-start.14 = (bf16[2,256,768]{2,1,0:T(8,128)(2,1)}, bf16[2,256,768]{2,1,0:T(8,128)(2,1)}, u32[]{:S(2)}, u32[]{:S(2)}) collective-permute-start(bf16[2,256,768]{2,1,0:T(8,128)(2,1)} %get-tuple-element.71), channel_id=1, source_target_pairs={{0,12},{4,0},{8,4},{12,8},{1,13},{5,1},{9,5},{13,9},{2,14},{6,2},{... | collective-permute-start | bytes 2359304 | tf_op jit(solution)/shard_map/ppermute | solution.py:45
  54.1 2.6 %collective-permute-start.15 = (bf16[2,256,768]{2,1,0:T(8,128)(2,1)S(1)}, bf16[2,256,768]{2,1,0:T(8,128)(2,1)}, u32[]{:S(2)}, u32[]{:S(2)}) collective-permute-start(bf16[2,256,768]{2,1,0:T(8,128)(2,1)S(1)} %pad_maximum_fusion), channel_id=1, source_target_pairs={{0,112},{16,0},{32,16},{48,32},{64,48},{80,64},{96,80},{112,96},{1... | collective-permute-start | bytes 2359304 | tf_op jit(solution)/shard_map/ppermute | solution.py:43
  56.6 0.6 collective-permute-done.17
  57.2 15.8 %pairs.8 = (f32[12,8,256]{2,1,0:T(8,128)}, f32[16,256]{1,0:T(8,128)}, f32[8,128]{1,0:T(8,128)}, f32[32,1,256]{2,1,0:T(1,128)}) custom-call(s32[46]{0:T(128)} %concatenate.3.table, bf16[1,256,768]{2,1,0:T(8,128)(2,1)} %collective-permute-done.12.refs_0_, bf16[1,256,768]{2,1,0:T(8,128)(2,1)} %collective-permute-done.10.refs_1_, bf16[1,256,768]{2,1,0:T(8,128)(2,1)} %copy-done, ...), custom_call_target="tpu_custom_call" | custom-call | flops 6845104128 | bytes 13600000 | tf_op jit(solution)/shard_map/pairs/pallas_call | solution.py:223
  73.1 0.6 dynamic_slice.19
  73.7 1.4 fusion
  75.1 1.3 convert_reduce_fusion.1
  76.4 0.1 dynamic_slice.18
  76.5 0.2 convert_reduce_fusion.2
  76.7 0.2 convert_reduce_fusion
  78.3 0.1 collective-permute-start.18
  78.3 5.9 %collective-permute-start.19 = (bf16[2,256,768]{2,1,0:T(8,128)(2,1)}, bf16[2,256,768]{2,1,0:T(8,128)(2,1)}, u32[]{:S(2)}, u32[]{:S(2)}) collective-permute-start(bf16[2,256,768]{2,1,0:T(8,128)(2,1)} %collective-permute-done.13.refs_2_), channel_id=1, source_target_pairs={{0,16},{16,32},{32,48},{48,64},{64,80},{80,96},{96,112},{112,0},{1... | collective-permute-start | bytes 2359304 | tf_op jit(solution)/shard_map/ppermute | solution.py:43
  84.2 2.2 %collective-permute-start.20 = (bf16[2,256,768]{2,1,0:T(8,128)(2,1)}, bf16[2,256,768]{2,1,0:T(8,128)(2,1)}, u32[]{:S(2)}, u32[]{:S(2)}) collective-permute-start(bf16[2,256,768]{2,1,0:T(8,128)(2,1)} %get-tuple-element.79), channel_id=1, source_target_pairs={{0,112},{16,0},{32,16},{48,32},{64,48},{80,64},{96,80},{112,96},{1... | collective-permute-start | bytes 2359304 | tf_op jit(solution)/shard_map/ppermute | solution.py:43
  86.4 1.2 collective-permute-start.21
  87.5 10.0 %pairs.9 = (f32[12,8,256]{2,1,0:T(8,128)}, f32[16,256]{1,0:T(8,128)}, f32[8,128]{1,0:T(8,128)}, f32[32,1,256]{2,1,0:T(1,128)}) custom-call(s32[46]{0:T(128)} %concatenate.3.table, bf16[2,256,768]{2,1,0:T(8,128)(2,1)} %collective-permute-done.15.refs_0_, bf16[2,256,768]{2,1,0:T(8,128)(2,1)} %collective-permute-done.14.refs_1_, ...), custom_call_target="tpu_custom_call" | custom-call | flops 6442450944 | bytes 12800000 | tf_op jit(solution)/shard_map/pairs/pallas_call | solution.py:223
  97.5 1.0 slice.24
  98.6 5.1 %collective-permute-done.19.refs_0_ = bf16[2,256,768]{2,1,0:T(8,128)(2,1)} collective-permute-done((bf16[2,256,768]{2,1,0:T(8,128)(2,1)}, bf16[2,256,768]{2,1,0:T(8,128)(2,1)}, u32[]{:S(2)}, u32[]{:S(2)}) %collective-permute-start.19) | collective-permute-done | bytes 786464 | tf_op jit(solution)/shard_map/ppermute | solution.py:43
  103.7 0.8 collective-permute-done.21.refs_3_
  104.4 3.2 %collective-permute-start.22 = (bf16[1,256,768]{2,1,0:T(8,128)(2,1)}, bf16[1,256,768]{2,1,0:T(8,128)(2,1)}, u32[]{:S(2)}, u32[]{:S(2)}) collective-permute-start(bf16[1,256,768]{2,1,0:T(8,128)(2,1)} %collective-permute-done.5.refs_3_.refs_12_), channel_id=1, source_target_pairs={{0,112},{16,0},{32,16},{48,32},{64,48},{80,64},{96,80},{112,96},{1... | collective-permute-start | bytes 1179656 | tf_op jit(solution)/shard_map/ppermute | solution.py:43
  107.6 10.1 %pairs.10 = (f32[12,8,256]{2,1,0:T(8,128)}, f32[16,256]{1,0:T(8,128)}, f32[8,128]{1,0:T(8,128)}, f32[32,1,256]{2,1,0:T(1,128)}) custom-call(s32[46]{0:T(128)} %concatenate.3.table, bf16[2,256,768]{2,1,0:T(8,128)(2,1)} %collective-permute-done.19.refs_0_, bf16[2,256,768]{2,1,0:T(8,128)(2,1)} %collective-permute-done.18.refs_1_, ...), custom_call_target="tpu_custom_call" | custom-call | flops 6442450944 | bytes 12800000 | tf_op jit(solution)/shard_map/pairs/pallas_call | solution.py:223
  117.8 8.9 %all-to-all-start = ((f32[32,1,256]{2,1,0:T(1,128)}), f32[32,1,256]{2,1,0:T(1,128)S(1)}, u32[]{:S(2)}, u32[]{:S(2)}) async-start(f32[32,1,256]{2,1,0:T(1,128)} %get-tuple-element.97), calls=%async_computation | async-start | bytes 65536 | tf_op jit(solution)/shard_map/all_to_all | solution.py:298
  126.8 7.4 %pairs.11 = (f32[12,8,256]{2,1,0:T(8,128)}, f32[16,256]{1,0:T(8,128)}, f32[8,128]{1,0:T(8,128)}, f32[3,1,256]{2,1,0:T(1,128)}) custom-call(s32[46]{0:T(128)} %concatenate.3.table, bf16[1,256,768]{2,1,0:T(8,128)(2,1)} %collective-permute-done.22.refs_0_, bf16[1,256,768]{2,1,0:T(8,128)(2,1)} %collective-permute-done.23.refs_1_, ...), custom_call_target="tpu_custom_call" | custom-call | flops 2415919104 | bytes 4800000 | tf_op jit(solution)/shard_map/pairs/pallas_call | solution.py:223
  134.2 0.7 slice_bitcast_fusion.1
  134.9 6.5 %collective-permute-start.28 = (f32[1,256]{1,0:T(1,128)S(1)}, f32[1,256]{1,0:T(1,128)S(1)}, u32[]{:S(2)}, u32[]{:S(2)}) collective-permute-start(f32[1,256]{1,0:T(1,128)S(1)} %get-tuple-element.106), channel_id=1, source_target_pairs={{0,104},{4,108},{8,96},{12,100},{16,120},{20,124},{24,112},{28,116... | collective-permute-start | bytes 3080 | tf_op jit(solution)/shard_map/ppermute | solution.py:46
  141.4 1.1 collective-permute-start.29
  142.5 3.9 %collective-permute-start.27 = (f32[1,256]{1,0:T(1,128)S(1)}, f32[1,256]{1,0:T(1,128)S(1)}, u32[]{:S(2)}, u32[]{:S(2)}) collective-permute-start(f32[1,256]{1,0:T(1,128)S(1)} %get-tuple-element.108), channel_id=1, source_target_pairs={{0,24},{4,28},{8,16},{12,20},{16,40},{20,44},{24,32},{28,36},{32,5... | collective-permute-start | bytes 3080 | tf_op jit(solution)/shard_map/ppermute | solution.py:46
  146.3 0.9 reduce_sum.54
  147.3 0.1 reduce_sum.57
  147.3 4.7 %collective-permute-start.26 = (f32[6,256]{1,0:T(8,128)S(1)}, f32[6,256]{1,0:T(8,128)S(1)}, u32[]{:S(2)}, u32[]{:S(2)}) collective-permute-start(f32[6,256]{1,0:T(8,128)S(1)} %get-tuple-element.102), channel_id=1, source_target_pairs={{0,129},{1,128},{128,1},{129,0},{2,131},{3,130},{130,3},{131,2},{4... | collective-permute-start | bytes 18440 | tf_op jit(solution)/shard_map/ppermute | solution.py:58
  152.1 0.6 log_subtract_fusion.1
  152.6 0.7 collective-permute-done.26
  153.4 0.1 log_subtract_fusion
  153.4 0.6 reshape.49
  (42 shorter events, 0.1 us)
Async XLA Ops:
  0.6 10.9 %collective-permute-start.2 = (bf16[1536,768]{1,0:T(8,128)(2,1)}, bf16[1536,768]{1,0:T(8,128)(2,1)S(1)}, u32[]{:S(2)}, u32[]{:S(2)}) collective-permute-start(bf16[1536,768]{1,0:T(8,128)(2,1)} %param.5), channel_id=1, source_target_pairs={{0,1},{1,0},{2,3},{3,2},{4,5},{5,4},{6,7},{7,6},{8,9},{9,8},{10,11... | collective-permute-start | bytes 7077896 | tf_op jit(solution)/shard_map/ppermute | solution.py:54
  4.0 53.3 %collective-permute-start.17 = (bf16[1536,768]{1,0:T(8,128)(2,1)}, bf16[1536,768]{1,0:T(8,128)(2,1)}, u32[]{:S(2)}, u32[]{:S(2)}) collective-permute-start(bf16[1536,768]{1,0:T(8,128)(2,1)} %param.5), channel_id=1, source_target_pairs={{0,129},{1,128},{128,1},{129,0},{2,131},{3,130},{130,3},{131,2},{4... | collective-permute-start | bytes 7077896 | tf_op jit(solution)/shard_map/ppermute | solution.py:58
  4.0 13.5 %collective-permute-start = (bf16[1,256,768]{2,1,0:T(8,128)(2,1)}, bf16[1,256,768]{2,1,0:T(8,128)(2,1)S(1)}, u32[]{:S(2)}, u32[]{:S(2)}) collective-permute-start(bf16[1,256,768]{2,1,0:T(8,128)(2,1)} %bitcast.20), channel_id=1, source_target_pairs={{0,112},{16,0},{32,16},{48,32},{64,48},{80,64},{96,80},{112,96},{1... | collective-permute-start | bytes 1179656 | tf_op jit(solution)/shard_map/ppermute | solution.py:43
  9.1 11.5 %collective-permute-start.1 = (bf16[1,256,768]{2,1,0:T(8,128)(2,1)}, bf16[1,256,768]{2,1,0:T(8,128)(2,1)}, u32[]{:S(2)}, u32[]{:S(2)}) collective-permute-start(bf16[1,256,768]{2,1,0:T(8,128)(2,1)} %bitcast.21), channel_id=1, source_target_pairs={{0,16},{16,32},{32,48},{48,64},{64,80},{80,96},{96,112},{112,0},{1... | collective-permute-start | bytes 1179656 | tf_op jit(solution)/shard_map/ppermute | solution.py:43
  9.1 11.5 %collective-permute-start.4 = (bf16[1,256,768]{2,1,0:T(8,128)(2,1)}, bf16[1,256,768]{2,1,0:T(8,128)(2,1)S(1)}, u32[]{:S(2)}, u32[]{:S(2)}) collective-permute-start(bf16[1,256,768]{2,1,0:T(8,128)(2,1)} %bitcast.22), channel_id=1, source_target_pairs={{0,12},{4,0},{8,4},{12,8},{1,13},{5,1},{9,5},{13,9},{2,14},{6,2},{... | collective-permute-start | bytes 1179656 | tf_op jit(solution)/shard_map/ppermute | solution.py:45
  11.6 1.4 copy-start.5
  13.0 11.0 %collective-permute-start.3 = (bf16[1,256,768]{2,1,0:T(8,128)(2,1)}, bf16[1,256,768]{2,1,0:T(8,128)(2,1)S(1)}, u32[]{:S(2)}, u32[]{:S(2)}) collective-permute-start(bf16[1,256,768]{2,1,0:T(8,128)(2,1)} %bitcast.23), channel_id=1, source_target_pairs={{0,4},{4,8},{8,12},{12,0},{1,5},{5,9},{9,13},{13,1},{2,6},{6,10},{... | collective-permute-start | bytes 1179656 | tf_op jit(solution)/shard_map/ppermute | solution.py:45
  17.5 12.0 %copy-start.6 = (bf16[1,256,768]{2,1,0:T(8,128)(2,1)}, bf16[1,256,768]{2,1,0:T(8,128)(2,1)S(1)}, u32[]{:S(2)}) copy-start(bf16[1,256,768]{2,1,0:T(8,128)(2,1)S(1)} %collective-permute-done.refs_2_.refs_6_) | copy-start | bytes 1179652
  20.6 3.5 %copy-start.7 = (bf16[1,256,768]{2,1,0:T(8,128)(2,1)}, bf16[1,256,768]{2,1,0:T(8,128)(2,1)S(1)}, u32[]{:S(2)}) copy-start(bf16[1,256,768]{2,1,0:T(8,128)(2,1)S(1)} %collective-permute-done.4.refs_1_.refs_5_) | copy-start | bytes 1179652
  24.1 5.4 %copy-start.2 = (bf16[1,256,768]{2,1,0:T(8,128)(2,1)}, bf16[1,256,768]{2,1,0:T(8,128)(2,1)S(1)}, u32[]{:S(2)}) copy-start(bf16[1,256,768]{2,1,0:T(8,128)(2,1)S(1)} %collective-permute-done.3.refs_4_.refs_8_) | copy-start | bytes 1179652
  24.1 13.3 %collective-permute-start.5 = (bf16[1,256,768]{2,1,0:T(8,128)(2,1)S(1)}, bf16[1,256,768]{2,1,0:T(8,128)(2,1)}, u32[]{:S(2)}, u32[]{:S(2)}) collective-permute-start(bf16[1,256,768]{2,1,0:T(8,128)(2,1)S(1)} %collective-permute-done.3.refs_4_.refs_8_), channel_id=1, source_target_pairs={{0,4},{4,8},{8,12},{12,0},{1,5},{5,9},{9,13},{13,1},{2,6},{6,10},{... | collective-permute-start | bytes 1179656 | tf_op jit(solution)/shard_map/ppermute | solution.py:45
  24.1 13.3 %collective-permute-start.6 = (bf16[1,256,768]{2,1,0:T(8,128)(2,1)}, bf16[1,256,768]{2,1,0:T(8,128)(2,1)}, u32[]{:S(2)}, u32[]{:S(2)}) collective-permute-start(bf16[1,256,768]{2,1,0:T(8,128)(2,1)} %collective-permute-done.1.refs_3_.refs_7_), channel_id=1, source_target_pairs={{0,16},{16,32},{32,48},{48,64},{64,80},{80,96},{96,112},{112,0},{1... | collective-permute-start | bytes 1179656 | tf_op jit(solution)/shard_map/ppermute | solution.py:43
  24.1 13.3 %collective-permute-start.7 = (bf16[1,256,768]{2,1,0:T(8,128)(2,1)S(1)}, bf16[1,256,768]{2,1,0:T(8,128)(2,1)}, u32[]{:S(2)}, u32[]{:S(2)}) collective-permute-start(bf16[1,256,768]{2,1,0:T(8,128)(2,1)S(1)} %collective-permute-done.refs_2_.refs_6_), channel_id=1, source_target_pairs={{0,112},{16,0},{32,16},{48,32},{64,48},{80,64},{96,80},{112,96},{1... | collective-permute-start | bytes 1179656 | tf_op jit(solution)/shard_map/ppermute | solution.py:43
  26.7 10.6 %collective-permute-start.8 = (bf16[1,256,768]{2,1,0:T(8,128)(2,1)S(1)}, bf16[1,256,768]{2,1,0:T(8,128)(2,1)}, u32[]{:S(2)}, u32[]{:S(2)}) collective-permute-start(bf16[1,256,768]{2,1,0:T(8,128)(2,1)S(1)} %collective-permute-done.refs_2_.refs_6_), channel_id=1, source_target_pairs={{0,12},{4,0},{8,4},{12,8},{1,13},{5,1},{9,5},{13,9},{2,14},{6,2},{... | collective-permute-start | bytes 1179656 | tf_op jit(solution)/shard_map/ppermute | solution.py:45
  37.4 9.2 %collective-permute-start.9 = (bf16[1,256,768]{2,1,0:T(8,128)(2,1)}, bf16[1,256,768]{2,1,0:T(8,128)(2,1)S(1)}, u32[]{:S(2)}, u32[]{:S(2)}) collective-permute-start(bf16[1,256,768]{2,1,0:T(8,128)(2,1)} %collective-permute-done.6.refs_1_.refs_10_), channel_id=1, source_target_pairs={{0,12},{4,0},{8,4},{12,8},{1,13},{5,1},{9,5},{13,9},{2,14},{6,2},{... | collective-permute-start | bytes 1179656 | tf_op jit(solution)/shard_map/ppermute | solution.py:45
  38.6 8.8 %collective-permute-start.10 = (bf16[1,256,768]{2,1,0:T(8,128)(2,1)}, bf16[1,256,768]{2,1,0:T(8,128)(2,1)}, u32[]{:S(2)}, u32[]{:S(2)}) collective-permute-start(bf16[1,256,768]{2,1,0:T(8,128)(2,1)} %collective-permute-done.6.refs_1_.refs_10_), channel_id=1, source_target_pairs={{0,4},{4,8},{8,12},{12,0},{1,5},{5,9},{9,13},{13,1},{2,6},{6,10},{... | collective-permute-start | bytes 1179656 | tf_op jit(solution)/shard_map/ppermute | solution.py:45
  38.9 9.7 %collective-permute-start.11 = (bf16[1,256,768]{2,1,0:T(8,128)(2,1)}, bf16[1,256,768]{2,1,0:T(8,128)(2,1)}, u32[]{:S(2)}, u32[]{:S(2)}) collective-permute-start(bf16[1,256,768]{2,1,0:T(8,128)(2,1)} %collective-permute-done.7.refs_0_.refs_9_), channel_id=1, source_target_pairs={{0,112},{16,0},{32,16},{48,32},{64,48},{80,64},{96,80},{112,96},{1... | collective-permute-start | bytes 1179656 | tf_op jit(solution)/shard_map/ppermute | solution.py:43
  40.1 11.2 %collective-permute-start.12 = (bf16[1,256,768]{2,1,0:T(8,128)(2,1)}, bf16[1,256,768]{2,1,0:T(8,128)(2,1)}, u32[]{:S(2)}, u32[]{:S(2)}) collective-permute-start(bf16[1,256,768]{2,1,0:T(8,128)(2,1)} %collective-permute-done.5.refs_3_.refs_12_), channel_id=1, source_target_pairs={{0,16},{16,32},{32,48},{48,64},{64,80},{80,96},{96,112},{112,0},{1... | collective-permute-start | bytes 1179656 | tf_op jit(solution)/shard_map/ppermute | solution.py:43
  46.6 0.8 copy-start
  51.3 21.8 %collective-permute-start.13 = (bf16[2,256,768]{2,1,0:T(8,128)(2,1)S(1)}, bf16[2,256,768]{2,1,0:T(8,128)(2,1)}, u32[]{:S(2)}, u32[]{:S(2)}) collective-permute-start(bf16[2,256,768]{2,1,0:T(8,128)(2,1)S(1)} %pad_maximum_fusion), channel_id=1, source_target_pairs={{0,16},{16,32},{32,48},{48,64},{64,80},{80,96},{96,112},{112,0},{1... | collective-permute-start | bytes 2359304 | tf_op jit(solution)/shard_map/ppermute | solution.py:43
  51.6 21.5 %collective-permute-start.14 = (bf16[2,256,768]{2,1,0:T(8,128)(2,1)}, bf16[2,256,768]{2,1,0:T(8,128)(2,1)}, u32[]{:S(2)}, u32[]{:S(2)}) collective-permute-start(bf16[2,256,768]{2,1,0:T(8,128)(2,1)} %get-tuple-element.71), channel_id=1, source_target_pairs={{0,12},{4,0},{8,4},{12,8},{1,13},{5,1},{9,5},{13,9},{2,14},{6,2},{... | collective-permute-start | bytes 2359304 | tf_op jit(solution)/shard_map/ppermute | solution.py:45
  54.1 19.0 %collective-permute-start.15 = (bf16[2,256,768]{2,1,0:T(8,128)(2,1)S(1)}, bf16[2,256,768]{2,1,0:T(8,128)(2,1)}, u32[]{:S(2)}, u32[]{:S(2)}) collective-permute-start(bf16[2,256,768]{2,1,0:T(8,128)(2,1)S(1)} %pad_maximum_fusion), channel_id=1, source_target_pairs={{0,112},{16,0},{32,16},{48,32},{64,48},{80,64},{96,80},{112,96},{1... | collective-permute-start | bytes 2359304 | tf_op jit(solution)/shard_map/ppermute | solution.py:43
  56.6 16.5 %collective-permute-start.16 = (bf16[2,256,768]{2,1,0:T(8,128)(2,1)}, bf16[2,256,768]{2,1,0:T(8,128)(2,1)}, u32[]{:S(2)}, u32[]{:S(2)}) collective-permute-start(bf16[2,256,768]{2,1,0:T(8,128)(2,1)} %get-tuple-element.71), channel_id=1, source_target_pairs={{0,4},{4,8},{8,12},{12,0},{1,5},{5,9},{9,13},{13,1},{2,6},{6,10},{... | collective-permute-start | bytes 2359304 | tf_op jit(solution)/shard_map/ppermute | solution.py:45
  57.2 15.9 %copy-start.4 = (s32[256]{0:T(256)S(1)}, s32[256]{0:T(256)}, u32[]{:S(2)}) copy-start(s32[256]{0:T(256)} %param.8) | copy-start | bytes 3076
  57.2 17.9 %copy-start.3 = (s32[1536]{0:T(1024)S(1)}, s32[1536]{0:T(1024)}, u32[]{:S(2)}) copy-start(s32[1536]{0:T(1024)} %param.7) | copy-start | bytes 18436
  78.3 19.3 %collective-permute-start.18 = (bf16[2,256,768]{2,1,0:T(8,128)(2,1)}, bf16[2,256,768]{2,1,0:T(8,128)(2,1)}, u32[]{:S(2)}, u32[]{:S(2)}) collective-permute-start(bf16[2,256,768]{2,1,0:T(8,128)(2,1)} %collective-permute-done.13.refs_2_), channel_id=1, source_target_pairs={{0,4},{4,8},{8,12},{12,0},{1,5},{5,9},{9,13},{13,1},{2,6},{6,10},{... | collective-permute-start | bytes 2359304 | tf_op jit(solution)/shard_map/ppermute | solution.py:45
  78.3 25.3 %collective-permute-start.19 = (bf16[2,256,768]{2,1,0:T(8,128)(2,1)}, bf16[2,256,768]{2,1,0:T(8,128)(2,1)}, u32[]{:S(2)}, u32[]{:S(2)}) collective-permute-start(bf16[2,256,768]{2,1,0:T(8,128)(2,1)} %collective-permute-done.13.refs_2_), channel_id=1, source_target_pairs={{0,16},{16,32},{32,48},{48,64},{64,80},{80,96},{96,112},{112,0},{1... | collective-permute-start | bytes 2359304 | tf_op jit(solution)/shard_map/ppermute | solution.py:43
  84.2 19.5 %collective-permute-start.20 = (bf16[2,256,768]{2,1,0:T(8,128)(2,1)}, bf16[2,256,768]{2,1,0:T(8,128)(2,1)}, u32[]{:S(2)}, u32[]{:S(2)}) collective-permute-start(bf16[2,256,768]{2,1,0:T(8,128)(2,1)} %get-tuple-element.79), channel_id=1, source_target_pairs={{0,112},{16,0},{32,16},{48,32},{64,48},{80,64},{96,80},{112,96},{1... | collective-permute-start | bytes 2359304 | tf_op jit(solution)/shard_map/ppermute | solution.py:43
  86.4 18.1 %collective-permute-start.21 = (bf16[2,256,768]{2,1,0:T(8,128)(2,1)}, bf16[2,256,768]{2,1,0:T(8,128)(2,1)}, u32[]{:S(2)}, u32[]{:S(2)}) collective-permute-start(bf16[2,256,768]{2,1,0:T(8,128)(2,1)} %collective-permute-done.14.refs_1_), channel_id=1, source_target_pairs={{0,12},{4,0},{8,4},{12,8},{1,13},{5,1},{9,5},{13,9},{2,14},{6,2},{... | collective-permute-start | bytes 2359304 | tf_op jit(solution)/shard_map/ppermute | solution.py:45
  87.5 20.1 %copy-start.1 = (bf16[1,256,768]{2,1,0:T(8,128)(2,1)S(1)}, bf16[1,256,768]{2,1,0:T(8,128)(2,1)}, u32[]{:S(2)}) copy-start(bf16[1,256,768]{2,1,0:T(8,128)(2,1)} %copy-done) | copy-start | bytes 1179652
  104.4 22.3 %collective-permute-start.22 = (bf16[1,256,768]{2,1,0:T(8,128)(2,1)}, bf16[1,256,768]{2,1,0:T(8,128)(2,1)}, u32[]{:S(2)}, u32[]{:S(2)}) collective-permute-start(bf16[1,256,768]{2,1,0:T(8,128)(2,1)} %collective-permute-done.5.refs_3_.refs_12_), channel_id=1, source_target_pairs={{0,112},{16,0},{32,16},{48,32},{64,48},{80,64},{96,80},{112,96},{1... | collective-permute-start | bytes 1179656 | tf_op jit(solution)/shard_map/ppermute | solution.py:43
  107.6 19.1 %collective-permute-start.23 = (bf16[1,256,768]{2,1,0:T(8,128)(2,1)S(1)}, bf16[1,256,768]{2,1,0:T(8,128)(2,1)}, u32[]{:S(2)}, u32[]{:S(2)}) collective-permute-start(bf16[1,256,768]{2,1,0:T(8,128)(2,1)S(1)} %copy-done.1), channel_id=1, source_target_pairs={{0,12},{4,0},{8,4},{12,8},{1,13},{5,1},{9,5},{13,9},{2,14},{6,2},{... | collective-permute-start | bytes 1179656 | tf_op jit(solution)/shard_map/ppermute | solution.py:45
  107.6 19.1 %collective-permute-start.24 = (bf16[1,256,768]{2,1,0:T(8,128)(2,1)S(1)}, bf16[1,256,768]{2,1,0:T(8,128)(2,1)}, u32[]{:S(2)}, u32[]{:S(2)}) collective-permute-start(bf16[1,256,768]{2,1,0:T(8,128)(2,1)S(1)} %slice.24), channel_id=1, source_target_pairs={{0,16},{16,32},{32,48},{48,64},{64,80},{80,96},{96,112},{112,0},{1... | collective-permute-start | bytes 1179656 | tf_op jit(solution)/shard_map/ppermute | solution.py:43
  117.8 29.5 %all-to-all-start = ((f32[32,1,256]{2,1,0:T(1,128)}), f32[32,1,256]{2,1,0:T(1,128)S(1)}, u32[]{:S(2)}, u32[]{:S(2)}) async-start(f32[32,1,256]{2,1,0:T(1,128)} %get-tuple-element.97), calls=%async_computation | async-start | bytes 65536 | tf_op jit(solution)/shard_map/all_to_all | solution.py:298
  134.9 17.1 %collective-permute-start.28 = (f32[1,256]{1,0:T(1,128)S(1)}, f32[1,256]{1,0:T(1,128)S(1)}, u32[]{:S(2)}, u32[]{:S(2)}) collective-permute-start(f32[1,256]{1,0:T(1,128)S(1)} %get-tuple-element.106), channel_id=1, source_target_pairs={{0,104},{4,108},{8,96},{12,100},{16,120},{20,124},{24,112},{28,116... | collective-permute-start | bytes 3080 | tf_op jit(solution)/shard_map/ppermute | solution.py:46
  141.4 10.6 %collective-permute-start.29 = (f32[1,256]{1,0:T(1,128)S(1)}, f32[1,256]{1,0:T(1,128)S(1)}, u32[]{:S(2)}, u32[]{:S(2)}) collective-permute-start(f32[1,256]{1,0:T(1,128)S(1)} %get-tuple-element.107), channel_id=1, source_target_pairs={{0,72},{4,76},{8,64},{12,68},{16,88},{20,92},{24,80},{28,84},{32,1... | collective-permute-start | bytes 3080 | tf_op jit(solution)/shard_map/ppermute | solution.py:46
  142.5 9.6 %collective-permute-start.27 = (f32[1,256]{1,0:T(1,128)S(1)}, f32[1,256]{1,0:T(1,128)S(1)}, u32[]{:S(2)}, u32[]{:S(2)}) collective-permute-start(f32[1,256]{1,0:T(1,128)S(1)} %get-tuple-element.108), channel_id=1, source_target_pairs={{0,24},{4,28},{8,16},{12,20},{16,40},{20,44},{24,32},{28,36},{32,5... | collective-permute-start | bytes 3080 | tf_op jit(solution)/shard_map/ppermute | solution.py:46
  147.3 6.0 %collective-permute-start.26 = (f32[6,256]{1,0:T(8,128)S(1)}, f32[6,256]{1,0:T(8,128)S(1)}, u32[]{:S(2)}, u32[]{:S(2)}) collective-permute-start(f32[6,256]{1,0:T(8,128)S(1)} %get-tuple-element.102), channel_id=1, source_target_pairs={{0,129},{1,128},{128,1},{129,0},{2,131},{3,130},{130,3},{131,2},{4... | collective-permute-start | bytes 18440 | tf_op jit(solution)/shard_map/ppermute | solution.py:58
  152.0 1.3 collective-permute-start.25
